TPU v7x, 256 devices: a whole 4x4x8 slice. The times are simulated.
256 devices in a mesh: comp: 4 (over x), tile: 32 (over y, z), lev: 2 (over core).
Axes of the slice: x: 4, y: 4, z: 8, core: 2. Of those that a mesh axis runs over, the one named last changes fastest.
Arguments:
- atm_state: float32 [2, 48, 256, 2304], P(None, None, ('comp', 'tile'), 'lev'), may hold values from -6 to 6
- atm_diffusion: float32 [48], replicated, may hold values from 0.04 to 0.2
- atm_surface_coef: float32 [2, 256, 2304], P(None, ('comp', 'tile'), 'lev'), may hold values from 0.03 to 0.3
- ocn_state: float32 [2, 24, 512, 3584], P(None, None, ('comp', 'tile'), 'lev'), may hold values from -6 to 6
- ocn_diffusion: float32 [24], replicated, may hold values from 0.03 to 0.2
- sea_mask: int32 [512, 3584], P(('comp', 'tile'), 'lev'), may hold values 0 or 1
- atm_pair_cols: int32 [2, 128, 128, 512], P('lev', ('comp', 'tile')), may hold values from 0 to 2303, as said below
- a2o_weights: float32 [2, 128, 128, 512], P('lev', ('comp', 'tile')), as said below
- ocn_pair_cells: int32 [2, 128, 128, 512], P('lev', ('comp', 'tile')), may hold values from 0 to 7167, as said below
- o2a_weights: float32 [2, 128, 128, 512], P('lev', ('comp', 'tile')), as said below
Outputs:
- atm_next: float32 [2, 48, 256, 2304], P(None, None, ('comp', 'tile'), 'lev')
- ocean_next: float32 [2, 24, 512, 3584], P(None, None, ('comp', 'tile'), 'lev')
Inputs may be any that keep to these rules, and one draw needn't show every extreme that they name: `atm_pair_cols`: entry [l, s, d, k] is a local column i * 1152 + j of the atmosphere block at lev index l and comp+tile index s. Every (l, s, d) has 1 to 512 live entries in its first slots; all other slots are padding with index 0. In every draw some ocean block receives 512 live entries from every atmosphere block at its lev index, and some atmosphere block sends 512 to every ocean block. `ocn_pair_cells`: entry [l, d, s, k] is the local ocean cell r * 1792 + c of block (l, d) for the margin that atm_pair_cols holds at [l, s, d, k]; padding slots hold 0. `a2o_weights`: entry [l, s, d, k] belongs to the margin of atm_pair_cols[l, s, d, k]; exactly 0 on padding slots. `o2a_weights`: entry [l, d, s, k] belongs to the margin of ocn_pair_cells[l, d, s, k]; exactly 0 on padding slots.
All inputs are finite; a program needn't handle non-finite values. No bound on the sum of `sea_mask` on one device may be relied on, other than what follows from the above.
Results may differ from a plain program's by a relative error of at most 0.00002.
Values sent between devices are 32-bit elements; how exact they have to be, the bound alone decides.
No kernel may reach another device: no remote copies, remote signals or barrier semaphores. Data moves between devices by JAX's collectives and lax.ppermute only.
A program may use at most 128 MiB of HBM per device.

v0:
```python
import jax
import jax.numpy as jnp
from jax import lax
from jax.sharding import PartitionSpec as P

ASTEPS = 4
OSTEPS = 2


VERT_MIX = 0.1
OCEAN_MIX = 0.15
HEAT_GAIN = 2.0
SALT_GAIN = 1.0
MOIST_RATIO = 0.8


def in_blocks(value, dim, count):
    dims = value.shape
    pieces = value.reshape(*dims[:dim], count, dims[dim] // count, *dims[dim + 1 :])
    return jnp.moveaxis(pieces, dim, 0)


def laid_out(pieces, dim):
    pieces = jnp.moveaxis(pieces, 0, dim)
    dims = pieces.shape
    return pieces.reshape(*dims[:dim], dims[dim] * dims[dim + 1], *dims[dim + 2 :])


def one_exchange(value, axis, axes, splits, concats):
    sizes = [lax.axis_size(a) for a in axes]
    pieces = in_blocks(value, splits[0], sizes[0])
    pieces = jnp.moveaxis(in_blocks(pieces, splits[1] + 1, sizes[1]), 0, 1)
    inside = pieces.shape[2:]
    pieces = pieces.reshape(-1, *inside)
    pieces = lax.all_to_all(pieces, axis, split_axis=0, concat_axis=0, tiled=True)
    pieces = laid_out(pieces.reshape(*sizes, *inside), concats[0] + 1)
    return laid_out(pieces, concats[1])


def padded_2(value, sides, width):
    edges = {}
    for axis, dim in sides:
        count, length = (lax.axis_size(axis), value.shape[dim])
        up = [(i, (i + 1) % count) for i in range(count)]
        last = lax.slice_in_dim(value, length - width, length, axis=dim)
        first = lax.slice_in_dim(value, 0, width, axis=dim)
        edges[dim] = (
            lax.ppermute(last, axis, up),
            lax.ppermute(first, axis, [(b, a) for a, b in up]),
        )
    done = []
    for _, dim in sides:
        low, high = edges[dim]
        around = [(width, width) if d in done else (0, 0) for d in range(value.ndim)]
        value = jnp.concatenate([jnp.pad(low, around), value, jnp.pad(high, around)], axis=dim)
        done.append(dim)
    return value


def level_mix(middle):
    upper_level = jnp.concatenate([middle[:, 1:], middle[:, -1:]], axis=1)
    lower_level = jnp.concatenate([middle[:, :1], middle[:, :-1]], axis=1)
    return upper_level + lower_level - 2.0 * middle


def lateral_mix(padded):
    middle = padded[:, :, 1:-1, 1:-1]
    lateral = (
        padded[:, :, 2:, 1:-1]
        + padded[:, :, :-2, 1:-1]
        + padded[:, :, 1:-1, 2:]
        + padded[:, :, 1:-1, :-2]
        - 4.0 * middle
    )
    return (middle, lateral)


def atm_step(padded, surface, diffusion):
    middle, lateral = lateral_mix(padded)
    result = middle + diffusion[None, :, None, None] * lateral + VERT_MIX * level_mix(middle)
    result = result.at[0, 0].add(surface[1, 0] * (surface[0, 0] - middle[0, 0]))
    result = result.at[1, 0].add(surface[2, 0] * (MOIST_RATIO * surface[0, 0] - middle[1, 0]))
    return result


def ocean_step(padded, diffusion, forcing, sea_frac):
    middle, lateral = lateral_mix(padded)
    result = middle + diffusion[None, :, None, None] * lateral + OCEAN_MIX * level_mix(middle)
    result = result.at[0, 0].add(HEAT_GAIN * forcing[0])
    result = result.at[1, 0].add(-SALT_GAIN * forcing[1])
    return result * sea_frac[None, None]


def shards(
    atm_state,
    atm_diffusion,
    atm_surface_coef,
    ocn_state,
    ocn_diffusion,
    sea_mask,
    atm_pair_cols,
    a2o_weights,
    ocn_pair_cells,
    o2a_weights,
):
    group_size = lax.axis_size(("comp", "tile"))
    comp_size = lax.axis_size("comp")
    tile_size = lax.axis_size("tile")
    my_block = lax.axis_index(("comp", "tile"))
    atm_rows = atm_state.shape[2]
    atm_cols = atm_state.shape[3]
    ocn_rows = ocn_state.shape[2]
    ocn_cols = ocn_state.shape[3]
    slot_count = atm_pair_cols.shape[3]
    row_ids = my_block * ocn_rows + jnp.arange(ocn_rows, dtype=jnp.int32)
    inner_rows = ((row_ids > 0) & (row_ids < ocn_rows * group_size - 1)).astype(jnp.float32)
    sea_frac = sea_mask.astype(jnp.float32) * inner_rows[:, None]
    ocean_now = ocn_state * sea_frac[None, None]
    col_index = atm_pair_cols[0, 0]
    cell_index = ocn_pair_cells[0, 0]
    top_temp = ocean_now[0, 0].reshape(-1)
    outgoing = o2a_weights[0, 0] * top_temp[cell_index]
    incoming = one_exchange(
        outgoing.reshape(comp_size, tile_size, slot_count),
        ("comp", "tile"),
        ("comp", "tile"),
        (0, 1),
        (0, 1),
    ).reshape(group_size, slot_count)
    sea_temp = (
        jnp.zeros((atm_rows * atm_cols,), jnp.float32)
        .at[col_index.reshape(-1)]
        .add(incoming.reshape(-1))
        .reshape(atm_rows, atm_cols)
    )
    heat_flux = atm_surface_coef[0] * (atm_state[0, 0] - sea_temp)
    fresh_flux = atm_surface_coef[1] * (atm_state[1, 0] - MOIST_RATIO * sea_temp)
    fluxes = jnp.stack([heat_flux, fresh_flux]).reshape(2, -1)
    outgoing_flux = a2o_weights[0, 0][None] * fluxes[:, col_index]
    incoming_flux = one_exchange(
        outgoing_flux.reshape(2, comp_size, tile_size, slot_count),
        ("comp", "tile"),
        ("comp", "tile"),
        (1, 2),
        (1, 2),
    ).reshape(2, group_size, slot_count)
    forcing = (
        jnp.zeros((2, ocn_rows * ocn_cols), jnp.float32)
        .at[:, cell_index.reshape(-1)]
        .add(incoming_flux.reshape(2, -1))
        .reshape(2, ocn_rows, ocn_cols)
    )
    surface = jnp.stack([sea_temp, atm_surface_coef[0], atm_surface_coef[1]])[:, None]
    atm_now = atm_state
    for step_index in range(ASTEPS):
        padded = padded_2(atm_now, ((("comp", "tile"), 2), ("lev", 3)), 1)
        atm_now = atm_step(padded, surface, atm_diffusion)
    for step_index in range(OSTEPS):
        padded_ocean = padded_2(ocean_now, ((("comp", "tile"), 2), ("lev", 3)), 1)
        ocean_now = ocean_step(padded_ocean, ocn_diffusion, forcing, sea_frac)
    return (atm_now, ocean_now)


def solution(mesh):
    placed = (
        P(None, None, ("comp", "tile"), "lev"),
        P(),
        P(None, ("comp", "tile"), "lev"),
        P(None, None, ("comp", "tile"), "lev"),
        P(),
        P(("comp", "tile"), "lev"),
        P("lev", ("comp", "tile"), None, None),
        P("lev", ("comp", "tile"), None, None),
        P("lev", ("comp", "tile"), None, None),
        P("lev", ("comp", "tile"), None, None),
    )
    return jax.shard_map(
        shards,
        mesh=mesh,
        in_specs=placed,
        out_specs=(P(None, None, ("comp", "tile"), "lev"), P(None, None, ("comp", "tile"), "lev")),
        check_vma=False,
    )
```

profile of v0, /device:TPU:1, one launch (start us, length us, event | category | flops | bytes accessed | tf_op | source)
XLA Modules:
  0.0 1576.8 jit_solution(2475088307360962646)
XLA Ops:
  4.3 11.1 collective-permute-start.16
  17.3 362.7 %gather_fusion = f32[65536]{0:T(1024)S(1)} fusion(f32[7168]{0:T(1024)S(1)} %reshape_squeeze.10, s32[65536]{0:T(1024)S(1)} %broadcast_clamp_fusion.1), kind=kCustom, calls=%fused_computation | custom fusion | bytes 786432 | tf_op jit(solution)/shard_map/gather | solution.py:122
  381.0 10.7 all-to-all-start
  392.4 6.8 collective-permute-start
  404.3 8.1 fusion.18
  412.4 5.6 collective-permute-done.1
  418.0 8.0 fusion.52
  426.2 394.1 %scatter_custom_fusion = f32[2304]{0:T(1024)S(1)} fusion(s32[65536]{0:T(1024)S(1)} %bitcast.136, f32[65536]{0:T(1024)S(1)} %bitcast.137, f32[]{:T(128)} %constant.307.clone.1), kind=kCustom, calls=%fused_computation.179 | custom fusion | flops 65536 | bytes 9220 | tf_op jit(solution)/shard_map/scatter-add | solution.py:133
  824.8 215.5 %gather_fusion.1 = f32[65536,2]{1,0:T(8,128)} fusion(f32[2,2304]{0,1:T(8,128)S(1)} %copy.14, s32[65536]{0:T(1024)S(1)} %broadcast_clamp_fusion), kind=kCustom, calls=%fused_computation.1 | custom fusion | bytes 1310720 | tf_op jit(solution)/shard_map/gather | solution.py:139
  1040.3 17.6 %copy.15 = f32[2,4,1,32,512]{4,0,3,1,2:T(2,128)S(1)} copy(f32[2,4,1,32,512]{0,4,3,1,2:T(8,128)} %bitcast.109) | data formatting | bytes 1048576 | tf_op jit(solution)/shard_map/gather | solution.py:139
  1060.4 6.1 collective-permute-start.6
  1067.6 11.6 all-to-all-start.1
  1079.3 9.2 fusion.55
  1090.0 6.9 collective-permute-start.8
  1099.3 6.3 collective-permute-done.8
  1105.6 7.3 collective-permute-done.9
  1112.9 8.0 fusion.58
  1124.3 2.6 collective-permute-start.14
  1128.4 16.1 %copy.16 = f32[2,4,32,1,512]{0,4,2,1,3:T(8,128)} copy(f32[2,4,32,1,512]{4,0,2,1,3:T(2,128)} %bitcast.23) | data formatting | bytes 1048576 | tf_op jit(solution)/shard_map/transpose | solution.py:24
  1144.5 401.2 %scatter_custom_fusion.1 = f32[2,7168]{0,1:T(8,128)} fusion(s32[65536]{0:T(1024)} %bitcast.135, f32[65536,2]{1,0:T(8,128)} %bitcast.110, f32[]{:T(128)} %constant.307.clone.1), kind=kCustom, calls=%fused_computation.8 | custom fusion | flops 131072 | bytes 57856 | tf_op jit(solution)/shard_map/scatter-add | solution.py:150
  1545.7 6.2 fusion
  1554.7 4.7 collective-permute-start.22
  1559.8 9.2 fusion.61
  1569.1 6.1 fusion.9
  (141 shorter events, 33.4 us)
Async XLA Ops:
  4.3 399.4 %collective-permute-start.16 = (f32[2,24,1,1792]{3,2,1,0:T(1,128)}, f32[2,24,1,1792]{3,2,1,0:T(1,128)}, u32[]{:S(2)}, u32[]{:S(2)}) collective-permute-start(f32[2,24,1,1792]{3,2,1,0:T(1,128)} %get-tuple-element.167), channel_id=1, source_target_pairs={{2,0},{4,2},{6,4},{8,6},{10,8},{12,10},{14,12},{16,14},{18,16},{20... | collective-permute-start | bytes 1032200 | tf_op jit(solution)/shard_map/ppermute | solution.py:49
  15.4 389.0 %collective-permute-start.17 = (f32[2,24,1,1792]{3,2,1,0:T(1,128)}, f32[2,24,1,1792]{3,2,1,0:T(1,128)}, u32[]{:S(2)}, u32[]{:S(2)}) collective-permute-start(f32[2,24,1,1792]{3,2,1,0:T(1,128)} %get-tuple-element.166), channel_id=1, source_target_pairs={{0,2},{2,4},{4,6},{6,8},{8,10},{10,12},{12,14},{14,16},{16,18},{18... | collective-permute-start | bytes 1032200 | tf_op jit(solution)/shard_map/ppermute | solution.py:48
  16.1 386.1 %collective-permute-start.18 = (f32[2,24,4,1]{3,2,1,0:T(4,128)}, f32[2,24,4,1]{3,2,1,0:T(4,128)}, u32[]{:S(2)}, u32[]{:S(2)}) collective-permute-start(f32[2,24,4,1]{3,2,1,0:T(4,128)} %get-tuple-element.164), channel_id=1, source_target_pairs={{1,0},{0,1},{3,2},{2,3},{5,4},{4,5},{7,6},{6,7},{9,8},{8,9},{11,10... | collective-permute-start | bytes 2312 | tf_op jit(solution)/shard_map/ppermute | solution.py:49
  17.1 385.2 %collective-permute-start.19 = (f32[2,24,4,1]{3,2,1,0:T(4,128)}, f32[2,24,4,1]{3,2,1,0:T(4,128)}, u32[]{:S(2)}, u32[]{:S(2)}) collective-permute-start(f32[2,24,4,1]{3,2,1,0:T(4,128)} %get-tuple-element.165), channel_id=1, source_target_pairs={{0,1},{1,0},{2,3},{3,2},{4,5},{5,4},{6,7},{7,6},{8,9},{9,8},{10,11... | collective-permute-start | bytes 2312 | tf_op jit(solution)/shard_map/ppermute | solution.py:48
  381.0 45.1 %all-to-all-start = ((f32[128,1,1,512]{3,2,1,0:T(1,128)}), f32[128,1,1,512]{3,2,1,0:T(1,128)S(1)}, u32[]{:S(2)}, u32[]{:S(2)}) async-start(f32[128,1,1,512]{3,2,1,0:T(1,128)} %reshape_multiply_fusion), calls=%async_computation | async-start | bytes 524288 | tf_op jit(solution)/shard_map/all_to_all | solution.py:35
  392.4 20.0 %collective-permute-start = (f32[2,48,1,1152]{3,2,1,0:T(1,128)S(1)}, f32[2,48,1,1152]{3,2,1,0:T(1,128)S(1)}, u32[]{:S(2)}, u32[]{:S(2)}) collective-permute-start(f32[2,48,1,1152]{3,2,1,0:T(1,128)S(1)} %get-tuple-element.197), channel_id=1, source_target_pairs={{2,0},{4,2},{6,4},{8,6},{10,8},{12,10},{14,12},{16,14},{18,16},{20... | collective-permute-start | bytes 1327112 | tf_op jit(solution)/shard_map/ppermute | solution.py:49
  402.2 15.8 %collective-permute-start.1 = (f32[2,48,1,1152]{3,2,1,0:T(1,128)S(1)}, f32[2,48,1,1152]{3,2,1,0:T(1,128)S(1)}, u32[]{:S(2)}, u32[]{:S(2)}) collective-permute-start(f32[2,48,1,1152]{3,2,1,0:T(1,128)S(1)} %get-tuple-element.196), channel_id=1, source_target_pairs={{0,2},{2,4},{4,6},{6,8},{8,10},{10,12},{12,14},{14,16},{16,18},{18... | collective-permute-start | bytes 1327112 | tf_op jit(solution)/shard_map/ppermute | solution.py:48
  402.3 10.1 collective-permute-start.2
  403.7 8.7 collective-permute-start.3
  1057.9 21.3 %collective-permute-start.4 = (f32[2,48,1,1152]{3,2,1,0:T(1,128)}, f32[2,48,1,1152]{3,2,1,0:T(1,128)}, u32[]{:S(2)}, u32[]{:S(2)}) collective-permute-start(f32[2,48,1,1152]{3,2,1,0:T(1,128)} %get-tuple-element.189), channel_id=1, source_target_pairs={{2,0},{4,2},{6,4},{8,6},{10,8},{12,10},{14,12},{16,14},{18,16},{20... | collective-permute-start | bytes 1327112 | tf_op jit(solution)/shard_map/ppermute | solution.py:49
  1058.0 21.2 %collective-permute-start.5 = (f32[2,48,1,1152]{3,2,1,0:T(1,128)}, f32[2,48,1,1152]{3,2,1,0:T(1,128)}, u32[]{:S(2)}, u32[]{:S(2)}) collective-permute-start(f32[2,48,1,1152]{3,2,1,0:T(1,128)} %get-tuple-element.188), channel_id=1, source_target_pairs={{0,2},{2,4},{4,6},{6,8},{8,10},{10,12},{12,14},{14,16},{16,18},{18... | collective-permute-start | bytes 1327112 | tf_op jit(solution)/shard_map/ppermute | solution.py:48
  1060.4 18.9 %collective-permute-start.6 = (f32[2,48,2,1]{3,2,1,0:T(2,128)}, f32[2,48,2,1]{3,2,1,0:T(2,128)}, u32[]{:S(2)}, u32[]{:S(2)}) collective-permute-start(f32[2,48,2,1]{3,2,1,0:T(2,128)} %get-tuple-element.186), channel_id=1, source_target_pairs={{1,0},{0,1},{3,2},{2,3},{5,4},{4,5},{7,6},{6,7},{9,8},{8,9},{11,10... | collective-permute-start | bytes 2312 | tf_op jit(solution)/shard_map/ppermute | solution.py:49
  1066.5 12.8 collective-permute-start.7
  1067.6 60.8 %all-to-all-start.1 = ((f32[128,2,1,1,512]{4,1,3,2,0:T(2,128)}), f32[128,2,1,1,512]{4,1,3,2,0:T(2,128)}, u32[]{:S(2)}, u32[]{:S(2)}) async-start(f32[128,2,1,1,512]{4,1,3,2,0:T(2,128)} %bitcast.124), calls=%async_computation.1 | async-start | bytes 1048576 | tf_op jit(solution)/shard_map/all_to_all | solution.py:35
  1090.0 15.6 collective-permute-start.8
  1096.9 16.0 %collective-permute-start.9 = (f32[2,48,1,1152]{3,2,1,0:T(1,128)S(1)}, f32[2,48,1,1152]{3,2,1,0:T(1,128)S(1)}, u32[]{:S(2)}, u32[]{:S(2)}) collective-permute-start(f32[2,48,1,1152]{3,2,1,0:T(1,128)S(1)} %get-tuple-element.180), channel_id=1, source_target_pairs={{0,2},{2,4},{4,6},{6,8},{8,10},{10,12},{12,14},{14,16},{16,18},{18... | collective-permute-start | bytes 1327112 | tf_op jit(solution)/shard_map/ppermute | solution.py:48
  1122.7 436.7 %collective-permute-start.12 = (f32[2,48,1,1152]{3,2,1,0:T(1,128)}, f32[2,48,1,1152]{3,2,1,0:T(1,128)}, u32[]{:S(2)}, u32[]{:S(2)}) collective-permute-start(f32[2,48,1,1152]{3,2,1,0:T(1,128)} %get-tuple-element.173), channel_id=1, source_target_pairs={{2,0},{4,2},{6,4},{8,6},{10,8},{12,10},{14,12},{16,14},{18,16},{20... | collective-permute-start | bytes 1327112 | tf_op jit(solution)/shard_map/ppermute | solution.py:49
  1123.1 436.7 %collective-permute-start.13 = (f32[2,48,1,1152]{3,2,1,0:T(1,128)}, f32[2,48,1,1152]{3,2,1,0:T(1,128)}, u32[]{:S(2)}, u32[]{:S(2)}) collective-permute-start(f32[2,48,1,1152]{3,2,1,0:T(1,128)} %get-tuple-element.172), channel_id=1, source_target_pairs={{0,2},{2,4},{4,6},{6,8},{8,10},{10,12},{12,14},{14,16},{16,18},{18... | collective-permute-start | bytes 1327112 | tf_op jit(solution)/shard_map/ppermute | solution.py:48
  1124.3 430.5 %collective-permute-start.14 = (f32[2,48,2,1]{3,2,1,0:T(2,128)S(1)}, f32[2,48,2,1]{3,2,1,0:T(2,128)}, u32[]{:S(2)}, u32[]{:S(2)}) collective-permute-start(f32[2,48,2,1]{3,2,1,0:T(2,128)S(1)} %get-tuple-element.170), channel_id=1, source_target_pairs={{1,0},{0,1},{3,2},{2,3},{5,4},{4,5},{7,6},{6,7},{9,8},{8,9},{11,10... | collective-permute-start | bytes 2312 | tf_op jit(solution)/shard_map/ppermute | solution.py:49
  1126.8 427.9 %collective-permute-start.15 = (f32[2,48,2,1]{3,2,1,0:T(2,128)S(1)}, f32[2,48,2,1]{3,2,1,0:T(2,128)}, u32[]{:S(2)}, u32[]{:S(2)}) collective-permute-start(f32[2,48,2,1]{3,2,1,0:T(2,128)S(1)} %get-tuple-element.171), channel_id=1, source_target_pairs={{0,1},{1,0},{2,3},{3,2},{4,5},{5,4},{6,7},{7,6},{8,9},{9,8},{10,11... | collective-permute-start | bytes 2312 | tf_op jit(solution)/shard_map/ppermute | solution.py:48
  1553.1 16.0 %collective-permute-start.20 = (f32[2,24,1,1792]{3,2,1,0:T(1,128)S(1)}, f32[2,24,1,1792]{3,2,1,0:T(1,128)S(1)}, u32[]{:S(2)}, u32[]{:S(2)}) collective-permute-start(f32[2,24,1,1792]{3,2,1,0:T(1,128)S(1)} %get-tuple-element.159), channel_id=1, source_target_pairs={{2,0},{4,2},{6,4},{8,6},{10,8},{12,10},{14,12},{16,14},{18,16},{20... | collective-permute-start | bytes 1032200 | tf_op jit(solution)/shard_map/ppermute | solution.py:49
  1554.7 14.4 collective-permute-start.21
  1554.7 14.3 collective-permute-start.22
  1559.4 9.6 collective-permute-start.23
  (17 other events, 949.7 us)
where the time goes:
time: 1590 us; the launch traced here: 1580 us
  other arithmetic  857 us (54%)
  local copies, waits for them, and re-layouts  627 us (39%)
  starting transfers between devices  69.9 us (4%)
  waiting for transfers between devices  20.6 us (1%)
    scatter-add x1, other arithmetic, shards(): forcing = jnp.zeros((2, ocn_rows * ocn_cols), jnp.float32).at[:, cell_ind...  401 us
    scatter-add x1, other arithmetic, shards(): sea_temp = jnp.zeros((atm_rows * atm_cols,), jnp.float32).at[col_index.re...  394 us
    gather x1, local copies, waits for them, and re-layouts, shards(): outgoing = o2a_weights[0, 0] * top_temp[cell_index]  363 us
    gather x2, local copies, waits for them, and re-layouts, shards(): outgoing_flux = a2o_weights[0, 0][None] * fluxes[:, col_index]  233 us
    ppermute x12, starting transfers between devices, padded_2(): lax.ppermute(first, axis, [(b, a) for a, b in up])  43.7 us
    add x4, other arithmetic, atm_step(): middle + diffusion[None, :, None, None] * lateral  34.4 us
  transfers between devices with their start and end apart: 26, of which 5 were waited for; matrix products, arithmetic and copies ran while one was open for 53% of the time, Pallas kernels for 0%

commit v1 on v0

v1 whole, which is shorter than its diff:
```python
import functools

import jax
import jax.numpy as jnp
from jax import lax
from jax.experimental import pallas as pl
from jax.experimental.pallas import tpu as pltpu
from jax.sharding import PartitionSpec as P

ASTEPS = 4
OSTEPS = 2
VERT_MIX = 0.1
OCEAN_MIX = 0.15
HEAT_GAIN = 2.0
SALT_GAIN = 1.0
MOIST_RATIO = 0.8
LANES = 128
GROUP = ("comp", "tile")
F32, BF16 = jnp.float32, jnp.bfloat16


SPLITS = 3


def parts_of(v):
    out = []
    for _ in range(SPLITS):
        p = v.astype(BF16)
        out.append(p)
        v = v - p.astype(F32)
    return out


def spread(row):
    return jnp.broadcast_to(row.astype(F32), (16, row.shape[1])).astype(BF16)


def hits(row, size):
    b = spread(row)
    base = lax.broadcasted_iota(jnp.int32, b.shape, 0).astype(F32)
    return [b == (base + 16.0 * j).astype(BF16) for j in range(size // 16)]


def one_hot(row, size):
    masks = hits(row, size)
    one, zero = jnp.ones(masks[0].shape, BF16), jnp.zeros(masks[0].shape, BF16)
    return jnp.concatenate([jnp.where(m, one, zero) for m in masks], axis=0)


def gather_loop(t_ref, index_ref, w_ref, out_ref, split, H, L, F):
    def group(g, c):
        base = pl.multiple_of(g * 8, 8)
        hi, lo = split(index_ref[pl.ds(base, 8), :])
        w = w_ref[pl.ds(base, 8), :]
        for r in range(8):
            hot = jnp.concatenate([one_hot(hi[r : r + 1], H)] * SPLITS, axis=0)
            o = jnp.dot(t_ref[...], hot, preferred_element_type=F32)
            rows = lax.broadcasted_iota(jnp.int32, (L, o.shape[1]), 0)
            mine = rows == lo[r : r + 1]
            for f in range(F):
                picked = jnp.where(mine, o[f * L : (f + 1) * L], 0.0)
                value = jnp.sum(picked, axis=0, keepdims=True) * w[r : r + 1]
                for q in range(4):
                    out_ref[base + r, 4 * f + q : 4 * f + q + 1, :] = value[:, q * 128 : (q + 1) * 128]
        return c
    lax.fori_loop(0, index_ref.shape[0] // 8, group, 0)


def scatter_loop(val_ref, index_ref, H, L, F):
    shift = L.bit_length() - 1
    def group(g, acc):
        base = pl.multiple_of(g * 8, 8)
        index = index_ref[pl.ds(base, 8), :]
        hi, lo = index >> shift, index & (L - 1)
        for r in range(8):
            masks = hits(hi[r : r + 1], H)
            a = []
            for f in range(F):
                v = jnp.concatenate([val_ref[base + r, 4 * f + q : 4 * f + q + 1, :] for q in range(4)], axis=1)
                for p in parts_of(jnp.broadcast_to(v, (16, v.shape[1]))):
                    a += [jnp.where(m, p, jnp.zeros_like(p)) for m in masks]
            a = jnp.concatenate(a, axis=0)
            acc = acc + lax.dot_general(a, one_hot(lo[r : r + 1], L), (((1,), (1,)), ((), ())), preferred_element_type=F32)
        return acc
    acc = lax.fori_loop(0, index_ref.shape[0] // 8, group, jnp.zeros((F * SPLITS * H, L), F32))
    return [sum(acc[(f * SPLITS + i) * H : (f * SPLITS + i + 1) * H] for i in range(SPLITS)) for f in range(F)]


def temp_kernel(table_ref, cell_ref, w_ref, out_ref, t_ref):
    t_ref[...] = jnp.concatenate(parts_of(table_ref[...].T), axis=1)
    gather_loop(t_ref, cell_ref, w_ref, out_ref, lambda i: (i >> 7, i & 127), 64, 128, 1)


def flux_kernel(val_ref, col_ref, state_ref, coef_ref, temp_ref, t_ref):
    temp, = scatter_loop(val_ref, col_ref, 32, 128, 1)
    temp_ref[...] = temp
    tables = []
    for f in range(2):
        flux = coef_ref[f] * (state_ref[f] - (1.0, MOIST_RATIO)[f] * temp)
        halves = jnp.concatenate([flux[:24, :64], flux[:24, 64:]], axis=0)
        tables.append(jnp.concatenate(parts_of(halves.T), axis=1))
    t_ref[...] = jnp.concatenate(tables, axis=0)


def half_split(i):
    return (i >> 7) + 24 * ((i >> 6) & 1), i & 63


def send_kernel(t_ref, col_ref, w_ref, out_ref):
    gather_loop(t_ref, col_ref, w_ref, out_ref, half_split, 48, 64, 2)


def forcing_kernel(val_ref, cell_ref, out_ref):
    sums = scatter_loop(val_ref, cell_ref, 32, 256, 2)
    out_ref[0] = HEAT_GAIN * sums[0][:28]
    out_ref[1] = -SALT_GAIN * sums[1][:28]


VM = pl.BlockSpec(memory_space=pltpu.VMEM)


def tile_steps(tile, before, after, other, diffusion, vertical):
    above = jnp.concatenate([tile[1:], tile[-1:]], axis=0)
    below = jnp.concatenate([tile[:1], tile[:-1]], axis=0)
    lateral = other + after + before - 4.0 * tile
    return tile + diffusion * lateral + vertical * (above + below - 2.0 * tile)


def stepped_row(get, get_up, get_down, f, tiles, left, right, diffusion, vertical, finish):
    lane = lax.broadcasted_iota(jnp.int32, left.shape, 1)
    values = [get(f, j) for j in range(tiles)]
    to_right = [pltpu.roll(v, 1, 1) for v in values]
    to_left = [pltpu.roll(v, LANES - 1, 1) for v in values]
    ends = []
    for j in range(tiles):
        before = jnp.where(lane == 0, left if j == 0 else to_right[j - 1], to_right[j])
        after = jnp.where(lane == LANES - 1, right if j == tiles - 1 else to_left[j + 1], to_left[j])
        other = get_down(f, j) + get_up(f, j)
        fresh = tile_steps(values[j], before, after, other, diffusion, vertical)
        fresh = finish(f, j, fresh, values[j])
        if j in (0, tiles - 1):
            ends.append(fresh)
    return ends


def edges_of(rows):
    lane = lax.broadcasted_iota(jnp.int32, rows[0][0].shape, 1)
    out = jnp.zeros(rows[0][0].shape, F32)
    for i, (first, last) in enumerate(rows):
        out = jnp.where(lane == 2 * i, pltpu.roll(first, 2 * i, 1) if i else first, out)
        out = jnp.where(lane == 2 * i + 1, pltpu.roll(last, 2 * i + 2, 1), out)
    return out


def edge(edges, i):
    return jnp.broadcast_to(edges[:, i : i + 1], edges.shape)


def atm_kernel(row0, row1, up, down, edges_ref, diff_ref, coef_ref, temp_ref, out0, out1, out_edges):
    tiles = row0.shape[1]
    edges, diffusion = edges_ref[...], diff_ref[...]
    top = lax.broadcasted_iota(jnp.int32, (8, LANES), 0) == 0
    rows = [up, row0, row1, down]
    ends = []
    for r, out in enumerate((out0, out1)):
        def finish(f, j, fresh, old, r=r, out=out):
            at = r * tiles + j
            gain = (1.0, MOIST_RATIO)[f] * temp_ref[at : at + 1, :]
            gain = coef_ref[f, at : at + 1, :] * (gain - old[:1])
            fresh = jnp.concatenate([fresh[:8] + jnp.where(top, gain, 0.0), fresh[8:]], axis=0)
            out[f, j] = fresh
            return fresh
        for f in range(2):
            i = 2 * r + f
            ends.append(stepped_row(*(lambda f, j, ref=ref: ref[f, j] for ref in (rows[r + 1], rows[r], rows[r + 2])), f, tiles, edge(edges, 2 * i + 1), edge(edges, 2 * i), diffusion, VERT_MIX, finish))
    out_edges[...] = edges_of(ends)


def atm_stepped(row0, row1, up, down, edges, diffusion, coef, temp):
    row = jax.ShapeDtypeStruct(row0.shape, F32)
    return pl.pallas_call(
        atm_kernel,
        out_shape=(row, row, jax.ShapeDtypeStruct(edges.shape, F32)),
        in_specs=[VM] * 8,
        out_specs=(VM,) * 3,
        cost_estimate=pl.CostEstimate(flops=12 * 4 * row0.size, bytes_accessed=24 * row0.size, transcendentals=0),
        name="atm_step",
    )(row0, row1, up, down, edges, diffusion, coef, temp)


def ocn_kernel(own, up, down, edges_ref, diff_ref, frac_ref, out, out_edges):
    count, _, tiles = own.shape[:3]
    edges, diffusion = edges_ref[...], diff_ref[...]
    rows = [up] + [own.at[r] for r in range(count)] + [down]
    ends = []
    for r in range(count):
        def finish(f, j, fresh, old, r=r):
            fresh = fresh * frac_ref[r * tiles + j : r * tiles + j + 1, :]
            out[r, f, j] = fresh
            return fresh
        for f in range(2):
            i = 2 * r + f
            ends.append(stepped_row(*(lambda f, j, ref=ref: ref[f, j] for ref in (rows[r + 1], rows[r], rows[r + 2])), f, tiles, edge(edges, 2 * i + 1), edge(edges, 2 * i), diffusion, OCEAN_MIX, finish))
    out_edges[...] = edges_of(ends)


def ocn_stepped(own, up, down, edges, diffusion, frac):
    return pl.pallas_call(
        ocn_kernel,
        out_shape=(jax.ShapeDtypeStruct(own.shape, F32), jax.ShapeDtypeStruct(edges.shape, F32)),
        in_specs=[VM] * 6,
        out_specs=(VM,) * 2,
        cost_estimate=pl.CostEstimate(flops=12 * own.size, bytes_accessed=12 * own.size, transcendentals=0),
        name="ocn_step",
    )(own, up, down, edges, diffusion, frac)


def call(kernel, name, flops, out_shape, *args, scratch=()):
    return pl.pallas_call(
        kernel,
        out_shape=out_shape,
        in_specs=[VM] * len(args),
        out_specs=jax.tree.map(lambda _: VM, out_shape),
        scratch_shapes=list(scratch),
        cost_estimate=pl.CostEstimate(flops=flops, bytes_accessed=1 << 20, transcendentals=0),
        name=name,
    )(*args)


def by_rows(field):
    fields, levels, rows, cols = field.shape
    return field.reshape(fields, levels, rows, cols // LANES, LANES).transpose(2, 0, 3, 1, 4)


def from_rows(tiles):
    rows, fields, count, levels, lanes = tiles.shape
    return tiles.transpose(1, 3, 0, 2, 4).reshape(fields, levels, rows, count * lanes)


def row_halos(first, last):
    count = lax.axis_size(GROUP)
    up = [(i, (i + 1) % count) for i in range(count)]
    return lax.ppermute(last, GROUP, up), lax.ppermute(first, GROUP, [(b, a) for a, b in up])


def partner(edges):
    count = lax.axis_size("lev")
    return lax.ppermute(edges, "lev", [(i, (i + 1) % count) for i in range(count)])


def first_edges(field):
    ends = jnp.stack([field[..., 0], field[..., -1]], axis=-1)
    ends = ends.transpose(1, 2, 0, 3).reshape(field.shape[1], -1)
    return jnp.pad(ends, ((0, 0), (0, LANES - ends.shape[1])))


def shards(
    atm_state,
    atm_diffusion,
    atm_surface_coef,
    ocn_state,
    ocn_diffusion,
    sea_mask,
    atm_pair_cols,
    a2o_weights,
    ocn_pair_cells,
    o2a_weights,
):
    group_size = lax.axis_size(GROUP)
    my_block = lax.axis_index(GROUP)
    atm_levels, atm_rows, atm_cols = atm_state.shape[1:]
    ocn_levels, ocn_rows, ocn_cols = ocn_state.shape[1:]
    slots = atm_pair_cols.shape[3]
    shape = lambda *s: jax.ShapeDtypeStruct(s, F32)

    row_ids = my_block * ocn_rows + jnp.arange(ocn_rows, dtype=jnp.int32)
    inner_rows = ((row_ids > 0) & (row_ids < ocn_rows * group_size - 1)).astype(F32)
    sea_frac = sea_mask.astype(F32) * inner_rows[:, None]
    ocean_start = ocn_state * sea_frac[None, None]
    cols, cells = atm_pair_cols[0, 0], ocn_pair_cells[0, 0]

    table = jnp.pad((ocn_state[0, 0] * sea_frac).reshape(-1, LANES), ((0, 8), (0, 0)))
    outgoing = call(temp_kernel, "temp_gather", 1 << 33, shape(group_size, slots // LANES, LANES), table, cells, o2a_weights[0, 0], scratch=[pltpu.VMEM((128, SPLITS * 64), BF16)])
    incoming = lax.all_to_all(outgoing, GROUP, split_axis=0, concat_axis=0, tiled=True)

    atm = by_rows(atm_state)
    row0, row1 = atm[0], atm[1]
    atm_diff = jnp.broadcast_to(atm_diffusion[:, None], (atm_levels, LANES))
    edges = first_edges(atm_state)
    ocean = by_rows(ocean_start)
    ocn_diff = jnp.broadcast_to(ocn_diffusion[:, None], (ocn_levels, LANES))
    frac_tiles = sea_frac.reshape(-1, LANES)
    ocn_edges = first_edges(ocean_start)

    up, down = row_halos(row0, row1)
    beside = partner(edges)
    ocean, ocn_edges = ocn_stepped(ocean, *row_halos(ocean[0], ocean[-1]), partner(ocn_edges), ocn_diff, frac_tiles)

    pad = ((0, 0), (0, 32 - atm_rows * atm_cols // LANES), (0, 0))
    coef = jnp.pad(atm_surface_coef.reshape(2, -1, LANES), pad)
    surface = jnp.pad(atm_state[:, 0].reshape(2, -1, LANES), pad)
    temp, flux_table = call(flux_kernel, "temp_scatter", 1 << 33, (shape(32, LANES), jax.ShapeDtypeStruct((128, SPLITS * 48), BF16)), incoming, cols, surface, coef)
    outgoing = call(send_kernel, "flux_gather", 1 << 33, shape(group_size, 2 * slots // LANES, LANES), flux_table, cols, a2o_weights[0, 0])
    incoming = lax.all_to_all(outgoing, GROUP, split_axis=0, concat_axis=0, tiled=True)

    for step in range(ASTEPS):
        row0, row1, edges = atm_stepped(row0, row1, up, down, beside, atm_diff, coef, temp)
        if step < ASTEPS - 1:
            up, down = row_halos(row0, row1)
            beside = partner(edges)
    atm_next = from_rows(jnp.stack([row0, row1]))

    ocean, _ = ocn_stepped(ocean, *row_halos(ocean[0], ocean[-1]), partner(ocn_edges), ocn_diff, frac_tiles)
    ocean = from_rows(ocean)

    forcing = call(forcing_kernel, "forcing_scatter", 1 << 33, shape(2, 28, 256), incoming, cells).reshape(2, ocn_rows, ocn_cols)
    gained = forcing * sea_frac
    above, below = row_halos(gained[:, :1], gained[:, -1:])
    ends = partner(jnp.stack([gained[:, :, 0], gained[:, :, -1]]))
    tall = jnp.concatenate([above, gained, below], axis=1)
    wide = jnp.concatenate([ends[1][:, :, None], gained, ends[0][:, :, None]], axis=2)
    lateral = tall[:, 2:] + tall[:, :-2] + wide[:, :, 2:] + wide[:, :, :-2] - 4.0 * gained
    second = gained + ocn_diffusion[0] * lateral - OCEAN_MIX * gained + forcing
    added = jnp.stack([second, OCEAN_MIX * gained], axis=1) * sea_frac
    return (atm_next, ocean.at[:, :2].add(added))


def solution(mesh):
    across = P(None, None, GROUP, "lev")
    pairs = P("lev", GROUP, None, None)
    placed = (across, P(), P(None, GROUP, "lev"), across, P(), P(GROUP, "lev"), pairs, pairs, pairs, pairs)
    return jax.shard_map(shards, mesh=mesh, in_specs=placed, out_specs=(across, across), check_vma=False)
```

time: 1590 us -> 217 us (0.14)
  other arithmetic: 857 us -> 9.71 us
  local copies, waits for them, and re-layouts: 627 us -> 30.5 us
  Pallas kernels: 0 us -> 64.1 us
    scatter-add x14 -> x0, other arithmetic: 796 us -> none  [the longest x1 401 us: shards(): forcing = jnp.zeros((2, ocn_rows * ocn_cols), jnp.float32).at[:, cell_ind...]
    gather x3 -> x0, local copies, waits for them, and re-layouts: 596 us -> none  [the longest x1 363 us: shards(): outgoing = o2a_weights[0, 0] * top_temp[cell_index]]
    pallas_call x0 -> x10, Pallas kernels: none -> 64.1 us  [the longest x4 44.4 us: call(): pl.pallas_call(kernel, out_shape=out_shape, in_specs=[VM] * len(args), ou...]
    add x6 -> x1, other arithmetic: 48.5 us -> 0.06 us  [shards(): return (atm_next, ocean.at[:, :2].add(added))]
    ppermute x24 -> x21, starting transfers between devices: 47.6 us -> 56.7 us  [the longest x7 46.6 us: row_halos(): lax.ppermute(first, GROUP, [(b, a) for a, b in up])]
  transfers between devices with their start and end apart: 26 -> 23, of which waited for: 5 -> 6; matrix products, arithmetic and copies ran while one was open for 53% -> 14% of each run, Pallas kernels for 0% -> 24%
where the time goes in v1:
time: 217 us
  starting transfers between devices  83.3 us (38%)
  Pallas kernels  64.1 us (30%)
  local copies, waits for them, and re-layouts  30.5 us (14%)
  waiting for transfers between devices  27.8 us (13%)
  other arithmetic  9.71 us (4%)
    ppermute x7, starting transfers between devices, row_halos(): lax.ppermute(first, GROUP, [(b, a) for a, b in up])  46.6 us
    pallas_call x4, Pallas kernels, call(): pl.pallas_call(kernel, out_shape=out_shape, in_specs=[VM] * len(args), ou...  44.4 us
    all_to_all x2, starting transfers between devices, shards(): lax.all_to_all(outgoing, GROUP, split_axis=0, concat_axis=0, tiled=True)  26.6 us
    ppermute x7, waiting for transfers between devices, row_halos(): lax.ppermute(last, GROUP, up)  25.6 us
    unnamed x59, local copies, waits for them, and re-layouts  13.9 us
    pallas_call x4, Pallas kernels, atm_stepped(): pl.pallas_call(atm_kernel, out_shape=(row, row, jax.ShapeDtypeStruct(edge...  12.3 us
    ppermute x7, starting transfers between devices, partner(): lax.ppermute(edges, 'lev', [(i, (i + 1) % count) for i in range(count)])  8.81 us
    mul x1, other arithmetic, shards(): ocean_start = ocn_state * sea_frac[None, None]  7.36 us
  transfers between devices with their start and end apart: 23, of which 6 were waited for; matrix products, arithmetic and copies ran while one was open for 14% of the time, Pallas kernels for 24%

profile of v1, /device:TPU:1, one launch (start us, length us, event | category | flops | bytes accessed | tf_op | source)
XLA Modules:
  0.0 216.6 jit_solution(2323724805575308343)
XLA Ops:
  2.1 9.8 %temp_gather.1 = f32[128,4,128]{2,1,0:T(4,128)} custom-call(f32[64,128]{1,0:T(8,128)} %pad.23.table_ref, s32[128,512]{1,0:T(8,128)} %bitcast.74, f32[128,512]{1,0:T(8,128)} %bitcast.70), custom_call_target="tpu_custom_call" | custom-call | flops 8589934592 | bytes 1048576 | tf_op jit(solution)/shard_map/temp_gather/pallas_call | solution.py:219
  11.9 16.9 %all-to-all-start = ((f32[128,4,128]{2,1,0:T(4,128)}), f32[128,4,128]{2,1,0:T(4,128)}, u32[]{:S(2)}, u32[]{:S(2)}) async-start(f32[128,4,128]{2,1,0:T(4,128)} %temp_gather.1), calls=%async_computation | async-start | bytes 524288 | tf_op jit(solution)/shard_map/all_to_all | solution.py:284
  30.8 6.4 %collective-permute-start.1 = (f32[2,9,48,128]{3,2,1,0:T(8,128)S(1)}, f32[2,9,48,128]{3,2,1,0:T(8,128)}, u32[]{:S(2)}, u32[]{:S(2)}) collective-permute-start(f32[2,9,48,128]{3,2,1,0:T(8,128)S(1)} %get-tuple-element.65.row0), channel_id=1, source_target_pairs={{2,0},{4,2},{6,4},{8,6},{10,8},{12,10},{14,12},{16,14},{18,16},{20... | collective-permute-start | bytes 1327112 | tf_op jit(solution)/shard_map/ppermute | solution.py:243
  39.2 5.1 %copy.59 = f32[2,24,4,1792]{1,2,3,0:T(4,128)} copy(f32[2,24,4,1792]{3,2,1,0:T(4,128)S(1)} %copy-done.4) | data formatting | bytes 2752512 | tf_op args[3]
  44.7 7.4 %broadcast_multiply_fusion = f32[2,24,4,1792]{1,2,3,0:T(4,128)} fusion(f32[2,24,4,1792]{1,2,3,0:T(4,128)} %copy.59, f32[4,1792]{0,1:T(8,128)S(1)} %copy.58), kind=kLoop, calls=%fused_computation | loop fusion | flops 344064 | bytes 2781184 | tf_op jit(solution)/shard_map/mul | solution.py:279
  52.0 5.8 %copy.61 = f32[2,24,4,14,128]{4,1,3,0,2:T(8,128)S(1)} copy(f32[2,24,4,14,128]{1,2,4,3,0:T(4,128)} %bitcast.53) | data formatting | bytes 2752512 | tf_op jit(solution)/shard_map/reshape | solution.py:232
  59.1 9.6 %temp_scatter.1 = (f32[32,128]{1,0:T(8,128)}, bf16[128,144]{1,0:T(8,128)(2,1)}) custom-call(f32[128,4,128]{2,1,0:T(4,128)} %all-to-all-done.val_ref, s32[128,512]{1,0:T(8,128)} %bitcast.71, f32[2,32,128]{2,1,0:T(8,128)} %pad.24.state_ref, f32[2,32,128]{2,1,0:T(8,128)} %pad.22.coef_ref), custom_call_target="tpu_custom_call" | custom-call | flops 8589934592 | bytes 1048576 | tf_op jit(solution)/shard_map/temp_scatter/pallas_call | solution.py:219
  68.7 10.0 %flux_gather.1 = f32[128,8,128]{2,1,0:T(8,128)} custom-call(bf16[128,144]{1,0:T(8,128)(2,1)} %get-tuple-element.45.t_ref, s32[128,512]{1,0:T(8,128)} %bitcast.72, f32[128,512]{1,0:T(8,128)} %bitcast.73), custom_call_target="tpu_custom_call" | custom-call | flops 8589934592 | bytes 1048576 | tf_op jit(solution)/shard_map/flux_gather/pallas_call | solution.py:219
  78.7 9.8 %all-to-all-start.1 = ((f32[128,8,128]{2,1,0:T(8,128)}), f32[128,8,128]{2,1,0:T(8,128)}, u32[]{:S(2)}, u32[]{:S(2)}) async-start(f32[128,8,128]{2,1,0:T(8,128)} %flux_gather.1), calls=%async_computation.1 | async-start | bytes 1048576 | tf_op jit(solution)/shard_map/all_to_all | solution.py:304
  89.2 3.1 %atm_step.4 = (f32[2,9,48,128]{3,2,1,0:T(8,128)}, f32[2,9,48,128]{3,2,1,0:T(8,128)}, f32[48,128]{1,0:T(8,128)}) custom-call(f32[2,9,48,128]{3,2,1,0:T(8,128)} %copy-done.3, f32[2,9,48,128]{3,2,1,0:T(8,128)} %copy-done.2, f32[2,9,48,128]{3,2,1,0:T(8,128)} %collective-permute-done.up, f32[2,9,48,128]{3,2,1,0:T(8,128)} %collective-permute-done.1.down, ...), custom_call_target="tpu_custom_call" | custom-call | flops 5308416 | bytes 2654208 | tf_op jit(solution)/shard_map/atm_step/pallas_call | solution.py:181
  92.8 6.4 %collective-permute-start.4 = (f32[2,9,48,128]{3,2,1,0:T(8,128)}, f32[2,9,48,128]{3,2,1,0:T(8,128)S(1)}, u32[]{:S(2)}, u32[]{:S(2)}) collective-permute-start(f32[2,9,48,128]{3,2,1,0:T(8,128)} %get-tuple-element.31.row0), channel_id=1, source_target_pairs={{2,0},{4,2},{6,4},{8,6},{10,8},{12,10},{14,12},{16,14},{18,16},{20... | collective-permute-start | bytes 1327112 | tf_op jit(solution)/shard_map/ppermute | solution.py:243
  99.3 6.9 %collective-permute-start.13 = (f32[2,14,24,128]{3,2,1,0:T(8,128)S(1)}, f32[2,14,24,128]{3,2,1,0:T(8,128)S(1)}, u32[]{:S(2)}, u32[]{:S(2)}) collective-permute-start(f32[2,14,24,128]{3,2,1,0:T(8,128)S(1)} %get-tuple-element.60), channel_id=1, source_target_pairs={{2,0},{4,2},{6,4},{8,6},{10,8},{12,10},{14,12},{16,14},{18,16},{20... | collective-permute-start | bytes 1032200 | tf_op jit(solution)/shard_map/ppermute | solution.py:243
  110.3 12.2 %collective-permute-done.12.up = f32[2,14,24,128]{3,2,1,0:T(8,128)S(1)} collective-permute-done((f32[2,14,24,128]{3,2,1,0:T(8,128)S(1)}, f32[2,14,24,128]{3,2,1,0:T(8,128)S(1)}, u32[]{:S(2)}, u32[]{:S(2)}) %collective-permute-start.12) | collective-permute-done | bytes 344096 | tf_op jit(solution)/shard_map/ppermute | solution.py:243
  123.4 3.7 %ocn_step.2 = (f32[4,2,14,24,128]{4,3,2,1,0:T(8,128)}, f32[24,128]{1,0:T(8,128)}) custom-call(f32[4,2,14,24,128]{4,3,2,1,0:T(8,128)} %bitcast.55, f32[2,14,24,128]{3,2,1,0:T(8,128)} %copy-done.10, f32[2,14,24,128]{3,2,1,0:T(8,128)} %copy-done.11, f32[24,128]{1,0:T(8,128)} %copy-done.19, f32[24,128]{1,0:T(8,128)} %broadcast_in_dim.5.diff_ref, ...), custom_call_target="tpu_custom_call" | custom-call | flops 4128768 | bytes 4128768 | tf_op jit(solution)/shard_map/ocn_step/pallas_call | solution.py:208
  131.7 6.9 %collective-permute-start.7 = (f32[2,9,48,128]{3,2,1,0:T(8,128)}, f32[2,9,48,128]{3,2,1,0:T(8,128)}, u32[]{:S(2)}, u32[]{:S(2)}) collective-permute-start(f32[2,9,48,128]{3,2,1,0:T(8,128)} %get-tuple-element.34.row0), channel_id=1, source_target_pairs={{2,0},{4,2},{6,4},{8,6},{10,8},{12,10},{14,12},{16,14},{18,16},{20... | collective-permute-start | bytes 1327112 | tf_op jit(solution)/shard_map/ppermute | solution.py:243
  138.8 6.9 %collective-permute-start.16 = (f32[2,14,24,128]{3,2,1,0:T(8,128)S(1)}, f32[2,14,24,128]{3,2,1,0:T(8,128)S(1)}, u32[]{:S(2)}, u32[]{:S(2)}) collective-permute-start(f32[2,14,24,128]{3,2,1,0:T(8,128)S(1)} %get-tuple-element.58), channel_id=1, source_target_pairs={{2,0},{4,2},{6,4},{8,6},{10,8},{12,10},{14,12},{16,14},{18,16},{20... | collective-permute-start | bytes 1032200 | tf_op jit(solution)/shard_map/ppermute | solution.py:243
  149.1 6.1 %collective-permute-done.15.up = f32[2,14,24,128]{3,2,1,0:T(8,128)S(1)} collective-permute-done((f32[2,14,24,128]{3,2,1,0:T(8,128)S(1)}, f32[2,14,24,128]{3,2,1,0:T(8,128)S(1)}, u32[]{:S(2)}, u32[]{:S(2)}) %collective-permute-start.15) | collective-permute-done | bytes 344096 | tf_op jit(solution)/shard_map/ppermute | solution.py:243
  156.8 3.6 %ocn_step.3 = (f32[4,2,14,24,128]{4,3,2,1,0:T(8,128)}, f32[24,128]{1,0:T(8,128)}) custom-call(f32[4,2,14,24,128]{4,3,2,1,0:T(8,128)} %get-tuple-element.42.own, f32[2,14,24,128]{3,2,1,0:T(8,128)} %copy-done.12, f32[2,14,24,128]{3,2,1,0:T(8,128)} %copy-done.13, f32[24,128]{1,0:T(8,128)} %copy-done.20, f32[24,128]{1,0:T(8,128)} %broadcast_in_dim.5.diff_ref, ...), custom_call_target="tpu_custom_call" | custom-call | flops 4128768 | bytes 4128768 | tf_op jit(solution)/shard_map/ocn_step/pallas_call | solution.py:208
  162.9 3.1 %atm_step.6 = (f32[2,9,48,128]{3,2,1,0:T(8,128)}, f32[2,9,48,128]{3,2,1,0:T(8,128)}, f32[48,128]{1,0:T(8,128)}) custom-call(f32[2,9,48,128]{3,2,1,0:T(8,128)} %get-tuple-element.34.row0, f32[2,9,48,128]{3,2,1,0:T(8,128)} %get-tuple-element.35.row1, f32[2,9,48,128]{3,2,1,0:T(8,128)} %collective-permute-done.6.up, ...), custom_call_target="tpu_custom_call" | custom-call | flops 5308416 | bytes 2654208 | tf_op jit(solution)/shard_map/atm_step/pallas_call | solution.py:181
  166.0 5.9 %collective-permute-start.10 = (f32[2,9,48,128]{3,2,1,0:T(8,128)}, f32[2,9,48,128]{3,2,1,0:T(8,128)S(1)}, u32[]{:S(2)}, u32[]{:S(2)}) collective-permute-start(f32[2,9,48,128]{3,2,1,0:T(8,128)} %get-tuple-element.37.row0), channel_id=1, source_target_pairs={{2,0},{4,2},{6,4},{8,6},{10,8},{12,10},{14,12},{16,14},{18,16},{20... | collective-permute-start | bytes 1327112 | tf_op jit(solution)/shard_map/ppermute | solution.py:243
  174.5 15.1 %forcing_scatter.1 = f32[2,28,256]{2,1,0:T(8,128)} custom-call(f32[128,8,128]{2,1,0:T(8,128)} %all-to-all-done.1.val_ref, s32[128,512]{1,0:T(8,128)} %bitcast.75), custom_call_target="tpu_custom_call" | custom-call | flops 8589934592 | bytes 1048576 | tf_op jit(solution)/shard_map/forcing_scatter/pallas_call | solution.py:219
  191.7 7.2 %collective-permute-start.18 = (f32[2,1,1792]{2,1,0:T(1,128)S(1)}, f32[2,1,1792]{2,1,0:T(1,128)S(1)}, u32[]{:S(2)}, u32[]{:S(2)}) collective-permute-start(f32[2,1,1792]{2,1,0:T(1,128)S(1)} %get-tuple-element.66), channel_id=1, source_target_pairs={{2,0},{4,2},{6,4},{8,6},{10,8},{12,10},{14,12},{16,14},{18,16},{20... | collective-permute-start | bytes 43016 | tf_op jit(solution)/shard_map/ppermute | solution.py:243
  199.8 7.3 %collective-permute-done.19 = f32[2,1,1792]{2,1,0:T(1,128)S(1)} collective-permute-done((f32[2,1,1792]{2,1,0:T(1,128)S(1)}, f32[2,1,1792]{2,1,0:T(1,128)S(1)}, u32[]{:S(2)}, u32[]{:S(2)}) %collective-permute-start.19) | collective-permute-done | bytes 14368 | tf_op jit(solution)/shard_map/ppermute | solution.py:243
  210.6 3.1 %atm_step.7 = (f32[2,9,48,128]{3,2,1,0:T(8,128)}, f32[2,9,48,128]{3,2,1,0:T(8,128)}, f32[48,128]{1,0:T(8,128)}) custom-call(f32[2,9,48,128]{3,2,1,0:T(8,128)} %get-tuple-element.37.row0, f32[2,9,48,128]{3,2,1,0:T(8,128)} %get-tuple-element.38.row1, f32[2,9,48,128]{3,2,1,0:T(8,128)} %copy-done.7, f32[2,9,48,128]{3,2,1,0:T(8,128)} %copy-done.6, ...), custom_call_target="tpu_custom_call" | custom-call | flops 5308416 | bytes 2654208 | tf_op jit(solution)/shard_map/atm_step/pallas_call | solution.py:181
  (139 shorter events, 37.5 us)
Async XLA Ops:
  11.9 47.2 %all-to-all-start = ((f32[128,4,128]{2,1,0:T(4,128)}), f32[128,4,128]{2,1,0:T(4,128)}, u32[]{:S(2)}, u32[]{:S(2)}) async-start(f32[128,4,128]{2,1,0:T(4,128)} %temp_gather.1), calls=%async_computation | async-start | bytes 524288 | tf_op jit(solution)/shard_map/all_to_all | solution.py:284
  30.2 58.3 %collective-permute-start = (f32[2,9,48,128]{3,2,1,0:T(8,128)S(1)}, f32[2,9,48,128]{3,2,1,0:T(8,128)}, u32[]{:S(2)}, u32[]{:S(2)}) collective-permute-start(f32[2,9,48,128]{3,2,1,0:T(8,128)S(1)} %get-tuple-element.64.row1), channel_id=1, source_target_pairs={{0,2},{2,4},{4,6},{6,8},{8,10},{10,12},{12,14},{14,16},{16,18},{18... | collective-permute-start | bytes 1327112 | tf_op jit(solution)/shard_map/ppermute | solution.py:243
  30.8 57.7 %collective-permute-start.1 = (f32[2,9,48,128]{3,2,1,0:T(8,128)S(1)}, f32[2,9,48,128]{3,2,1,0:T(8,128)}, u32[]{:S(2)}, u32[]{:S(2)}) collective-permute-start(f32[2,9,48,128]{3,2,1,0:T(8,128)S(1)} %get-tuple-element.65.row0), channel_id=1, source_target_pairs={{2,0},{4,2},{6,4},{8,6},{10,8},{12,10},{14,12},{16,14},{18,16},{20... | collective-permute-start | bytes 1327112 | tf_op jit(solution)/shard_map/ppermute | solution.py:243
  37.6 50.8 %collective-permute-start.2 = (f32[48,128]{1,0:T(8,128)S(1)}, f32[48,128]{1,0:T(8,128)S(1)}, u32[]{:S(2)}, u32[]{:S(2)}) collective-permute-start(f32[48,128]{1,0:T(8,128)S(1)} %pad.21), channel_id=1, source_target_pairs={{0,1},{1,0},{2,3},{3,2},{4,5},{5,4},{6,7},{7,6},{8,9},{9,8},{10,11... | collective-permute-start | bytes 73736 | tf_op jit(solution)/shard_map/ppermute | solution.py:248
  57.8 41.4 %copy-start = (f32[2,24,4,14,128]{4,1,3,0,2:T(8,128)}, f32[2,24,4,14,128]{4,1,3,0,2:T(8,128)S(1)}, u32[]{:S(2)}) copy-start(f32[2,24,4,14,128]{4,1,3,0,2:T(8,128)S(1)} %copy.61) | copy-start | bytes 4128772
  78.7 95.8 %all-to-all-start.1 = ((f32[128,8,128]{2,1,0:T(8,128)}), f32[128,8,128]{2,1,0:T(8,128)}, u32[]{:S(2)}, u32[]{:S(2)}) async-start(f32[128,8,128]{2,1,0:T(8,128)} %flux_gather.1), calls=%async_computation.1 | async-start | bytes 1048576 | tf_op jit(solution)/shard_map/all_to_all | solution.py:304
  92.3 34.8 %collective-permute-start.3 = (f32[2,9,48,128]{3,2,1,0:T(8,128)}, f32[2,9,48,128]{3,2,1,0:T(8,128)S(1)}, u32[]{:S(2)}, u32[]{:S(2)}) collective-permute-start(f32[2,9,48,128]{3,2,1,0:T(8,128)} %get-tuple-element.32.row1), channel_id=1, source_target_pairs={{0,2},{2,4},{4,6},{6,8},{8,10},{10,12},{12,14},{14,16},{16,18},{18... | collective-permute-start | bytes 1327112 | tf_op jit(solution)/shard_map/ppermute | solution.py:243
  92.8 34.3 %collective-permute-start.4 = (f32[2,9,48,128]{3,2,1,0:T(8,128)}, f32[2,9,48,128]{3,2,1,0:T(8,128)S(1)}, u32[]{:S(2)}, u32[]{:S(2)}) collective-permute-start(f32[2,9,48,128]{3,2,1,0:T(8,128)} %get-tuple-element.31.row0), channel_id=1, source_target_pairs={{2,0},{4,2},{6,4},{8,6},{10,8},{12,10},{14,12},{16,14},{18,16},{20... | collective-permute-start | bytes 1327112 | tf_op jit(solution)/shard_map/ppermute | solution.py:243
  99.2 23.3 %collective-permute-start.12 = (f32[2,14,24,128]{3,2,1,0:T(8,128)S(1)}, f32[2,14,24,128]{3,2,1,0:T(8,128)S(1)}, u32[]{:S(2)}, u32[]{:S(2)}) collective-permute-start(f32[2,14,24,128]{3,2,1,0:T(8,128)S(1)} %get-tuple-element.61), channel_id=1, source_target_pairs={{0,2},{2,4},{4,6},{6,8},{8,10},{10,12},{12,14},{14,16},{16,18},{18... | collective-permute-start | bytes 1032200 | tf_op jit(solution)/shard_map/ppermute | solution.py:243
  99.3 23.2 %collective-permute-start.13 = (f32[2,14,24,128]{3,2,1,0:T(8,128)S(1)}, f32[2,14,24,128]{3,2,1,0:T(8,128)S(1)}, u32[]{:S(2)}, u32[]{:S(2)}) collective-permute-start(f32[2,14,24,128]{3,2,1,0:T(8,128)S(1)} %get-tuple-element.60), channel_id=1, source_target_pairs={{2,0},{4,2},{6,4},{8,6},{10,8},{12,10},{14,12},{16,14},{18,16},{20... | collective-permute-start | bytes 1032200 | tf_op jit(solution)/shard_map/ppermute | solution.py:243
  107.0 2.3 %collective-permute-start.14 = (f32[24,128]{1,0:T(8,128)S(1)}, f32[24,128]{1,0:T(8,128)S(1)}, u32[]{:S(2)}, u32[]{:S(2)}) collective-permute-start(f32[24,128]{1,0:T(8,128)S(1)} %pad.25), channel_id=1, source_target_pairs={{0,1},{1,0},{2,3},{3,2},{4,5},{5,4},{6,7},{7,6},{8,9},{9,8},{10,11... | collective-permute-start | bytes 36872 | tf_op jit(solution)/shard_map/ppermute | solution.py:248
  109.4 17.7 %collective-permute-start.5 = (f32[48,128]{1,0:T(8,128)S(1)}, f32[48,128]{1,0:T(8,128)S(1)}, u32[]{:S(2)}, u32[]{:S(2)}) collective-permute-start(f32[48,128]{1,0:T(8,128)S(1)} %copy-done.23), channel_id=1, source_target_pairs={{0,1},{1,0},{2,3},{3,2},{4,5},{5,4},{6,7},{7,6},{8,9},{9,8},{10,11... | collective-permute-start | bytes 73736 | tf_op jit(solution)/shard_map/ppermute | solution.py:248
  131.7 30.6 %collective-permute-start.6 = (f32[2,9,48,128]{3,2,1,0:T(8,128)}, f32[2,9,48,128]{3,2,1,0:T(8,128)}, u32[]{:S(2)}, u32[]{:S(2)}) collective-permute-start(f32[2,9,48,128]{3,2,1,0:T(8,128)} %get-tuple-element.35.row1), channel_id=1, source_target_pairs={{0,2},{2,4},{4,6},{6,8},{8,10},{10,12},{12,14},{14,16},{16,18},{18... | collective-permute-start | bytes 1327112 | tf_op jit(solution)/shard_map/ppermute | solution.py:243
  131.7 30.6 %collective-permute-start.7 = (f32[2,9,48,128]{3,2,1,0:T(8,128)}, f32[2,9,48,128]{3,2,1,0:T(8,128)}, u32[]{:S(2)}, u32[]{:S(2)}) collective-permute-start(f32[2,9,48,128]{3,2,1,0:T(8,128)} %get-tuple-element.34.row0), channel_id=1, source_target_pairs={{2,0},{4,2},{6,4},{8,6},{10,8},{12,10},{14,12},{16,14},{18,16},{20... | collective-permute-start | bytes 1327112 | tf_op jit(solution)/shard_map/ppermute | solution.py:243
  138.7 16.6 %collective-permute-start.15 = (f32[2,14,24,128]{3,2,1,0:T(8,128)S(1)}, f32[2,14,24,128]{3,2,1,0:T(8,128)S(1)}, u32[]{:S(2)}, u32[]{:S(2)}) collective-permute-start(f32[2,14,24,128]{3,2,1,0:T(8,128)S(1)} %get-tuple-element.59), channel_id=1, source_target_pairs={{0,2},{2,4},{4,6},{6,8},{8,10},{10,12},{12,14},{14,16},{16,18},{18... | collective-permute-start | bytes 1032200 | tf_op jit(solution)/shard_map/ppermute | solution.py:243
  138.8 16.5 %collective-permute-start.16 = (f32[2,14,24,128]{3,2,1,0:T(8,128)S(1)}, f32[2,14,24,128]{3,2,1,0:T(8,128)S(1)}, u32[]{:S(2)}, u32[]{:S(2)}) collective-permute-start(f32[2,14,24,128]{3,2,1,0:T(8,128)S(1)} %get-tuple-element.58), channel_id=1, source_target_pairs={{2,0},{4,2},{6,4},{8,6},{10,8},{12,10},{14,12},{16,14},{18,16},{20... | collective-permute-start | bytes 1032200 | tf_op jit(solution)/shard_map/ppermute | solution.py:243
  145.7 3.1 %collective-permute-start.17 = (f32[24,128]{1,0:T(8,128)S(1)}, f32[24,128]{1,0:T(8,128)S(1)}, u32[]{:S(2)}, u32[]{:S(2)}) collective-permute-start(f32[24,128]{1,0:T(8,128)S(1)} %copy-done.25), channel_id=1, source_target_pairs={{0,1},{1,0},{2,3},{3,2},{4,5},{5,4},{6,7},{7,6},{8,9},{9,8},{10,11... | collective-permute-start | bytes 36872 | tf_op jit(solution)/shard_map/ppermute | solution.py:248
  148.8 13.5 %collective-permute-start.8 = (f32[48,128]{1,0:T(8,128)S(1)}, f32[48,128]{1,0:T(8,128)S(1)}, u32[]{:S(2)}, u32[]{:S(2)}) collective-permute-start(f32[48,128]{1,0:T(8,128)S(1)} %copy-done.24), channel_id=1, source_target_pairs={{0,1},{1,0},{2,3},{3,2},{4,5},{5,4},{6,7},{7,6},{8,9},{9,8},{10,11... | collective-permute-start | bytes 73736 | tf_op jit(solution)/shard_map/ppermute | solution.py:248
  166.0 43.0 %collective-permute-start.10 = (f32[2,9,48,128]{3,2,1,0:T(8,128)}, f32[2,9,48,128]{3,2,1,0:T(8,128)S(1)}, u32[]{:S(2)}, u32[]{:S(2)}) collective-permute-start(f32[2,9,48,128]{3,2,1,0:T(8,128)} %get-tuple-element.37.row0), channel_id=1, source_target_pairs={{2,0},{4,2},{6,4},{8,6},{10,8},{12,10},{14,12},{16,14},{18,16},{20... | collective-permute-start | bytes 1327112 | tf_op jit(solution)/shard_map/ppermute | solution.py:243
  171.9 37.1 %collective-permute-start.9 = (f32[2,9,48,128]{3,2,1,0:T(8,128)}, f32[2,9,48,128]{3,2,1,0:T(8,128)S(1)}, u32[]{:S(2)}, u32[]{:S(2)}) collective-permute-start(f32[2,9,48,128]{3,2,1,0:T(8,128)} %get-tuple-element.38.row1), channel_id=1, source_target_pairs={{0,2},{2,4},{4,6},{6,8},{8,10},{10,12},{12,14},{14,16},{16,18},{18... | collective-permute-start | bytes 1327112 | tf_op jit(solution)/shard_map/ppermute | solution.py:243
  171.9 37.1 %collective-permute-start.11 = (f32[48,128]{1,0:T(8,128)}, f32[48,128]{1,0:T(8,128)S(1)}, u32[]{:S(2)}, u32[]{:S(2)}) collective-permute-start(f32[48,128]{1,0:T(8,128)} %get-tuple-element.39), channel_id=1, source_target_pairs={{0,1},{1,0},{2,3},{3,2},{4,5},{5,4},{6,7},{7,6},{8,9},{9,8},{10,11... | collective-permute-start | bytes 73736 | tf_op jit(solution)/shard_map/ppermute | solution.py:248
  191.6 7.4 %collective-permute-start.20 = (f32[2,2,4]{2,1,0:T(2,128)S(1)}, f32[2,2,4]{2,1,0:T(2,128)S(1)}, u32[]{:S(2)}, u32[]{:S(2)}) collective-permute-start(f32[2,2,4]{2,1,0:T(2,128)S(1)} %pad_maximum_fusion.4), channel_id=1, source_target_pairs={{0,1},{1,0},{2,3},{3,2},{4,5},{5,4},{6,7},{7,6},{8,9},{9,8},{10,11... | collective-permute-start | bytes 200 | tf_op jit(solution)/shard_map/ppermute | solution.py:248
  191.7 8.1 %collective-permute-start.18 = (f32[2,1,1792]{2,1,0:T(1,128)S(1)}, f32[2,1,1792]{2,1,0:T(1,128)S(1)}, u32[]{:S(2)}, u32[]{:S(2)}) collective-permute-start(f32[2,1,1792]{2,1,0:T(1,128)S(1)} %get-tuple-element.66), channel_id=1, source_target_pairs={{2,0},{4,2},{6,4},{8,6},{10,8},{12,10},{14,12},{16,14},{18,16},{20... | collective-permute-start | bytes 43016 | tf_op jit(solution)/shard_map/ppermute | solution.py:243
  199.0 8.1 %collective-permute-start.19 = (f32[2,1,1792]{2,1,0:T(1,128)S(1)}, f32[2,1,1792]{2,1,0:T(1,128)S(1)}, u32[]{:S(2)}, u32[]{:S(2)}) collective-permute-start(f32[2,1,1792]{2,1,0:T(1,128)S(1)} %get-tuple-element.67), channel_id=1, source_target_pairs={{0,2},{2,4},{4,6},{6,8},{8,10},{10,12},{12,14},{14,16},{16,18},{18... | collective-permute-start | bytes 43016 | tf_op jit(solution)/shard_map/ppermute | solution.py:243
  (26 other events, 223.1 us)

commit v2 on v1

v2 whole, which is shorter than its diff:
```python
import jax
import jax.numpy as jnp
from jax import lax
from jax.experimental import pallas as pl
from jax.experimental.pallas import tpu as pltpu
from jax.sharding import PartitionSpec as P

ASTEPS = 4
OSTEPS = 2
VERT_MIX = 0.1
OCEAN_MIX = 0.15
HEAT_GAIN = 2.0
SALT_GAIN = 1.0
MOIST_RATIO = 0.8
LANES = 128
GROUP = ("comp", "tile")
F32, BF16 = jnp.float32, jnp.bfloat16


SPLITS = 3


def parts_of(v):
    out = []
    for _ in range(SPLITS):
        p = v.astype(BF16)
        out.append(p)
        v = v - p.astype(F32)
    return out


def spread(row):
    return jnp.broadcast_to(row.astype(F32), (16, row.shape[1])).astype(BF16)


def hits(row, size):
    b = spread(row)
    base = lax.broadcasted_iota(jnp.int32, b.shape, 0).astype(F32)
    return [b == (base + 16.0 * j).astype(BF16) for j in range(size // 16)]


def one_hot(row, size):
    masks = hits(row, size)
    one, zero = jnp.ones(masks[0].shape, BF16), jnp.zeros(masks[0].shape, BF16)
    return jnp.concatenate([jnp.where(m, one, zero) for m in masks], axis=0)


def gather_loop(t_ref, index_ref, w_ref, out_ref, split, H, L, F):
    def group(g, c):
        base = pl.multiple_of(g * 8, 8)
        hi, lo = split(index_ref[pl.ds(base, 8), :])
        w = w_ref[pl.ds(base, 8), :]
        for r in range(8):
            hot = jnp.concatenate([one_hot(hi[r : r + 1], H)] * SPLITS, axis=0)
            o = jnp.dot(t_ref[...], hot, preferred_element_type=F32)
            rows = lax.broadcasted_iota(jnp.int32, (L, o.shape[1]), 0)
            mine = rows == lo[r : r + 1]
            for f in range(F):
                picked = jnp.where(mine, o[f * L : (f + 1) * L], 0.0)
                value = jnp.sum(picked, axis=0, keepdims=True) * w[r : r + 1]
                for q in range(4):
                    out_ref[base + r, 4 * f + q : 4 * f + q + 1, :] = value[:, q * 128 : (q + 1) * 128]
        return c
    lax.fori_loop(0, index_ref.shape[0] // 8, group, 0)


def scatter_loop(val_ref, index_ref, H, L, F, place_of=lambda h: h):
    shift = L.bit_length() - 1
    def group(g, acc):
        base = pl.multiple_of(g * 8, 8)
        index = index_ref[pl.ds(base, 8), :]
        hi, lo = place_of(index >> shift), index & (L - 1)
        for r in range(8):
            masks = hits(hi[r : r + 1], H)
            a = []
            for f in range(F):
                v = jnp.concatenate([val_ref[base + r, 4 * f + q : 4 * f + q + 1, :] for q in range(4)], axis=1)
                for p in parts_of(jnp.broadcast_to(v, (16, v.shape[1]))):
                    a += [jnp.where(m, p, jnp.zeros_like(p)) for m in masks]
            a = jnp.concatenate(a, axis=0)
            acc = acc + lax.dot_general(a, one_hot(lo[r : r + 1], L), (((1,), (1,)), ((), ())), preferred_element_type=F32)
        return acc
    acc = lax.fori_loop(0, index_ref.shape[0] // 8, group, jnp.zeros((F * SPLITS * H, L), F32))
    return [sum(acc[(f * SPLITS + i) * H : (f * SPLITS + i + 1) * H] for i in range(SPLITS)) for f in range(F)]


def temp_kernel(table_ref, cell_ref, w_ref, out_ref, t_ref):
    t_ref[...] = jnp.concatenate(parts_of(table_ref[...].T), axis=1)
    gather_loop(t_ref, cell_ref, w_ref, out_ref, lambda i: (i >> 7, i & 127), 64, 128, 1)


AT, AL, AR = 9, 48, 2
OT, OL, OR = 14, 24, 4
ASIZE, OSIZE = 2 * AT * AL, 2 * OT * OL


def flux_kernel(val_ref, col_ref, state_ref, coef_ref, temp_ref, t_ref, flux_ref):
    temp, = scatter_loop(val_ref, col_ref, 32, 128, 1)
    temp = temp[: AR * AT]
    temp_ref[...] = temp
    flux_ref[...] = jnp.zeros_like(flux_ref)
    tables = []
    for f in range(2):
        flux_ref[: AR * AT, :] = coef_ref[f] * (state_ref[f] - (1.0, MOIST_RATIO)[f] * temp)
        flux = flux_ref[...]
        halves = jnp.concatenate([flux[:, :64], flux[:, 64:]], axis=0)
        tables.append(jnp.concatenate(parts_of(halves.T), axis=1))
    t_ref[...] = jnp.concatenate(tables, axis=0)


def half_split(i):
    return (i >> 7) + 24 * ((i >> 6) & 1), i & 63


def send_kernel(t_ref, col_ref, w_ref, out_ref):
    gather_loop(t_ref, col_ref, w_ref, out_ref, half_split, 48, 64, 2)


def shifted_levels(ref, base, levels, tile):
    side = lax.broadcasted_iota(jnp.int32, (8, LANES), 0)
    first, last = tile[:8], tile[-8:]
    above = jnp.concatenate([ref[base + 1 : base + levels - 7, :], jnp.where(side == 7, last, pltpu.roll(last, 7, 0))], axis=0)
    below = jnp.concatenate([jnp.where(side == 0, first, pltpu.roll(first, 1, 0)), ref[base + 7 : base + levels - 1, :]], axis=0)
    return above, below


def step_row(own, up, down, tiles, levels, left, right, own_gain, side_gain, vertical, finish):
    lane = lax.broadcasted_iota(jnp.int32, (levels, LANES), 1)
    load = lambda place, j: place[0][place[1] + j * levels : place[1] + (j + 1) * levels, :]
    ends = []
    tile = load(own, 0)
    low_side = left
    for j in range(tiles):
        if j < tiles - 1:
            ahead = load(own, j + 1)
            high_side = pltpu.roll(ahead, LANES - 1, 1)
        else:
            ahead, high_side = None, right
        to_right = pltpu.roll(tile, 1, 1)
        before = jnp.where(lane == 0, low_side, to_right)
        after = jnp.where(lane == LANES - 1, high_side, pltpu.roll(tile, LANES - 1, 1))
        above, below = shifted_levels(own[0], own[1] + j * levels, levels, tile)
        around = (load(up, j) + load(down, j)) + (before + after)
        fresh = own_gain * tile + side_gain * around + vertical * (above + below)
        fresh = finish(j, fresh, tile)
        if j in (0, tiles - 1):
            ends.append(fresh)
        tile, low_side = ahead, to_right
    return ends


def edges_of(rows):
    lane = lax.broadcasted_iota(jnp.int32, rows[0][0].shape, 1)
    out = jnp.zeros(rows[0][0].shape, F32)
    for i, (first, last) in enumerate(rows):
        out = jnp.where(lane == 2 * i, pltpu.roll(first, 2 * i, 1) if i else first, out)
        out = jnp.where(lane == 2 * i + 1, pltpu.roll(last, 2 * i + 2, 1), out)
    return out


def edge(edges, i):
    return jnp.broadcast_to(edges[:, i : i + 1], edges.shape)


def prep_kernel(atm_ref, ocn_ref, mask_ref, inner_ref, coef_ref, adiff_ref, odiff_ref, low, high, edges, ocean, frac, table, surface, coef, adiff, odiff):
    adiff[...] = jnp.broadcast_to(adiff_ref[...], (LANES, AL)).T
    odiff[...] = jnp.broadcast_to(odiff_ref[...], (LANES, OL)).T
    ends = []
    for r, out in enumerate((low, high)):
        for f in range(2):
            pair = []
            for j in range(AT):
                tile = atm_ref[f, :, r, j * LANES : (j + 1) * LANES]
                out[(f * AT + j) * AL : (f * AT + j + 1) * AL, :] = tile
                at = r * AT + j
                surface[f, at : at + 1, :] = tile[:1]
                coef[f, at : at + 1, :] = coef_ref[f, r : r + 1, j * LANES : (j + 1) * LANES]
                if j in (0, AT - 1):
                    pair.append(tile)
            ends.append(pair)
    edges[:AL, :] = edges_of(ends)
    table[...] = jnp.zeros_like(table)
    ends = []
    for r in range(OR):
        for j in range(OT):
            at = r * OT + j
            frac[at : at + 1, :] = mask_ref[r : r + 1, j * LANES : (j + 1) * LANES].astype(F32) * inner_ref[r : r + 1, :]
        for f in range(2):
            pair = []
            for j in range(OT):
                at = r * OT + j
                tile = ocn_ref[f, :, r, j * LANES : (j + 1) * LANES] * frac[at : at + 1, :]
                line = ((r * 2 + f) * OT + j) * OL
                ocean[line : line + OL, :] = tile
                if r in (0, OR - 1):
                    line = ASIZE + (f * OT + j) * OL
                    (high if r else low)[line : line + OL, :] = tile
                if f == 0:
                    table[at : at + 1, :] = tile[:1]
                if j in (0, OT - 1):
                    pair.append(tile)
            ends.append(pair)
    edges[AL:, :] = edges_of(ends)


def atm_kernel(share, low, high, up, down, edges_ref, diff_ref, coef_ref, temp_ref, *rest):
    if share:
        ocean, ocn_edges, out_low, out_high, out_edges = rest
    else:
        out_low, out_high, out_edges = rest
    edges, side_gain = edges_ref[:AL, :], diff_ref[...]
    own_gain = (1.0 - 2.0 * VERT_MIX) - 4.0 * side_gain
    top = lax.broadcasted_iota(jnp.int32, (8, LANES), 0) == 0
    rows = [up, low, high, down]
    ends = []
    for r, out in enumerate((out_low, out_high)):
        for f in range(2):
            def finish(j, fresh, old, f=f, r=r, out=out):
                at = r * AT + j
                gain = (1.0, MOIST_RATIO)[f] * temp_ref[at : at + 1, :]
                gain = coef_ref[f, at : at + 1, :] * (gain - old[:1])
                fresh = jnp.concatenate([fresh[:8] + jnp.where(top, gain, 0.0), fresh[8:]], axis=0)
                out[(f * AT + j) * AL : (f * AT + j + 1) * AL, :] = fresh
                return fresh
            i, base = 2 * r + f, f * AT * AL
            ends.append(step_row(*((rows[k], base) for k in (r + 1, r, r + 2)), AT, AL, edge(edges, 2 * i + 1), edge(edges, 2 * i), own_gain, side_gain, VERT_MIX, finish))
    out_edges[:AL, :] = edges_of(ends)
    if share:
        out_low[ASIZE:, :] = ocean[:OSIZE, :]
        out_high[ASIZE:, :] = ocean[(OR - 1) * OSIZE :, :]
        out_edges[AL:, :] = ocn_edges[...]


def ocn_kernel(own, up, down, edges_ref, diff_ref, frac_ref, out, *out_edges):
    edges, side_gain = edges_ref[AL:, :], diff_ref[...]
    own_gain = (1.0 - 2.0 * OCEAN_MIX) - 4.0 * side_gain
    ends = []
    for r in range(OR):
        for f in range(2):
            def finish(j, fresh, old, f=f, r=r):
                fresh = fresh * frac_ref[r * OT + j : r * OT + j + 1, :]
                line = ((r * 2 + f) * OT + j) * OL
                out[line : line + OL, :] = fresh
                return fresh
            i = 2 * r + f
            part = lambda k: (own, (k * 2 + f) * OT * OL)
            above = part(r - 1) if r else (up, ASIZE + f * OT * OL)
            below = part(r + 1) if r < OR - 1 else (down, ASIZE + f * OT * OL)
            ends.append(step_row(part(r), above, below, OT, OL, edge(edges, 2 * i + 1), edge(edges, 2 * i), own_gain, side_gain, OCEAN_MIX, finish))
    if out_edges:
        out_edges[0][...] = edges_of(ends)


def forcing_kernel(val_ref, cell_ref, frac_ref, out_ref, gain_ref, low, high):
    for f, total in enumerate(scatter_loop(val_ref, cell_ref, 32, 256, 2)):
        total = (HEAT_GAIN, -SALT_GAIN)[f] * total[: OR * OT // 2]
        for side in range(2):
            out_ref[f, pl.ds(side, OR * OT // 2, stride=2), :] = total[:, side * LANES : (side + 1) * LANES]
        gain_ref[f] = out_ref[f] * frac_ref[...]
        low[f] = gain_ref[f, :OT, :]
        high[f] = gain_ref[f, (OR - 1) * OT :, :]


def last_kernel(base_ref, top_ref, forcing_ref, gain_ref, up, down, beside, frac_ref, diff_ref, out_ref, tall, low_side, high_side, result, sem):
    count = OR * OT
    lane = lax.broadcasted_iota(jnp.int32, (count, LANES), 1)
    line = lax.broadcasted_iota(jnp.int32, (count, LANES), 0)
    starts = (line == 0) | (line == OT) | (line == 2 * OT) | (line == 3 * OT)
    stops = (line == OT - 1) | (line == 2 * OT - 1) | (line == 3 * OT - 1) | (line == 4 * OT - 1)
    frac = frac_ref[...]
    low_side[...] = jnp.zeros_like(low_side)
    high_side[...] = jnp.zeros_like(high_side)
    for f in range(2):
        forcing, gained = forcing_ref[f], gain_ref[f]
        tall[OT : 5 * OT, :] = gained
        tall[:OT, :] = up[f]
        tall[5 * OT :, :] = down[f]
        partner = beside[f]
        to_right, to_left = pltpu.roll(partner, 1, 1), pltpu.roll(partner, LANES - 1, 1)
        for r in range(OR):
            first, last = r * OT, (r + 1) * OT - 1
            low_side[first : first + 1, :] = to_right[last : last + 1]
            high_side[last : last + 1, :] = to_left[first : first + 1]
        to_right, to_left = pltpu.roll(gained, 1, 1), pltpu.roll(gained, LANES - 1, 1)
        before = jnp.where(lane == 0, jnp.where(starts, low_side[...], pltpu.roll(to_right, 1, 0)), to_right)
        after = jnp.where(lane == LANES - 1, jnp.where(stops, high_side[...], pltpu.roll(to_left, count - 1, 0)), to_left)
        lateral = tall[: 4 * OT, :] + tall[2 * OT :, :] + before + after - 4.0 * gained
        second = (gained + diff_ref[:1, :] * lateral - OCEAN_MIX * gained + forcing) * frac
        third = OCEAN_MIX * gained * frac
        for r in range(OR):
            for j in range(OT):
                at, cols = r * OT + j, pl.ds(j * LANES, LANES)
                result[f, 0, r : r + 1, cols] = top_ref[f, 0, r : r + 1, cols] + second[at : at + 1]
                result[f, 1, r : r + 1, cols] = top_ref[f, 1, r : r + 1, cols] + third[at : at + 1]
    copy = pltpu.make_async_copy(result, out_ref.at[:, pl.ds(0, 2)], sem)
    copy.start()
    copy.wait()


VM = pl.BlockSpec(memory_space=pltpu.VMEM)
ANY = pl.BlockSpec(memory_space=pl.ANY)


def call(kernel, name, micros, out_shape, *args, scratch=(), **more):
    specs = {"in_specs": [VM] * len(args), "out_specs": jax.tree.map(lambda _: VM, out_shape), **more}
    return pl.pallas_call(
        kernel,
        out_shape=out_shape,
        scratch_shapes=list(scratch),
        cost_estimate=pl.CostEstimate(flops=int(micros * 1.1e9), bytes_accessed=int(micros * 3e6), transcendentals=0),
        name=name,
        **specs,
    )(*args)


def from_rows(tiles):
    rows, fields, count, levels, lanes = tiles.shape
    return tiles.transpose(1, 3, 0, 2, 4).reshape(fields, levels, rows, count * lanes)


def row_halos(first, last):
    count = lax.axis_size(GROUP)
    up = [(i, (i + 1) % count) for i in range(count)]
    return lax.ppermute(last, GROUP, up), lax.ppermute(first, GROUP, [(b, a) for a, b in up])


def partner(edges):
    count = lax.axis_size("lev")
    return lax.ppermute(edges, "lev", [(i, (i + 1) % count) for i in range(count)])


def exchange(values):
    return lax.all_to_all(values, GROUP, split_axis=0, concat_axis=0, tiled=True)


def shards(
    atm_state,
    atm_diffusion,
    atm_surface_coef,
    ocn_state,
    ocn_diffusion,
    sea_mask,
    atm_pair_cols,
    a2o_weights,
    ocn_pair_cells,
    o2a_weights,
):
    group_size = lax.axis_size(GROUP)
    shape = lambda *s: jax.ShapeDtypeStruct(s, F32)
    row_ids = lax.axis_index(GROUP) * OR + lax.broadcasted_iota(jnp.int32, (OR, LANES), 0)
    inner = ((row_ids > 0) & (row_ids < OR * group_size - 1)).astype(F32)
    cols, cells = atm_pair_cols[0, 0], ocn_pair_cells[0, 0]
    both = shape(ASIZE + OSIZE, LANES)

    low, high, edges, ocean, frac, table, surface, coef, atm_diff, ocn_diff = call(
        prep_kernel,
        "prep",
        3,
        (both, both, shape(AL + OL, LANES), shape(OR * OSIZE, LANES), shape(OR * OT, LANES), shape(64, LANES), shape(2, AR * AT, LANES), shape(2, AR * AT, LANES), shape(AL, LANES), shape(OL, LANES)),
        atm_state,
        ocn_state,
        sea_mask,
        inner,
        atm_surface_coef,
        atm_diffusion[None],
        ocn_diffusion[None],
    )
    up, down = row_halos(low, high)
    beside = partner(edges)

    outgoing = call(temp_kernel, "temp_gather", 9, shape(group_size, 4, LANES), table, cells, o2a_weights[0, 0], scratch=[pltpu.VMEM((128, SPLITS * 64), BF16)])
    incoming = exchange(outgoing)
    ocean, ocn_edges = call(ocn_kernel, "ocn_step", 3, (shape(OR * OSIZE, LANES), shape(OL, LANES)), ocean, up, down, beside, ocn_diff, frac)
    incoming, ocean, ocn_edges = lax.optimization_barrier((incoming, ocean, ocn_edges))

    temp, flux_table = call(flux_kernel, "temp_scatter", 9, (shape(AR * AT, LANES), jax.ShapeDtypeStruct((128, SPLITS * 48), BF16)), incoming, cols, surface, coef, scratch=[pltpu.VMEM((24, LANES), F32)])

    def atm_step(share, low, high, up, down, beside, *more):
        rows = shape(ASIZE + OSIZE * share, LANES)
        outs = (rows, rows, shape(AL + OL * share, LANES))
        return call(lambda *refs: atm_kernel(share, *refs), "atm_step", 2.5, outs, low, high, up, down, beside, atm_diff, coef, temp, *more)

    low, high, edges = atm_step(True, low, high, up, down, beside, ocean, ocn_edges)
    up, down = row_halos(low, high)
    beside = partner(edges)
    flux_table, low, high = lax.optimization_barrier((flux_table, low, high))

    outgoing = call(send_kernel, "flux_gather", 9, shape(group_size, 8, LANES), flux_table, cols, a2o_weights[0, 0])
    outgoing, up, down, beside = lax.optimization_barrier((outgoing, up, down, beside))
    ocean = call(ocn_kernel, "ocn_step", 3, shape(OR * OSIZE, LANES), ocean, up, down, beside, ocn_diff, frac)
    ocean = from_rows(ocean.reshape(OR, 2, OT, OL, LANES))
    low, high, edges = atm_step(False, low, high, up, down, beside)
    outgoing, ocean, low, high, edges = lax.optimization_barrier((outgoing, ocean, low, high, edges))
    up, down = row_halos(low, high)
    beside = partner(edges)
    incoming = exchange(outgoing)
    low, high, edges = atm_step(False, low, high, up, down, beside)
    up, down = row_halos(low, high)
    beside = partner(edges)
    incoming, low, high = lax.optimization_barrier((incoming, low, high))

    every = shape(2, OR * OT, LANES)
    forcing, gained, first, last = call(forcing_kernel, "forcing_scatter", 15, (every, every, shape(2, OT, LANES), shape(2, OT, LANES)), incoming, cells, frac)
    forcing, gained, first, last, up, down, beside = lax.optimization_barrier((forcing, gained, first, last, up, down, beside))
    above, below = row_halos(first, last)
    side = partner(gained)

    low, high, _ = atm_step(False, low, high, up, down, beside)
    atm_next = from_rows(jnp.stack([low, high]).reshape(AR, 2, AT, AL, LANES))

    line = pltpu.VMEM((OR * OT, LANES), F32)
    ocean_next = call(
        last_kernel,
        "ocn_last",
        1,
        jax.ShapeDtypeStruct(ocean.shape, F32),
        ocean,
        ocean[:, :2],
        forcing,
        gained,
        above,
        below,
        side,
        frac,
        ocn_diff,
        in_specs=[ANY] + [VM] * 8,
        out_specs=ANY,
        scratch=[pltpu.VMEM((6 * OT, LANES), F32), line, line, pltpu.VMEM((2, 2, OR, OT * LANES), F32), pltpu.SemaphoreType.DMA],
        input_output_aliases={0: 0},
    )
    return atm_next, ocean_next


def solution(mesh):
    across = P(None, None, GROUP, "lev")
    pairs = P("lev", GROUP, None, None)
    placed = (across, P(), P(None, GROUP, "lev"), across, P(), P(GROUP, "lev"), pairs, pairs, pairs, pairs)
    return jax.shard_map(shards, mesh=mesh, in_specs=placed, out_specs=(across, across), check_vma=False)
```

time: 217 us -> 170 us (0.78)
  starting transfers between devices: 83.3 us -> 54.9 us
  local copies, waits for them, and re-layouts: 30.5 us -> 13.2 us
  other arithmetic: 9.71 us -> 0.11 us
  Pallas kernels: 64.1 us -> 71.1 us
    ppermute x7 -> x5, starting transfers between devices: 46.6 us -> 25 us  [row_halos(): lax.ppermute(first, GROUP, [(b, a) for a, b in up])]
    all_to_all x2, starting transfers between devices: 26.6 us -> 14 us  [exchange(): lax.all_to_all(values, GROUP, split_axis=0, concat_axis=0, tiled=True)]
    ppermute x7 -> x5, waiting for transfers between devices: 25.6 us -> 14.3 us  [row_halos(): lax.ppermute(last, GROUP, up)]
    mul x4 -> x0, other arithmetic: 8.23 us -> none  [the longest x1 7.36 us: shards(): ocean_start = ocn_state * sea_frac[None, None]]
    ppermute x7 -> x5, waiting for transfers between devices: 0.53 us -> 8.52 us  [row_halos(): lax.ppermute(first, GROUP, [(b, a) for a, b in up])]
    reshape x10 -> x1, local copies, waits for them, and re-layouts: 9.53 us -> 1.62 us  [shards(): ocean = from_rows(ocean.reshape(OR, 2, OT, OL, LANES))]
    pallas_call x10 -> x12, Pallas kernels: 64.1 us -> 71.1 us  [call(): pl.pallas_call(kernel, out_shape=out_shape, scratch_shapes=list(scratch),...]
    unnamed x59 -> x41, local copies, waits for them, and re-layouts: 13.9 us -> 7.99 us
  transfers between devices with their start and end apart: 23 -> 17, of which waited for: 6 -> 7; matrix products, arithmetic and copies ran while one was open for 14% -> 2% of each run, Pallas kernels for 24% -> 26%
where the time goes in v2:
time: 170 us
  Pallas kernels  71.1 us (42%)
  starting transfers between devices  54.9 us (32%)
  waiting for transfers between devices  29.3 us (17%)
  local copies, waits for them, and re-layouts  13.2 us (8%)
    pallas_call x12, Pallas kernels, call(): pl.pallas_call(kernel, out_shape=out_shape, scratch_shapes=list(scratch),...  71.1 us
    ppermute x5, starting transfers between devices, row_halos(): lax.ppermute(first, GROUP, [(b, a) for a, b in up])  25 us
    ppermute x5, waiting for transfers between devices, row_halos(): lax.ppermute(last, GROUP, up)  14.3 us
    all_to_all x2, starting transfers between devices, exchange(): lax.all_to_all(values, GROUP, split_axis=0, concat_axis=0, tiled=True)  14 us
    ppermute x5, starting transfers between devices, partner(): lax.ppermute(edges, 'lev', [(i, (i + 1) % count) for i in range(count)])  13 us
    ppermute x5, waiting for transfers between devices, row_halos(): lax.ppermute(first, GROUP, [(b, a) for a, b in up])  8.52 us
    unnamed x41, local copies, waits for them, and re-layouts  7.99 us
    all_to_all x2, waiting for transfers between devices, exchange(): lax.all_to_all(values, GROUP, split_axis=0, concat_axis=0, tiled=True)  5.61 us
  transfers between devices with their start and end apart: 17, of which 7 were waited for; matrix products, arithmetic and copies ran while one was open for 2% of the time, Pallas kernels for 26%

profile of v2, /device:TPU:1, one launch (start us, length us, event | category | flops | bytes accessed | tf_op | source)
XLA Modules:
  0.0 169.6 jit_solution(695200310831212193)
XLA Ops:
  1.3 4.4 %prep.1 = (f32[1536,128]{1,0:T(8,128)}, f32[1536,128]{1,0:T(8,128)}, f32[72,128]{1,0:T(8,128)}, f32[2688,128]{1,0:T(8,128)}, f32[56,128]{1,0:T(8,128)}, /*index=...) custom-call(f32[2,48,2,1152]{3,2,1,0:T(2,128)} %atm_ref.1, ...), custom_call_target="tpu_custom_call" | custom-call | flops 3300000000 | bytes 9000000 | tf_op jit(solution)/shard_map/prep/pallas_call | solution.py:306
  5.7 2.5 %collective-permute-start = (f32[1536,128]{1,0:T(8,128)}, f32[1536,128]{1,0:T(8,128)S(1)}, u32[]{:S(2)}, u32[]{:S(2)}) collective-permute-start(f32[1536,128]{1,0:T(8,128)} %get-tuple-element.58.refs_1_), channel_id=1, source_target_pairs={{0,2},{2,4},{4,6},{6,8},{8,10},{10,12},{12,14},{14,16},{16,18},{18... | collective-permute-start | bytes 2359304 | tf_op jit(solution)/shard_map/ppermute | solution.py:324
  8.2 8.7 %collective-permute-start.1 = (f32[1536,128]{1,0:T(8,128)}, f32[1536,128]{1,0:T(8,128)S(1)}, u32[]{:S(2)}, u32[]{:S(2)}) collective-permute-start(f32[1536,128]{1,0:T(8,128)} %get-tuple-element.59.refs_0_), channel_id=1, source_target_pairs={{2,0},{4,2},{6,4},{8,6},{10,8},{12,10},{14,12},{16,14},{18,16},{20... | collective-permute-start | bytes 2359304 | tf_op jit(solution)/shard_map/ppermute | solution.py:324
  16.9 9.8 %temp_gather.1 = f32[128,4,128]{2,1,0:T(4,128)} custom-call(f32[64,128]{1,0:T(8,128)} %get-tuple-element.56.table_ref, s32[128,512]{1,0:T(8,128)} %bitcast.26, f32[128,512]{1,0:T(8,128)} %bitcast.22), custom_call_target="tpu_custom_call" | custom-call | flops 9900000256 | bytes 27000000 | tf_op jit(solution)/shard_map/temp_gather/pallas_call | solution.py:306
  26.7 7.9 %all-to-all-start = ((f32[128,4,128]{2,1,0:T(4,128)}), f32[128,4,128]{2,1,0:T(4,128)S(1)}, u32[]{:S(2)}, u32[]{:S(2)}) async-start(f32[128,4,128]{2,1,0:T(4,128)} %temp_gather.1), calls=%async_computation | async-start | bytes 524288 | tf_op jit(solution)/shard_map/all_to_all | solution.py:333
  38.2 3.8 %ocn_step.2 = (f32[2688,128]{1,0:T(8,128)}, f32[24,128]{1,0:T(8,128)}) custom-call(f32[2688,128]{1,0:T(8,128)} %get-tuple-element.57.own, f32[1536,128]{1,0:T(8,128)} %copy-done.4, f32[1536,128]{1,0:T(8,128)} %copy-done.5, f32[72,128]{1,0:T(8,128)} %copy-done.13, f32[24,128]{1,0:T(8,128)} %get-tuple-element.61.diff_ref, f32[56,128]{1,0:T(8,128)} %get-tuple-element.62.frac_ref), custom_call_target="tpu_custom_call" | custom-call | flops 3300000000 | bytes 9000000 | tf_op jit(solution)/shard_map/ocn_step/pallas_call | solution.py:306
  42.0 5.6 %all-to-all-done.val_ref = f32[128,4,128]{2,1,0:T(4,128)S(1)} async-done(((f32[128,4,128]{2,1,0:T(4,128)}), f32[128,4,128]{2,1,0:T(4,128)S(1)}, u32[]{:S(2)}, u32[]{:S(2)}) %all-to-all-start) | async-done | bytes 262176 | tf_op jit(solution)/shard_map/all_to_all | solution.py:333
  48.3 9.5 %temp_scatter.1 = (f32[18,128]{1,0:T(8,128)}, bf16[128,144]{1,0:T(8,128)(2,1)}) custom-call(f32[128,4,128]{2,1,0:T(4,128)} %copy-done.3, s32[128,512]{1,0:T(8,128)} %bitcast.23, f32[2,18,128]{2,1,0:T(8,128)} %get-tuple-element.66.state_ref, f32[2,18,128]{2,1,0:T(8,128)} %get-tuple-element.67.coef_ref.refs_6_), custom_call_target="tpu_custom_call" | custom-call | flops 9900000256 | bytes 27000000 | tf_op jit(solution)/shard_map/temp_scatter/pallas_call | solution.py:306
  57.8 4.1 %atm_step.4 = (f32[1536,128]{1,0:T(8,128)}, f32[1536,128]{1,0:T(8,128)}, f32[72,128]{1,0:T(8,128)}) custom-call(f32[1536,128]{1,0:T(8,128)} %get-tuple-element.59.refs_0_, f32[1536,128]{1,0:T(8,128)} %get-tuple-element.58.refs_1_, f32[1536,128]{1,0:T(8,128)} %copy-done.4, f32[1536,128]{1,0:T(8,128)} %copy-done.5, f32[72,128]{1,0:T(8,128)} %copy-done.13, ...), custom_call_target="tpu_custom_call" | custom-call | flops 2750000128 | bytes 7500000 | tf_op jit(solution)/shard_map/atm_step/pallas_call | solution.py:306
  63.4 3.5 %collective-permute-start.5 = (f32[72,128]{1,0:T(8,128)}, f32[72,128]{1,0:T(8,128)S(1)}, u32[]{:S(2)}, u32[]{:S(2)}) collective-permute-start(f32[72,128]{1,0:T(8,128)} %get-tuple-element.76), channel_id=1, source_target_pairs={{0,1},{1,0},{2,3},{3,2},{4,5},{5,4},{6,7},{7,6},{8,9},{9,8},{10,11... | collective-permute-start | bytes 110600 | tf_op jit(solution)/shard_map/ppermute | solution.py:329
  66.9 10.0 %flux_gather.1 = f32[128,8,128]{2,1,0:T(8,128)} custom-call(bf16[128,144]{1,0:T(8,128)(2,1)} %get-tuple-element.75.t_ref, s32[128,512]{1,0:T(8,128)} %bitcast.24, f32[128,512]{1,0:T(8,128)} %bitcast.25), custom_call_target="tpu_custom_call" | custom-call | flops 9900000256 | bytes 27000000 | tf_op jit(solution)/shard_map/flux_gather/pallas_call | solution.py:306
  78.5 7.2 %collective-permute-done.3.up.refs_2_ = f32[1536,128]{1,0:T(8,128)S(1)} collective-permute-done((f32[1536,128]{1,0:T(8,128)}, f32[1536,128]{1,0:T(8,128)S(1)}, u32[]{:S(2)}, u32[]{:S(2)}) %collective-permute-start.3) | collective-permute-done | bytes 786464 | tf_op jit(solution)/shard_map/ppermute | solution.py:324
  86.6 3.8 %ocn_step.3 = f32[2688,128]{1,0:T(8,128)} custom-call(f32[2688,128]{1,0:T(8,128)} %get-tuple-element.71.refs_8_.own, f32[1536,128]{1,0:T(8,128)} %copy-done.7, f32[1536,128]{1,0:T(8,128)} %copy-done.6, f32[72,128]{1,0:T(8,128)} %copy-done.15, f32[24,128]{1,0:T(8,128)} %get-tuple-element.61.diff_ref, f32[56,128]{1,0:T(8,128)} %get-tuple-element.62.frac_ref), custom_call_target="tpu_custom_call" | custom-call | flops 3300000000 | bytes 9000000 | tf_op jit(solution)/shard_map/ocn_step/pallas_call | solution.py:306
  92.2 3.2 %atm_step.5 = (f32[864,128]{1,0:T(8,128)}, f32[864,128]{1,0:T(8,128)}, f32[48,128]{1,0:T(8,128)}) custom-call(f32[1536,128]{1,0:T(8,128)} %get-tuple-element.81.refs_0_, f32[1536,128]{1,0:T(8,128)} %get-tuple-element.82.refs_1_, f32[1536,128]{1,0:T(8,128)} %copy-done.7, f32[1536,128]{1,0:T(8,128)} %copy-done.6, f32[72,128]{1,0:T(8,128)} %copy-done.15, ...), custom_call_target="tpu_custom_call" | custom-call | flops 2750000128 | bytes 7500000 | tf_op jit(solution)/shard_map/atm_step/pallas_call | solution.py:306
  95.5 6.2 %all-to-all-start.1 = ((f32[128,8,128]{2,1,0:T(8,128)}), f32[128,8,128]{2,1,0:T(8,128)S(1)}, u32[]{:S(2)}, u32[]{:S(2)}) async-start(f32[128,8,128]{2,1,0:T(8,128)} %flux_gather.1), calls=%async_computation.1 | async-start | bytes 1048576 | tf_op jit(solution)/shard_map/all_to_all | solution.py:333
  101.6 6.8 %collective-permute-start.7 = (f32[864,128]{1,0:T(8,128)}, f32[864,128]{1,0:T(8,128)S(1)}, u32[]{:S(2)}, u32[]{:S(2)}) collective-permute-start(f32[864,128]{1,0:T(8,128)} %get-tuple-element.87.refs_0_), channel_id=1, source_target_pairs={{2,0},{4,2},{6,4},{8,6},{10,8},{12,10},{14,12},{16,14},{18,16},{20... | collective-permute-start | bytes 1327112 | tf_op jit(solution)/shard_map/ppermute | solution.py:324
  108.5 3.8 %collective-permute-start.8 = (f32[48,128]{1,0:T(8,128)}, f32[48,128]{1,0:T(8,128)S(1)}, u32[]{:S(2)}, u32[]{:S(2)}) collective-permute-start(f32[48,128]{1,0:T(8,128)} %get-tuple-element.89), channel_id=1, source_target_pairs={{0,1},{1,0},{2,3},{3,2},{4,5},{5,4},{6,7},{7,6},{8,9},{9,8},{10,11... | collective-permute-start | bytes 73736 | tf_op jit(solution)/shard_map/ppermute | solution.py:329
  114.6 6.9 %collective-permute-done.7.refs_3_ = f32[864,128]{1,0:T(8,128)S(1)} collective-permute-done((f32[864,128]{1,0:T(8,128)}, f32[864,128]{1,0:T(8,128)S(1)}, u32[]{:S(2)}, u32[]{:S(2)}) %collective-permute-start.7) | collective-permute-done | bytes 442400 | tf_op jit(solution)/shard_map/ppermute | solution.py:324
  121.5 6.2 %collective-permute-done.6.refs_2_ = f32[864,128]{1,0:T(8,128)S(1)} collective-permute-done((f32[864,128]{1,0:T(8,128)}, f32[864,128]{1,0:T(8,128)S(1)}, u32[]{:S(2)}, u32[]{:S(2)}) %collective-permute-start.6) | collective-permute-done | bytes 442400 | tf_op jit(solution)/shard_map/ppermute | solution.py:324
  128.5 2.8 %atm_step.6 = (f32[864,128]{1,0:T(8,128)}, f32[864,128]{1,0:T(8,128)}, f32[48,128]{1,0:T(8,128)}) custom-call(f32[864,128]{1,0:T(8,128)} %get-tuple-element.87.refs_0_, f32[864,128]{1,0:T(8,128)} %get-tuple-element.88.refs_1_, f32[864,128]{1,0:T(8,128)} %copy-done.11, f32[864,128]{1,0:T(8,128)} %copy-done.10, f32[48,128]{1,0:T(8,128)} %copy-done.17, ...), custom_call_target="tpu_custom_call" | custom-call | flops 2750000128 | bytes 7500000 | tf_op jit(solution)/shard_map/atm_step/pallas_call | solution.py:306
  131.3 2.4 %collective-permute-start.11 = (f32[48,128]{1,0:T(8,128)}, f32[48,128]{1,0:T(8,128)S(1)}, u32[]{:S(2)}, u32[]{:S(2)}) collective-permute-start(f32[48,128]{1,0:T(8,128)} %get-tuple-element.99), channel_id=1, source_target_pairs={{0,1},{1,0},{2,3},{3,2},{4,5},{5,4},{6,7},{7,6},{8,9},{9,8},{10,11... | collective-permute-start | bytes 73736 | tf_op jit(solution)/shard_map/ppermute | solution.py:329
  136.0 15.2 %forcing_scatter.1 = (f32[2,56,128]{2,1,0:T(8,128)}, f32[2,56,128]{2,1,0:T(8,128)}, f32[2,14,128]{2,1,0:T(8,128)}, f32[2,14,128]{2,1,0:T(8,128)}) custom-call(f32[128,8,128]{2,1,0:T(8,128)} %copy-done.1, s32[128,512]{1,0:T(8,128)} %bitcast.27, f32[56,128]{1,0:T(8,128)} %get-tuple-element.62.frac_ref), custom_call_target="tpu_custom_call" | custom-call | flops 16499999744 | bytes 45000000 | tf_op jit(solution)/shard_map/forcing_scatter/pallas_call | solution.py:306
  152.0 6.9 %collective-permute-start.13 = (f32[2,14,128]{2,1,0:T(8,128)}, f32[2,14,128]{2,1,0:T(8,128)S(1)}, u32[]{:S(2)}, u32[]{:S(2)}) collective-permute-start(f32[2,14,128]{2,1,0:T(8,128)} %get-tuple-element.109), channel_id=1, source_target_pairs={{2,0},{4,2},{6,4},{8,6},{10,8},{12,10},{14,12},{16,14},{18,16},{20... | collective-permute-start | bytes 43016 | tf_op jit(solution)/shard_map/ppermute | solution.py:324
  160.6 2.8 %atm_step.7 = (f32[864,128]{1,0:T(8,128)}, f32[864,128]{1,0:T(8,128)}, f32[48,128]{1,0:T(8,128)}) custom-call(f32[864,128]{1,0:T(8,128)} %get-tuple-element.92.refs_0_, f32[864,128]{1,0:T(8,128)} %get-tuple-element.93.refs_1_, f32[864,128]{1,0:T(8,128)} %copy-done.9, f32[864,128]{1,0:T(8,128)} %copy-done.8, f32[48,128]{1,0:T(8,128)} %copy-done.16, ...), custom_call_target="tpu_custom_call" | custom-call | flops 2750000128 | bytes 7500000 | tf_op jit(solution)/shard_map/atm_step/pallas_call | solution.py:306
  (73 shorter events, 24.7 us)
Async XLA Ops:
  5.7 31.3 %collective-permute-start = (f32[1536,128]{1,0:T(8,128)}, f32[1536,128]{1,0:T(8,128)S(1)}, u32[]{:S(2)}, u32[]{:S(2)}) collective-permute-start(f32[1536,128]{1,0:T(8,128)} %get-tuple-element.58.refs_1_), channel_id=1, source_target_pairs={{0,2},{2,4},{4,6},{6,8},{8,10},{10,12},{12,14},{14,16},{16,18},{18... | collective-permute-start | bytes 2359304 | tf_op jit(solution)/shard_map/ppermute | solution.py:324
  8.2 28.8 %collective-permute-start.1 = (f32[1536,128]{1,0:T(8,128)}, f32[1536,128]{1,0:T(8,128)S(1)}, u32[]{:S(2)}, u32[]{:S(2)}) collective-permute-start(f32[1536,128]{1,0:T(8,128)} %get-tuple-element.59.refs_0_), channel_id=1, source_target_pairs={{2,0},{4,2},{6,4},{8,6},{10,8},{12,10},{14,12},{16,14},{18,16},{20... | collective-permute-start | bytes 2359304 | tf_op jit(solution)/shard_map/ppermute | solution.py:324
  16.9 17.6 %copy-start.14 = (f32[72,128]{1,0:T(8,128)S(1)}, f32[72,128]{1,0:T(8,128)}, u32[]{:S(2)}) copy-start(f32[72,128]{1,0:T(8,128)} %get-tuple-element.60) | copy-start | bytes 110596
  26.7 21.0 %all-to-all-start = ((f32[128,4,128]{2,1,0:T(4,128)}), f32[128,4,128]{2,1,0:T(4,128)S(1)}, u32[]{:S(2)}, u32[]{:S(2)}) async-start(f32[128,4,128]{2,1,0:T(4,128)} %temp_gather.1), calls=%async_computation | async-start | bytes 524288 | tf_op jit(solution)/shard_map/all_to_all | solution.py:333
  34.5 2.5 %collective-permute-start.2 = (f32[72,128]{1,0:T(8,128)S(1)}, f32[72,128]{1,0:T(8,128)S(1)}, u32[]{:S(2)}, u32[]{:S(2)}) collective-permute-start(f32[72,128]{1,0:T(8,128)S(1)} %copy-done.14), channel_id=1, source_target_pairs={{0,1},{1,0},{2,3},{3,2},{4,5},{5,4},{6,7},{7,6},{8,9},{9,8},{10,11... | collective-permute-start | bytes 110600 | tf_op jit(solution)/shard_map/ppermute | solution.py:329
  62.0 16.5 %collective-permute-start.4 = (f32[1536,128]{1,0:T(8,128)}, f32[1536,128]{1,0:T(8,128)S(1)}, u32[]{:S(2)}, u32[]{:S(2)}) collective-permute-start(f32[1536,128]{1,0:T(8,128)} %get-tuple-element.81.refs_0_), channel_id=1, source_target_pairs={{2,0},{4,2},{6,4},{8,6},{10,8},{12,10},{14,12},{16,14},{18,16},{20... | collective-permute-start | bytes 2359304 | tf_op jit(solution)/shard_map/ppermute | solution.py:324
  63.4 22.3 %collective-permute-start.3 = (f32[1536,128]{1,0:T(8,128)}, f32[1536,128]{1,0:T(8,128)S(1)}, u32[]{:S(2)}, u32[]{:S(2)}) collective-permute-start(f32[1536,128]{1,0:T(8,128)} %get-tuple-element.82.refs_1_), channel_id=1, source_target_pairs={{0,2},{2,4},{4,6},{6,8},{8,10},{10,12},{12,14},{14,16},{16,18},{18... | collective-permute-start | bytes 2359304 | tf_op jit(solution)/shard_map/ppermute | solution.py:324
  63.4 13.5 %collective-permute-start.5 = (f32[72,128]{1,0:T(8,128)}, f32[72,128]{1,0:T(8,128)S(1)}, u32[]{:S(2)}, u32[]{:S(2)}) collective-permute-start(f32[72,128]{1,0:T(8,128)} %get-tuple-element.76), channel_id=1, source_target_pairs={{0,1},{1,0},{2,3},{3,2},{4,5},{5,4},{6,7},{7,6},{8,9},{9,8},{10,11... | collective-permute-start | bytes 110600 | tf_op jit(solution)/shard_map/ppermute | solution.py:329
  76.9 8.8 %copy-start.15 = (f32[72,128]{1,0:T(8,128)}, f32[72,128]{1,0:T(8,128)S(1)}, u32[]{:S(2)}) copy-start(f32[72,128]{1,0:T(8,128)S(1)} %collective-permute-done.5.edges_ref.refs_4_) | copy-start | bytes 110596
  78.5 7.2 %copy-start.6 = (f32[1536,128]{1,0:T(8,128)}, f32[1536,128]{1,0:T(8,128)S(1)}, u32[]{:S(2)}) copy-start(f32[1536,128]{1,0:T(8,128)S(1)} %collective-permute-done.4.down.refs_3_) | copy-start | bytes 2359300
  95.5 39.7 %all-to-all-start.1 = ((f32[128,8,128]{2,1,0:T(8,128)}), f32[128,8,128]{2,1,0:T(8,128)S(1)}, u32[]{:S(2)}, u32[]{:S(2)}) async-start(f32[128,8,128]{2,1,0:T(8,128)} %flux_gather.1), calls=%async_computation.1 | async-start | bytes 1048576 | tf_op jit(solution)/shard_map/all_to_all | solution.py:333
  101.6 19.9 %collective-permute-start.7 = (f32[864,128]{1,0:T(8,128)}, f32[864,128]{1,0:T(8,128)S(1)}, u32[]{:S(2)}, u32[]{:S(2)}) collective-permute-start(f32[864,128]{1,0:T(8,128)} %get-tuple-element.87.refs_0_), channel_id=1, source_target_pairs={{2,0},{4,2},{6,4},{8,6},{10,8},{12,10},{14,12},{16,14},{18,16},{20... | collective-permute-start | bytes 1327112 | tf_op jit(solution)/shard_map/ppermute | solution.py:324
  108.5 19.2 %collective-permute-start.6 = (f32[864,128]{1,0:T(8,128)}, f32[864,128]{1,0:T(8,128)S(1)}, u32[]{:S(2)}, u32[]{:S(2)}) collective-permute-start(f32[864,128]{1,0:T(8,128)} %get-tuple-element.88.refs_1_), channel_id=1, source_target_pairs={{0,2},{2,4},{4,6},{6,8},{8,10},{10,12},{12,14},{14,16},{16,18},{18... | collective-permute-start | bytes 1327112 | tf_op jit(solution)/shard_map/ppermute | solution.py:324
  108.5 6.1 %collective-permute-start.8 = (f32[48,128]{1,0:T(8,128)}, f32[48,128]{1,0:T(8,128)S(1)}, u32[]{:S(2)}, u32[]{:S(2)}) collective-permute-start(f32[48,128]{1,0:T(8,128)} %get-tuple-element.89), channel_id=1, source_target_pairs={{0,1},{1,0},{2,3},{3,2},{4,5},{5,4},{6,7},{7,6},{8,9},{9,8},{10,11... | collective-permute-start | bytes 73736 | tf_op jit(solution)/shard_map/ppermute | solution.py:329
  114.6 13.1 %copy-start.17 = (f32[48,128]{1,0:T(8,128)}, f32[48,128]{1,0:T(8,128)S(1)}, u32[]{:S(2)}) copy-start(f32[48,128]{1,0:T(8,128)S(1)} %collective-permute-done.8.refs_4_) | copy-start | bytes 73732
  131.3 19.8 %collective-permute-start.11 = (f32[48,128]{1,0:T(8,128)}, f32[48,128]{1,0:T(8,128)S(1)}, u32[]{:S(2)}, u32[]{:S(2)}) collective-permute-start(f32[48,128]{1,0:T(8,128)} %get-tuple-element.99), channel_id=1, source_target_pairs={{0,1},{1,0},{2,3},{3,2},{4,5},{5,4},{6,7},{7,6},{8,9},{9,8},{10,11... | collective-permute-start | bytes 73736 | tf_op jit(solution)/shard_map/ppermute | solution.py:329
  133.7 17.4 %collective-permute-start.10 = (f32[864,128]{1,0:T(8,128)}, f32[864,128]{1,0:T(8,128)S(1)}, u32[]{:S(2)}, u32[]{:S(2)}) collective-permute-start(f32[864,128]{1,0:T(8,128)} %get-tuple-element.92.refs_0_), channel_id=1, source_target_pairs={{2,0},{4,2},{6,4},{8,6},{10,8},{12,10},{14,12},{16,14},{18,16},{20... | collective-permute-start | bytes 1327112 | tf_op jit(solution)/shard_map/ppermute | solution.py:324
  134.9 17.1 %collective-permute-start.9 = (f32[864,128]{1,0:T(8,128)}, f32[864,128]{1,0:T(8,128)S(1)}, u32[]{:S(2)}, u32[]{:S(2)}) collective-permute-start(f32[864,128]{1,0:T(8,128)} %get-tuple-element.93.refs_1_), channel_id=1, source_target_pairs={{0,2},{2,4},{4,6},{6,8},{8,10},{10,12},{12,14},{14,16},{16,18},{18... | collective-permute-start | bytes 1327112 | tf_op jit(solution)/shard_map/ppermute | solution.py:324
  151.1 9.4 %copy-start.16 = (f32[48,128]{1,0:T(8,128)}, f32[48,128]{1,0:T(8,128)S(1)}, u32[]{:S(2)}) copy-start(f32[48,128]{1,0:T(8,128)S(1)} %collective-permute-done.11.refs_4_) | copy-start | bytes 73732
  151.1 9.4 %copy-start.8 = (f32[864,128]{1,0:T(8,128)}, f32[864,128]{1,0:T(8,128)S(1)}, u32[]{:S(2)}) copy-start(f32[864,128]{1,0:T(8,128)S(1)} %collective-permute-done.10.refs_3_) | copy-start | bytes 1327108
  152.0 8.6 %copy-start.9 = (f32[864,128]{1,0:T(8,128)}, f32[864,128]{1,0:T(8,128)S(1)}, u32[]{:S(2)}) copy-start(f32[864,128]{1,0:T(8,128)S(1)} %collective-permute-done.9.refs_2_) | copy-start | bytes 1327108
  152.0 14.4 %collective-permute-start.12 = (f32[2,14,128]{2,1,0:T(8,128)}, f32[2,14,128]{2,1,0:T(8,128)S(1)}, u32[]{:S(2)}, u32[]{:S(2)}) collective-permute-start(f32[2,14,128]{2,1,0:T(8,128)} %get-tuple-element.108), channel_id=1, source_target_pairs={{0,2},{2,4},{4,6},{6,8},{8,10},{10,12},{12,14},{14,16},{16,18},{18... | collective-permute-start | bytes 43016 | tf_op jit(solution)/shard_map/ppermute | solution.py:324
  152.0 14.5 %collective-permute-start.13 = (f32[2,14,128]{2,1,0:T(8,128)}, f32[2,14,128]{2,1,0:T(8,128)S(1)}, u32[]{:S(2)}, u32[]{:S(2)}) collective-permute-start(f32[2,14,128]{2,1,0:T(8,128)} %get-tuple-element.109), channel_id=1, source_target_pairs={{2,0},{4,2},{6,4},{8,6},{10,8},{12,10},{14,12},{16,14},{18,16},{20... | collective-permute-start | bytes 43016 | tf_op jit(solution)/shard_map/ppermute | solution.py:324
  158.9 7.6 %collective-permute-start.14 = (f32[2,56,128]{2,1,0:T(8,128)}, f32[2,56,128]{2,1,0:T(8,128)S(1)}, u32[]{:S(2)}, u32[]{:S(2)}) collective-permute-start(f32[2,56,128]{2,1,0:T(8,128)} %get-tuple-element.107.gain_ref), channel_id=1, source_target_pairs={{0,1},{1,0},{2,3},{3,2},{4,5},{5,4},{6,7},{7,6},{8,9},{9,8},{10,11... | collective-permute-start | bytes 172040 | tf_op jit(solution)/shard_map/ppermute | solution.py:329
  (13 other events, 16.2 us)

commit v3 on v2

--- a/solution.py
+++ b/solution.py
@@ -64,12 +64,12 @@
     lax.fori_loop(0, index_ref.shape[0] // 8, group, 0)
 
 
-def scatter_loop(val_ref, index_ref, H, L, F, place_of=lambda h: h):
+def scatter_loop(val_ref, index_ref, H, L, F, start=0, stop=None):
     shift = L.bit_length() - 1
     def group(g, acc):
         base = pl.multiple_of(g * 8, 8)
         index = index_ref[pl.ds(base, 8), :]
-        hi, lo = place_of(index >> shift), index & (L - 1)
+        hi, lo = index >> shift, index & (L - 1)
         for r in range(8):
             masks = hits(hi[r : r + 1], H)
             a = []
@@ -80,7 +80,8 @@
             a = jnp.concatenate(a, axis=0)
             acc = acc + lax.dot_general(a, one_hot(lo[r : r + 1], L), (((1,), (1,)), ((), ())), preferred_element_type=F32)
         return acc
-    acc = lax.fori_loop(0, index_ref.shape[0] // 8, group, jnp.zeros((F * SPLITS * H, L), F32))
+    stop = stop or index_ref.shape[0]
+    acc = lax.fori_loop(start // 8, stop // 8, group, jnp.zeros((F * SPLITS * H, L), F32))
     return [sum(acc[(f * SPLITS + i) * H : (f * SPLITS + i + 1) * H] for i in range(SPLITS)) for f in range(F)]
 
 
@@ -162,7 +163,7 @@
     return jnp.broadcast_to(edges[:, i : i + 1], edges.shape)
 
 
-def prep_kernel(atm_ref, ocn_ref, mask_ref, inner_ref, coef_ref, adiff_ref, odiff_ref, low, high, edges, ocean, frac, table, surface, coef, adiff, odiff):
+def prep_kernel(atm_ref, ocn_ref, mask_ref, coef_ref, adiff_ref, odiff_ref, low, high, edges, ocean, frac, table, surface, coef, adiff, odiff):
     adiff[...] = jnp.broadcast_to(adiff_ref[...], (LANES, AL)).T
     odiff[...] = jnp.broadcast_to(odiff_ref[...], (LANES, OL)).T
     ends = []
@@ -180,11 +181,14 @@
             ends.append(pair)
     edges[:AL, :] = edges_of(ends)
     table[...] = jnp.zeros_like(table)
+    block, count = lax.axis_index(GROUP), lax.axis_size(GROUP)
     ends = []
     for r in range(OR):
+        row = block * OR + r
+        inner = jnp.where((row > 0) & (row < OR * count - 1), 1.0, 0.0)
         for j in range(OT):
             at = r * OT + j
-            frac[at : at + 1, :] = mask_ref[r : r + 1, j * LANES : (j + 1) * LANES].astype(F32) * inner_ref[r : r + 1, :]
+            frac[at : at + 1, :] = mask_ref[r : r + 1, j * LANES : (j + 1) * LANES].astype(F32) * inner
         for f in range(2):
             pair = []
             for j in range(OT):
@@ -203,9 +207,12 @@
     edges[AL:, :] = edges_of(ends)
 
 
-def atm_kernel(share, low, high, up, down, edges_ref, diff_ref, coef_ref, temp_ref, *rest):
+def atm_kernel(low, high, up, down, edges_ref, diff_ref, coef_ref, temp_ref, *rest):
+    share, final = len(rest) == 5, len(rest) == 1
     if share:
         ocean, ocn_edges, out_low, out_high, out_edges = rest
+    elif final:
+        out_low = out_high = rest[0]
     else:
         out_low, out_high, out_edges = rest
     edges, side_gain = edges_ref[:AL, :], diff_ref[...]
@@ -220,18 +227,22 @@
                 gain = (1.0, MOIST_RATIO)[f] * temp_ref[at : at + 1, :]
                 gain = coef_ref[f, at : at + 1, :] * (gain - old[:1])
                 fresh = jnp.concatenate([fresh[:8] + jnp.where(top, gain, 0.0), fresh[8:]], axis=0)
-                out[(f * AT + j) * AL : (f * AT + j + 1) * AL, :] = fresh
+                if final:
+                    out[f, :, r, j * LANES : (j + 1) * LANES] = fresh
+                else:
+                    out[(f * AT + j) * AL : (f * AT + j + 1) * AL, :] = fresh
                 return fresh
             i, base = 2 * r + f, f * AT * AL
             ends.append(step_row(*((rows[k], base) for k in (r + 1, r, r + 2)), AT, AL, edge(edges, 2 * i + 1), edge(edges, 2 * i), own_gain, side_gain, VERT_MIX, finish))
-    out_edges[:AL, :] = edges_of(ends)
+    if not final:
+        out_edges[:AL, :] = edges_of(ends)
     if share:
         out_low[ASIZE:, :] = ocean[:OSIZE, :]
         out_high[ASIZE:, :] = ocean[(OR - 1) * OSIZE :, :]
         out_edges[AL:, :] = ocn_edges[...]
 
 
-def ocn_kernel(own, up, down, edges_ref, diff_ref, frac_ref, out, *out_edges):
+def ocn_kernel(final, own, up, down, edges_ref, diff_ref, frac_ref, out, out_more):
     edges, side_gain = edges_ref[AL:, :], diff_ref[...]
     own_gain = (1.0 - 2.0 * OCEAN_MIX) - 4.0 * side_gain
     ends = []
@@ -240,20 +251,29 @@
             def finish(j, fresh, old, f=f, r=r):
                 fresh = fresh * frac_ref[r * OT + j : r * OT + j + 1, :]
                 line = ((r * 2 + f) * OT + j) * OL
-                out[line : line + OL, :] = fresh
+                if final:
+                    out[f, :, r, j * LANES : (j + 1) * LANES] = fresh
+                    out_more[f, :, r, j * LANES : (j + 1) * LANES] = fresh[:2]
+                else:
+                    out[line : line + OL, :] = fresh
                 return fresh
             i = 2 * r + f
             part = lambda k: (own, (k * 2 + f) * OT * OL)
             above = part(r - 1) if r else (up, ASIZE + f * OT * OL)
             below = part(r + 1) if r < OR - 1 else (down, ASIZE + f * OT * OL)
             ends.append(step_row(part(r), above, below, OT, OL, edge(edges, 2 * i + 1), edge(edges, 2 * i), own_gain, side_gain, OCEAN_MIX, finish))
-    if out_edges:
-        out_edges[0][...] = edges_of(ends)
-
-
-def forcing_kernel(val_ref, cell_ref, frac_ref, out_ref, gain_ref, low, high):
-    for f, total in enumerate(scatter_loop(val_ref, cell_ref, 32, 256, 2)):
-        total = (HEAT_GAIN, -SALT_GAIN)[f] * total[: OR * OT // 2]
+    if not final:
+        out_more[...] = edges_of(ends)
+
+
+def half_kernel(val_ref, cell_ref, out_ref):
+    for f, total in enumerate(scatter_loop(val_ref, cell_ref, 32, 256, 2, stop=val_ref.shape[0] // 2)):
+        out_ref[f] = total
+
+
+def forcing_kernel(half_ref, val_ref, cell_ref, frac_ref, out_ref, gain_ref, low, high):
+    for f, total in enumerate(scatter_loop(val_ref, cell_ref, 32, 256, 2, start=val_ref.shape[0] // 2)):
+        total = (HEAT_GAIN, -SALT_GAIN)[f] * (half_ref[f] + total)[: OR * OT // 2]
         for side in range(2):
             out_ref[f, pl.ds(side, OR * OT // 2, stride=2), :] = total[:, side * LANES : (side + 1) * LANES]
         gain_ref[f] = out_ref[f] * frac_ref[...]
@@ -301,21 +321,18 @@
 ANY = pl.BlockSpec(memory_space=pl.ANY)
 
 
-def call(kernel, name, micros, out_shape, *args, scratch=(), **more):
+def call(kernel, name, micros, out_shape, *args, scratch=(), hbm=(), **more):
+    args = [x if i in hbm else pltpu.with_memory_space_constraint(x, pltpu.VMEM) for i, x in enumerate(args)]
     specs = {"in_specs": [VM] * len(args), "out_specs": jax.tree.map(lambda _: VM, out_shape), **more}
     return pl.pallas_call(
         kernel,
         out_shape=out_shape,
         scratch_shapes=list(scratch),
         cost_estimate=pl.CostEstimate(flops=int(micros * 1.1e9), bytes_accessed=int(micros * 3e6), transcendentals=0),
+        compiler_params=pltpu.CompilerParams(vmem_limit_bytes=20 << 20),
         name=name,
         **specs,
     )(*args)
-
-
-def from_rows(tiles):
-    rows, fields, count, levels, lanes = tiles.shape
-    return tiles.transpose(1, 3, 0, 2, 4).reshape(fields, levels, rows, count * lanes)
 
 
 def row_halos(first, last):
@@ -346,9 +363,7 @@
     o2a_weights,
 ):
     group_size = lax.axis_size(GROUP)
-    shape = lambda *s: jax.ShapeDtypeStruct(s, F32)
-    row_ids = lax.axis_index(GROUP) * OR + lax.broadcasted_iota(jnp.int32, (OR, LANES), 0)
-    inner = ((row_ids > 0) & (row_ids < OR * group_size - 1)).astype(F32)
+    shape = lambda *s: pltpu.VMEM(s, F32)
     cols, cells = atm_pair_cols[0, 0], ocn_pair_cells[0, 0]
     both = shape(ASIZE + OSIZE, LANES)
 
@@ -360,7 +375,6 @@
         atm_state,
         ocn_state,
         sea_mask,
-        inner,
         atm_surface_coef,
         atm_diffusion[None],
         ocn_diffusion[None],
@@ -370,43 +384,45 @@
 
     outgoing = call(temp_kernel, "temp_gather", 9, shape(group_size, 4, LANES), table, cells, o2a_weights[0, 0], scratch=[pltpu.VMEM((128, SPLITS * 64), BF16)])
     incoming = exchange(outgoing)
-    ocean, ocn_edges = call(ocn_kernel, "ocn_step", 3, (shape(OR * OSIZE, LANES), shape(OL, LANES)), ocean, up, down, beside, ocn_diff, frac)
+    ocn_step = lambda *refs: ocn_kernel(False, *refs)
+    ocean, ocn_edges = call(ocn_step, "ocn_step", 3, (shape(OR * OSIZE, LANES), shape(OL, LANES)), ocean, up, down, beside, ocn_diff, frac)
     incoming, ocean, ocn_edges = lax.optimization_barrier((incoming, ocean, ocn_edges))
 
-    temp, flux_table = call(flux_kernel, "temp_scatter", 9, (shape(AR * AT, LANES), jax.ShapeDtypeStruct((128, SPLITS * 48), BF16)), incoming, cols, surface, coef, scratch=[pltpu.VMEM((24, LANES), F32)])
-
-    def atm_step(share, low, high, up, down, beside, *more):
-        rows = shape(ASIZE + OSIZE * share, LANES)
-        outs = (rows, rows, shape(AL + OL * share, LANES))
-        return call(lambda *refs: atm_kernel(share, *refs), "atm_step", 2.5, outs, low, high, up, down, beside, atm_diff, coef, temp, *more)
-
-    low, high, edges = atm_step(True, low, high, up, down, beside, ocean, ocn_edges)
+    temp, flux_table = call(flux_kernel, "temp_scatter", 9, (shape(AR * AT, LANES), pltpu.VMEM((128, SPLITS * 48), BF16)), incoming, cols, surface, coef, scratch=[pltpu.VMEM((24, LANES), F32)])
+
+    def atm_step(low, high, up, down, beside, *more, outs=None):
+        rows = shape(ASIZE + (OSIZE if more else 0), LANES)
+        outs = outs or (rows, rows, shape(AL + (OL if more else 0), LANES))
+        return call(atm_kernel, "atm_step", 2.5, outs, low, high, up, down, beside, atm_diff, coef, temp, *more)
+
+    low, high, edges = atm_step(low, high, up, down, beside, ocean, ocn_edges)
     up, down = row_halos(low, high)
     beside = partner(edges)
     flux_table, low, high = lax.optimization_barrier((flux_table, low, high))
 
     outgoing = call(send_kernel, "flux_gather", 9, shape(group_size, 8, LANES), flux_table, cols, a2o_weights[0, 0])
+    incoming = exchange(outgoing)
     outgoing, up, down, beside = lax.optimization_barrier((outgoing, up, down, beside))
-    ocean = call(ocn_kernel, "ocn_step", 3, shape(OR * OSIZE, LANES), ocean, up, down, beside, ocn_diff, frac)
-    ocean = from_rows(ocean.reshape(OR, 2, OT, OL, LANES))
-    low, high, edges = atm_step(False, low, high, up, down, beside)
-    outgoing, ocean, low, high, edges = lax.optimization_barrier((outgoing, ocean, low, high, edges))
+    low, high, edges = atm_step(low, high, up, down, beside)
+    ocn_last_step = lambda *refs: ocn_kernel(True, *refs)
+    ocean, top = call(ocn_last_step, "ocn_step", 3, (jax.ShapeDtypeStruct(ocn_state.shape, F32), shape(2, 2, OR, OT * LANES)), ocean, up, down, beside, ocn_diff, frac)
     up, down = row_halos(low, high)
     beside = partner(edges)
-    incoming = exchange(outgoing)
-    low, high, edges = atm_step(False, low, high, up, down, beside)
+    incoming, ocean, top, low, high = lax.optimization_barrier((incoming, ocean, top, low, high))
+
+    half = call(half_kernel, "forcing_half", 7.5, shape(2, 32, 256), incoming, cells)
+    half, up, down, beside = lax.optimization_barrier((half, up, down, beside))
+    low, high, edges = atm_step(low, high, up, down, beside)
     up, down = row_halos(low, high)
     beside = partner(edges)
-    incoming, low, high = lax.optimization_barrier((incoming, low, high))
+    half, low, high = lax.optimization_barrier((half, low, high))
 
     every = shape(2, OR * OT, LANES)
-    forcing, gained, first, last = call(forcing_kernel, "forcing_scatter", 15, (every, every, shape(2, OT, LANES), shape(2, OT, LANES)), incoming, cells, frac)
-    forcing, gained, first, last, up, down, beside = lax.optimization_barrier((forcing, gained, first, last, up, down, beside))
+    forcing, gained, first, last = call(forcing_kernel, "forcing_scatter", 7.5, (every, every, shape(2, OT, LANES), shape(2, OT, LANES)), half, incoming, cells, frac)
     above, below = row_halos(first, last)
     side = partner(gained)
-
-    low, high, _ = atm_step(False, low, high, up, down, beside)
-    atm_next = from_rows(jnp.stack([low, high]).reshape(AR, 2, AT, AL, LANES))
+    forcing, up, down, beside = lax.optimization_barrier((forcing, up, down, beside))
+    atm_next = atm_step(low, high, up, down, beside, outs=(jax.ShapeDtypeStruct(atm_state.shape, F32),))[0]
 
     line = pltpu.VMEM((OR * OT, LANES), F32)
     ocean_next = call(
@@ -415,7 +431,7 @@
         1,
         jax.ShapeDtypeStruct(ocean.shape, F32),
         ocean,
-        ocean[:, :2],
+        top,
         forcing,
         gained,
         above,
@@ -427,6 +443,7 @@
         out_specs=ANY,
         scratch=[pltpu.VMEM((6 * OT, LANES), F32), line, line, pltpu.VMEM((2, 2, OR, OT * LANES), F32), pltpu.SemaphoreType.DMA],
         input_output_aliases={0: 0},
+        hbm=(0,),
     )
     return atm_next, ocean_next
 

time: 170 us -> 136 us (0.80)
  Pallas kernels: 71.1 us -> 52.4 us
  waiting for transfers between devices: 29.3 us -> 14.8 us
    pallas_call x12 -> x13, Pallas kernels: 71.1 us -> 52.4 us  [call(): pl.pallas_call(kernel, out_shape=out_shape, scratch_shapes=list(scratch),...]
    ppermute x5, waiting for transfers between devices: 8.52 us -> 0.01 us  [row_halos(): lax.ppermute(first, GROUP, [(b, a) for a, b in up])]
    ppermute x5, waiting for transfers between devices: 14.3 us -> 5.87 us  [row_halos(): lax.ppermute(last, GROUP, up)]
    unnamed x41 -> x62, local copies, waits for them, and re-layouts: 7.99 us -> 13.3 us
    all_to_all x2, starting transfers between devices: 14 us -> 17.4 us  [exchange(): lax.all_to_all(values, GROUP, split_axis=0, concat_axis=0, tiled=True)]
    ppermute x5, starting transfers between devices: 13 us -> 10 us  [partner(): lax.ppermute(edges, 'lev', [(i, (i + 1) % count) for i in range(count)])]
    ppermute x5, starting transfers between devices: 25 us -> 22.6 us  [row_halos(): lax.ppermute(first, GROUP, [(b, a) for a, b in up])]
    reshape x3 -> x0, local copies, waits for them, and re-layouts: 2.01 us -> none  [the longest x1 1.62 us: shards(): ocean = from_rows(ocean.reshape(OR, 2, OT, OL, LANES))]
  transfers between devices with their start and end apart: 17 -> 17, of which waited for: 7 -> 4; matrix products, arithmetic and copies ran while one was open for 2% -> 0% of each run, Pallas kernels for 26% -> 28%
where the time goes in v3:
time: 136 us; the launch traced here: 135 us
  starting transfers between devices  53.9 us (40%)
  Pallas kernels  52.4 us (39%)
  waiting for transfers between devices  14.8 us (11%)
  local copies, waits for them, and re-layouts  13.3 us (10%)
    pallas_call x13, Pallas kernels, call(): pl.pallas_call(kernel, out_shape=out_shape, scratch_shapes=list(scratch),...  52.4 us
    ppermute x5, starting transfers between devices, row_halos(): lax.ppermute(first, GROUP, [(b, a) for a, b in up])  22.6 us
    all_to_all x2, starting transfers between devices, exchange(): lax.all_to_all(values, GROUP, split_axis=0, concat_axis=0, tiled=True)  17.4 us
    unnamed x62, local copies, waits for them, and re-layouts  13.3 us
    ppermute x5, starting transfers between devices, partner(): lax.ppermute(edges, 'lev', [(i, (i + 1) % count) for i in range(count)])  10 us
    all_to_all x2, waiting for transfers between devices, exchange(): lax.all_to_all(values, GROUP, split_axis=0, concat_axis=0, tiled=True)  7.17 us
    ppermute x5, waiting for transfers between devices, row_halos(): lax.ppermute(last, GROUP, up)  5.87 us
    ppermute x5, starting transfers between devices, row_halos(): lax.ppermute(last, GROUP, up)  3.88 us
  transfers between devices with their start and end apart: 17, of which 4 were waited for; matrix products, arithmetic and copies ran while one was open for 0% of the time, Pallas kernels for 28%

profile of v3, /device:TPU:1, one launch (start us, length us, event | category | flops | bytes accessed | tf_op | source)
XLA Modules:
  0.0 135.3 jit_solution(11237484631222489519)
XLA Ops:
  5.9 1.7 %prep.1 = (f32[1536,128]{1,0:T(8,128)S(1)}, f32[1536,128]{1,0:T(8,128)S(1)}, f32[72,128]{1,0:T(8,128)S(1)}, f32[2688,128]{1,0:T(8,128)S(1)}, f32[56,128]{1,0:T(8...) custom-call(f32[2,48,2,1152]{3,2,1,0:T(2,128)S(1)} %copy-done.1, ...), custom_call_target="tpu_custom_call" | custom-call | flops 3300000000 | bytes 9000000 | tf_op jit(solution)/shard_map/prep/pallas_call | solution.py:327
  9.9 2.5 %collective-permute-start = (f32[1536,128]{1,0:T(8,128)S(1)}, f32[1536,128]{1,0:T(8,128)S(1)}, u32[]{:S(2)}, u32[]{:S(2)}) collective-permute-start(f32[1536,128]{1,0:T(8,128)S(1)} %get-tuple-element.58.high), channel_id=1, source_target_pairs={{0,2},{2,4},{4,6},{6,8},{8,10},{10,12},{12,14},{14,16},{16,18},{18... | collective-permute-start | bytes 2359304 | tf_op jit(solution)/shard_map/ppermute | solution.py:341
  12.4 8.6 %collective-permute-start.1 = (f32[1536,128]{1,0:T(8,128)S(1)}, f32[1536,128]{1,0:T(8,128)S(1)}, u32[]{:S(2)}, u32[]{:S(2)}) collective-permute-start(f32[1536,128]{1,0:T(8,128)S(1)} %get-tuple-element.59.low), channel_id=1, source_target_pairs={{2,0},{4,2},{6,4},{8,6},{10,8},{12,10},{14,12},{16,14},{18,16},{20... | collective-permute-start | bytes 2359304 | tf_op jit(solution)/shard_map/ppermute | solution.py:341
  20.9 8.7 %temp_gather.1 = f32[128,4,128]{2,1,0:T(4,128)} custom-call(f32[64,128]{1,0:T(8,128)S(1)} %get-tuple-element.56.table_ref, s32[128,512]{1,0:T(8,128)S(1)} %bitcast.10, f32[128,512]{1,0:T(8,128)S(1)} %bitcast.6), custom_call_target="tpu_custom_call" | custom-call | flops 9900000256 | bytes 27000000 | tf_op jit(solution)/shard_map/temp_gather/pallas_call | solution.py:327
  29.6 8.0 %all-to-all-start = ((f32[128,4,128]{2,1,0:T(4,128)}), f32[128,4,128]{2,1,0:T(4,128)S(1)}, u32[]{:S(2)}, u32[]{:S(2)}) async-start(f32[128,4,128]{2,1,0:T(4,128)} %temp_gather.1), calls=%async_computation | async-start | bytes 524288 | tf_op jit(solution)/shard_map/all_to_all | solution.py:350
  37.6 1.6 %collective-permute-start.2 = (f32[72,128]{1,0:T(8,128)S(1)}, f32[72,128]{1,0:T(8,128)S(1)}, u32[]{:S(2)}, u32[]{:S(2)}) collective-permute-start(f32[72,128]{1,0:T(8,128)S(1)} %get-tuple-element.60), channel_id=1, source_target_pairs={{0,1},{1,0},{2,3},{3,2},{4,5},{5,4},{6,7},{7,6},{8,9},{9,8},{10,11... | collective-permute-start | bytes 110600 | tf_op jit(solution)/shard_map/ppermute | solution.py:346
  40.1 1.3 copy-done.19
  43.5 7.2 %all-to-all-done.val_ref = f32[128,4,128]{2,1,0:T(4,128)S(1)} async-done(((f32[128,4,128]{2,1,0:T(4,128)}), f32[128,4,128]{2,1,0:T(4,128)S(1)}, u32[]{:S(2)}, u32[]{:S(2)}) %all-to-all-start) | async-done | bytes 262176 | tf_op jit(solution)/shard_map/all_to_all | solution.py:350
  51.6 7.8 %temp_scatter.1 = (f32[18,128]{1,0:T(8,128)S(1)}, bf16[128,144]{1,0:T(8,128)(2,1)S(1)}) custom-call(f32[128,4,128]{2,1,0:T(4,128)S(1)} %all-to-all-done.val_ref, s32[128,512]{1,0:T(8,128)S(1)} %bitcast.7, f32[2,18,128]{2,1,0:T(8,128)S(1)} %copy-done.30, f32[2,18,128]{2,1,0:T(8,128)S(1)} %get-tuple-element.67.coef_ref), custom_call_target="tpu_custom_call" | custom-call | flops 9900000256 | bytes 27000000 | tf_op jit(solution)/shard_map/temp_scatter/pallas_call | solution.py:327
  60.2 1.8 %atm_step.4 = (f32[1536,128]{1,0:T(8,128)}, f32[1536,128]{1,0:T(8,128)}, f32[72,128]{1,0:T(8,128)S(1)}) custom-call(f32[1536,128]{1,0:T(8,128)S(1)} %get-tuple-element.59.low, f32[1536,128]{1,0:T(8,128)S(1)} %get-tuple-element.58.high, f32[1536,128]{1,0:T(8,128)S(1)} %collective-permute-done.refs_1_.up, f32[1536,128]{1,0:T(8,128)S(1)} %collective-permute-done.1.refs_2_.down, ...), custom_call_target="tpu_custom_call" | custom-call | flops 2750000128 | bytes 7500000 | tf_op jit(solution)/shard_map/atm_step/pallas_call | solution.py:327
  63.5 8.9 %flux_gather.1 = f32[128,8,128]{2,1,0:T(8,128)} custom-call(bf16[128,144]{1,0:T(8,128)(2,1)S(1)} %get-tuple-element.75.t_ref, s32[128,512]{1,0:T(8,128)S(1)} %bitcast.8, f32[128,512]{1,0:T(8,128)S(1)} %bitcast.9), custom_call_target="tpu_custom_call" | custom-call | flops 9900000256 | bytes 27000000 | tf_op jit(solution)/shard_map/flux_gather/pallas_call | solution.py:327
  72.3 9.5 %all-to-all-start.1 = ((f32[128,8,128]{2,1,0:T(8,128)}), f32[128,8,128]{2,1,0:T(8,128)S(1)}, u32[]{:S(2)}, u32[]{:S(2)}) async-start(f32[128,8,128]{2,1,0:T(8,128)} %flux_gather.1), calls=%async_computation.1 | async-start | bytes 1048576 | tf_op jit(solution)/shard_map/all_to_all | solution.py:350
  81.8 4.0 %collective-permute-start.5 = (f32[72,128]{1,0:T(8,128)S(1)}, f32[72,128]{1,0:T(8,128)S(1)}, u32[]{:S(2)}, u32[]{:S(2)}) collective-permute-start(f32[72,128]{1,0:T(8,128)S(1)} %get-tuple-element.76), channel_id=1, source_target_pairs={{0,1},{1,0},{2,3},{3,2},{4,5},{5,4},{6,7},{7,6},{8,9},{9,8},{10,11... | collective-permute-start | bytes 110600 | tf_op jit(solution)/shard_map/ppermute | solution.py:346
  86.7 2.0 %atm_step.5 = (f32[864,128]{1,0:T(8,128)S(1)}, f32[864,128]{1,0:T(8,128)S(1)}, f32[48,128]{1,0:T(8,128)S(1)}) custom-call(f32[1536,128]{1,0:T(8,128)} %get-tuple-element.82.low, f32[1536,128]{1,0:T(8,128)} %get-tuple-element.83.high, f32[1536,128]{1,0:T(8,128)S(1)} %collective-permute-done.3.refs_1_.up, f32[1536,128]{1,0:T(8,128)S(1)} %collective-permute-done.4.refs_2_.down, ...), custom_call_target="tpu_custom_call" | custom-call | flops 2750000128 | bytes 7500000 | tf_op jit(solution)/shard_map/atm_step/pallas_call | solution.py:327
  88.7 2.0 %collective-permute-start.8 = (f32[48,128]{1,0:T(8,128)S(1)}, f32[48,128]{1,0:T(8,128)S(1)}, u32[]{:S(2)}, u32[]{:S(2)}) collective-permute-start(f32[48,128]{1,0:T(8,128)S(1)} %get-tuple-element.87), channel_id=1, source_target_pairs={{0,1},{1,0},{2,3},{3,2},{4,5},{5,4},{6,7},{7,6},{8,9},{9,8},{10,11... | collective-permute-start | bytes 73736 | tf_op jit(solution)/shard_map/ppermute | solution.py:346
  90.7 5.4 %collective-permute-start.7 = (f32[864,128]{1,0:T(8,128)S(1)}, f32[864,128]{1,0:T(8,128)S(1)}, u32[]{:S(2)}, u32[]{:S(2)}) collective-permute-start(f32[864,128]{1,0:T(8,128)S(1)} %get-tuple-element.89.low), channel_id=1, source_target_pairs={{2,0},{4,2},{6,4},{8,6},{10,8},{12,10},{14,12},{16,14},{18,16},{20... | collective-permute-start | bytes 1327112 | tf_op jit(solution)/shard_map/ppermute | solution.py:341
  96.2 2.6 %ocn_step.3 = (f32[2,24,4,1792]{3,2,1,0:T(4,128)}, f32[2,2,4,1792]{3,2,1,0:T(4,128)S(1)}) custom-call(f32[2688,128]{1,0:T(8,128)S(1)} %copy-done.17, f32[1536,128]{1,0:T(8,128)S(1)} %collective-permute-done.3.refs_1_.up, f32[1536,128]{1,0:T(8,128)S(1)} %collective-permute-done.4.refs_2_.down, f32[72,128]{1,0:T(8,128)S(1)} %collective-permute-done.5.refs_3_.edges_ref, ...), custom_call_target="tpu_custom_call" | custom-call | flops 3300000000 | bytes 9000000 | tf_op jit(solution)/shard_map/ocn_step/pallas_call | solution.py:327
  100.4 6.7 %forcing_half.1.half_ref = f32[2,32,256]{2,1,0:T(8,128)S(1)} custom-call(f32[128,8,128]{2,1,0:T(8,128)S(1)} %all-to-all-done.1.val_ref, s32[128,512]{1,0:T(8,128)S(1)} %bitcast.11), custom_call_target="tpu_custom_call" | custom-call | flops 8249999872 | bytes 22500000 | tf_op jit(solution)/shard_map/forcing_half/pallas_call | solution.py:327
  107.1 5.9 %collective-permute-done.6.up = f32[864,128]{1,0:T(8,128)} collective-permute-done((f32[864,128]{1,0:T(8,128)S(1)}, f32[864,128]{1,0:T(8,128)}, u32[]{:S(2)}, u32[]{:S(2)}) %collective-permute-start.6) | collective-permute-done | bytes 442400 | tf_op jit(solution)/shard_map/ppermute | solution.py:341
  113.0 1.7 %atm_step.6 = (f32[864,128]{1,0:T(8,128)S(1)}, f32[864,128]{1,0:T(8,128)S(1)}, f32[48,128]{1,0:T(8,128)S(1)}) custom-call(f32[864,128]{1,0:T(8,128)S(1)} %get-tuple-element.89.low, f32[864,128]{1,0:T(8,128)S(1)} %get-tuple-element.90.high, f32[864,128]{1,0:T(8,128)} %collective-permute-done.6.up, f32[864,128]{1,0:T(8,128)S(1)} %collective-permute-done.7.down, ...), custom_call_target="tpu_custom_call" | custom-call | flops 2750000128 | bytes 7500000 | tf_op jit(solution)/shard_map/atm_step/pallas_call | solution.py:327
  116.2 1.8 %collective-permute-start.11 = (f32[48,128]{1,0:T(8,128)S(1)}, f32[48,128]{1,0:T(8,128)S(1)}, u32[]{:S(2)}, u32[]{:S(2)}) collective-permute-start(f32[48,128]{1,0:T(8,128)S(1)} %get-tuple-element.100), channel_id=1, source_target_pairs={{0,1},{1,0},{2,3},{3,2},{4,5},{5,4},{6,7},{7,6},{8,9},{9,8},{10,11... | collective-permute-start | bytes 73736 | tf_op jit(solution)/shard_map/ppermute | solution.py:346
  118.1 6.7 %forcing_scatter.1 = (f32[2,56,128]{2,1,0:T(8,128)S(1)}, f32[2,56,128]{2,1,0:T(8,128)S(1)}, f32[2,14,128]{2,1,0:T(8,128)S(1)}, f32[2,14,128]{2,1,0:T(8,128)S(1)}) custom-call(f32[2,32,256]{2,1,0:T(8,128)S(1)} %forcing_half.1.half_ref, f32[128,8,128]{2,1,0:T(8,128)S(1)} %all-to-all-done.1.val_ref, s32[128,512]{1,0:T(8,128)S(1)} %bitcast.12, ...), custom_call_target="tpu_custom_call" | custom-call | flops 8249999872 | bytes 22500000 | tf_op jit(solution)/shard_map/forcing_scatter/pallas_call | solution.py:327
  124.9 6.9 %collective-permute-start.13 = (f32[2,14,128]{2,1,0:T(8,128)S(1)}, f32[2,14,128]{2,1,0:T(8,128)S(1)}, u32[]{:S(2)}, u32[]{:S(2)}) collective-permute-start(f32[2,14,128]{2,1,0:T(8,128)S(1)} %get-tuple-element.109), channel_id=1, source_target_pairs={{2,0},{4,2},{6,4},{8,6},{10,8},{12,10},{14,12},{16,14},{18,16},{20... | collective-permute-start | bytes 43016 | tf_op jit(solution)/shard_map/ppermute | solution.py:341
  132.3 2.0 %atm_step.7 = f32[2,48,2,1152]{3,2,1,0:T(2,128)} custom-call(f32[864,128]{1,0:T(8,128)S(1)} %get-tuple-element.96.low, f32[864,128]{1,0:T(8,128)S(1)} %get-tuple-element.97.high, f32[864,128]{1,0:T(8,128)S(1)} %collective-permute-done.9.up, f32[864,128]{1,0:T(8,128)S(1)} %collective-permute-done.10.down, f32[48,128]{1,0:T(8,128)S(1)} %collective-permute-done.11.edges_ref, ...), custom_call_target="tpu_custom_call" | custom-call | flops 2750000128 | bytes 7500000 | tf_op jit(solution)/shard_map/atm_step/pallas_call | solution.py:327
  (85 shorter events, 19.1 us)
Async XLA Ops:
  5.9 15.0 %copy-start.2 = (f32[1,1,128,512]{3,2,1,0:T(8,128)S(1)}, f32[1,1,128,512]{3,2,1,0:T(8,128)}, u32[]{:S(2)}) copy-start(f32[1,1,128,512]{3,2,1,0:T(8,128)} %param.19) | copy-start | bytes 786436
  5.9 15.0 %copy-start.6 = (s32[1,1,128,512]{3,2,1,0:T(8,128)S(1)}, s32[1,1,128,512]{3,2,1,0:T(8,128)}, u32[]{:S(2)}) copy-start(s32[1,1,128,512]{3,2,1,0:T(8,128)} %param.18) | copy-start | bytes 786436
  9.9 30.2 %collective-permute-start = (f32[1536,128]{1,0:T(8,128)S(1)}, f32[1536,128]{1,0:T(8,128)S(1)}, u32[]{:S(2)}, u32[]{:S(2)}) collective-permute-start(f32[1536,128]{1,0:T(8,128)S(1)} %get-tuple-element.58.high), channel_id=1, source_target_pairs={{0,2},{2,4},{4,6},{6,8},{8,10},{10,12},{12,14},{14,16},{16,18},{18... | collective-permute-start | bytes 2359304 | tf_op jit(solution)/shard_map/ppermute | solution.py:341
  12.4 27.7 %collective-permute-start.1 = (f32[1536,128]{1,0:T(8,128)S(1)}, f32[1536,128]{1,0:T(8,128)S(1)}, u32[]{:S(2)}, u32[]{:S(2)}) collective-permute-start(f32[1536,128]{1,0:T(8,128)S(1)} %get-tuple-element.59.low), channel_id=1, source_target_pairs={{2,0},{4,2},{6,4},{8,6},{10,8},{12,10},{14,12},{16,14},{18,16},{20... | collective-permute-start | bytes 2359304 | tf_op jit(solution)/shard_map/ppermute | solution.py:341
  29.6 21.0 %all-to-all-start = ((f32[128,4,128]{2,1,0:T(4,128)}), f32[128,4,128]{2,1,0:T(4,128)S(1)}, u32[]{:S(2)}, u32[]{:S(2)}) async-start(f32[128,4,128]{2,1,0:T(4,128)} %temp_gather.1), calls=%async_computation | async-start | bytes 524288 | tf_op jit(solution)/shard_map/all_to_all | solution.py:350
  37.6 2.5 %collective-permute-start.2 = (f32[72,128]{1,0:T(8,128)S(1)}, f32[72,128]{1,0:T(8,128)S(1)}, u32[]{:S(2)}, u32[]{:S(2)}) collective-permute-start(f32[72,128]{1,0:T(8,128)S(1)} %get-tuple-element.60), channel_id=1, source_target_pairs={{0,1},{1,0},{2,3},{3,2},{4,5},{5,4},{6,7},{7,6},{8,9},{9,8},{10,11... | collective-permute-start | bytes 110600 | tf_op jit(solution)/shard_map/ppermute | solution.py:346
  43.5 16.0 %copy-start.27 = (f32[24,128]{1,0:T(8,128)}, f32[24,128]{1,0:T(8,128)S(1)}, u32[]{:S(2)}) copy-start(f32[24,128]{1,0:T(8,128)S(1)} %get-tuple-element.72.rest_1_) | copy-start | bytes 36868
  62.0 24.7 %collective-permute-start.4 = (f32[1536,128]{1,0:T(8,128)}, f32[1536,128]{1,0:T(8,128)S(1)}, u32[]{:S(2)}, u32[]{:S(2)}) collective-permute-start(f32[1536,128]{1,0:T(8,128)} %get-tuple-element.82.low), channel_id=1, source_target_pairs={{2,0},{4,2},{6,4},{8,6},{10,8},{12,10},{14,12},{16,14},{18,16},{20... | collective-permute-start | bytes 2359304 | tf_op jit(solution)/shard_map/ppermute | solution.py:341
  62.5 24.1 %collective-permute-start.3 = (f32[1536,128]{1,0:T(8,128)}, f32[1536,128]{1,0:T(8,128)S(1)}, u32[]{:S(2)}, u32[]{:S(2)}) collective-permute-start(f32[1536,128]{1,0:T(8,128)} %get-tuple-element.83.high), channel_id=1, source_target_pairs={{0,2},{2,4},{4,6},{6,8},{8,10},{10,12},{12,14},{14,16},{16,18},{18... | collective-permute-start | bytes 2359304 | tf_op jit(solution)/shard_map/ppermute | solution.py:341
  63.5 23.2 %copy-start.22 = (f32[48,128]{1,0:T(8,128)S(1)}, f32[48,128]{1,0:T(8,128)}, u32[]{:S(2)}) copy-start(f32[48,128]{1,0:T(8,128)} %copy-done.20) | copy-start | bytes 73732
  63.5 23.2 %copy-start.25 = (f32[18,128]{1,0:T(8,128)S(1)}, f32[18,128]{1,0:T(8,128)}, u32[]{:S(2)}) copy-start(f32[18,128]{1,0:T(8,128)} %copy-done.24) | copy-start | bytes 27652
  72.3 27.1 %all-to-all-start.1 = ((f32[128,8,128]{2,1,0:T(8,128)}), f32[128,8,128]{2,1,0:T(8,128)S(1)}, u32[]{:S(2)}, u32[]{:S(2)}) async-start(f32[128,8,128]{2,1,0:T(8,128)} %flux_gather.1), calls=%async_computation.1 | async-start | bytes 1048576 | tf_op jit(solution)/shard_map/all_to_all | solution.py:350
  81.8 14.4 %copy-start.17 = (f32[2688,128]{1,0:T(8,128)S(1)}, f32[2688,128]{1,0:T(8,128)}, u32[]{:S(2)}) copy-start(f32[2688,128]{1,0:T(8,128)} %copy-done.15) | copy-start | bytes 4128772
  81.8 4.8 %collective-permute-start.5 = (f32[72,128]{1,0:T(8,128)S(1)}, f32[72,128]{1,0:T(8,128)S(1)}, u32[]{:S(2)}, u32[]{:S(2)}) collective-permute-start(f32[72,128]{1,0:T(8,128)S(1)} %get-tuple-element.76), channel_id=1, source_target_pairs={{0,1},{1,0},{2,3},{3,2},{4,5},{5,4},{6,7},{7,6},{8,9},{9,8},{10,11... | collective-permute-start | bytes 110600 | tf_op jit(solution)/shard_map/ppermute | solution.py:346
  88.7 18.4 %collective-permute-start.8 = (f32[48,128]{1,0:T(8,128)S(1)}, f32[48,128]{1,0:T(8,128)S(1)}, u32[]{:S(2)}, u32[]{:S(2)}) collective-permute-start(f32[48,128]{1,0:T(8,128)S(1)} %get-tuple-element.87), channel_id=1, source_target_pairs={{0,1},{1,0},{2,3},{3,2},{4,5},{5,4},{6,7},{7,6},{8,9},{9,8},{10,11... | collective-permute-start | bytes 73736 | tf_op jit(solution)/shard_map/ppermute | solution.py:346
  90.7 16.4 %collective-permute-start.7 = (f32[864,128]{1,0:T(8,128)S(1)}, f32[864,128]{1,0:T(8,128)S(1)}, u32[]{:S(2)}, u32[]{:S(2)}) collective-permute-start(f32[864,128]{1,0:T(8,128)S(1)} %get-tuple-element.89.low), channel_id=1, source_target_pairs={{2,0},{4,2},{6,4},{8,6},{10,8},{12,10},{14,12},{16,14},{18,16},{20... | collective-permute-start | bytes 1327112 | tf_op jit(solution)/shard_map/ppermute | solution.py:341
  96.2 16.8 %collective-permute-start.6 = (f32[864,128]{1,0:T(8,128)S(1)}, f32[864,128]{1,0:T(8,128)}, u32[]{:S(2)}, u32[]{:S(2)}) collective-permute-start(f32[864,128]{1,0:T(8,128)S(1)} %get-tuple-element.90.high), channel_id=1, source_target_pairs={{0,2},{2,4},{4,6},{6,8},{8,10},{10,12},{12,14},{14,16},{16,18},{18... | collective-permute-start | bytes 1327112 | tf_op jit(solution)/shard_map/ppermute | solution.py:341
  100.4 12.6 %copy-start.26 = (f32[18,128]{1,0:T(8,128)S(1)}, f32[18,128]{1,0:T(8,128)}, u32[]{:S(2)}) copy-start(f32[18,128]{1,0:T(8,128)} %copy-done.24) | copy-start | bytes 27652
  114.7 17.6 %collective-permute-start.10 = (f32[864,128]{1,0:T(8,128)S(1)}, f32[864,128]{1,0:T(8,128)S(1)}, u32[]{:S(2)}, u32[]{:S(2)}) collective-permute-start(f32[864,128]{1,0:T(8,128)S(1)} %get-tuple-element.96.low), channel_id=1, source_target_pairs={{2,0},{4,2},{6,4},{8,6},{10,8},{12,10},{14,12},{16,14},{18,16},{20... | collective-permute-start | bytes 1327112 | tf_op jit(solution)/shard_map/ppermute | solution.py:341
  115.8 16.5 %collective-permute-start.9 = (f32[864,128]{1,0:T(8,128)S(1)}, f32[864,128]{1,0:T(8,128)S(1)}, u32[]{:S(2)}, u32[]{:S(2)}) collective-permute-start(f32[864,128]{1,0:T(8,128)S(1)} %get-tuple-element.97.high), channel_id=1, source_target_pairs={{0,2},{2,4},{4,6},{6,8},{8,10},{10,12},{12,14},{14,16},{16,18},{18... | collective-permute-start | bytes 1327112 | tf_op jit(solution)/shard_map/ppermute | solution.py:341
  116.2 15.5 %collective-permute-start.11 = (f32[48,128]{1,0:T(8,128)S(1)}, f32[48,128]{1,0:T(8,128)S(1)}, u32[]{:S(2)}, u32[]{:S(2)}) collective-permute-start(f32[48,128]{1,0:T(8,128)S(1)} %get-tuple-element.100), channel_id=1, source_target_pairs={{0,1},{1,0},{2,3},{3,2},{4,5},{5,4},{6,7},{7,6},{8,9},{9,8},{10,11... | collective-permute-start | bytes 73736 | tf_op jit(solution)/shard_map/ppermute | solution.py:346
  124.8 9.5 %collective-permute-start.12 = (f32[2,14,128]{2,1,0:T(8,128)S(1)}, f32[2,14,128]{2,1,0:T(8,128)S(1)}, u32[]{:S(2)}, u32[]{:S(2)}) collective-permute-start(f32[2,14,128]{2,1,0:T(8,128)S(1)} %get-tuple-element.108), channel_id=1, source_target_pairs={{0,2},{2,4},{4,6},{6,8},{8,10},{10,12},{12,14},{14,16},{16,18},{18... | collective-permute-start | bytes 43016 | tf_op jit(solution)/shard_map/ppermute | solution.py:341
  124.9 9.4 %collective-permute-start.13 = (f32[2,14,128]{2,1,0:T(8,128)S(1)}, f32[2,14,128]{2,1,0:T(8,128)S(1)}, u32[]{:S(2)}, u32[]{:S(2)}) collective-permute-start(f32[2,14,128]{2,1,0:T(8,128)S(1)} %get-tuple-element.109), channel_id=1, source_target_pairs={{2,0},{4,2},{6,4},{8,6},{10,8},{12,10},{14,12},{16,14},{18,16},{20... | collective-permute-start | bytes 43016 | tf_op jit(solution)/shard_map/ppermute | solution.py:341
  131.7 2.6 %collective-permute-start.14 = (f32[2,56,128]{2,1,0:T(8,128)S(1)}, f32[2,56,128]{2,1,0:T(8,128)S(1)}, u32[]{:S(2)}, u32[]{:S(2)}) collective-permute-start(f32[2,56,128]{2,1,0:T(8,128)S(1)} %get-tuple-element.107.gain_ref), channel_id=1, source_target_pairs={{0,1},{1,0},{2,3},{3,2},{4,5},{5,4},{6,7},{7,6},{8,9},{9,8},{10,11... | collective-permute-start | bytes 172040 | tf_op jit(solution)/shard_map/ppermute | solution.py:346
  (24 other events, 72.8 us)

commit v4 on v3

--- a/solution.py
+++ b/solution.py
@@ -64,12 +64,19 @@
     lax.fori_loop(0, index_ref.shape[0] // 8, group, 0)
 
 
-def scatter_loop(val_ref, index_ref, H, L, F, start=0, stop=None):
+def scatter_loop(val_ref, index, H, L, F, start=0, stop=None):
+    index_hbm, index_ref, sems = index
+    stop = stop or index_ref.shape[0]
+    cuts = (start, start + 16, stop)
+    rows = [pl.ds(a, b - a) for a, b in zip(cuts, cuts[1:])]
+    copies = [pltpu.make_async_copy(index_hbm.at[r], index_ref.at[r], sems.at[i]) for i, r in enumerate(rows)]
+    for copy in copies:
+        copy.start()
     shift = L.bit_length() - 1
     def group(g, acc):
         base = pl.multiple_of(g * 8, 8)
-        index = index_ref[pl.ds(base, 8), :]
-        hi, lo = index >> shift, index & (L - 1)
+        place = index_ref[pl.ds(base, 8), :]
+        hi, lo = place >> shift, place & (L - 1)
         for r in range(8):
             masks = hits(hi[r : r + 1], H)
             a = []
@@ -78,10 +85,13 @@
                 for p in parts_of(jnp.broadcast_to(v, (16, v.shape[1]))):
                     a += [jnp.where(m, p, jnp.zeros_like(p)) for m in masks]
             a = jnp.concatenate(a, axis=0)
-            acc = acc + lax.dot_general(a, one_hot(lo[r : r + 1], L), (((1,), (1,)), ((), ())), preferred_element_type=F32)
+            acc = acc + lax.dot_general(one_hot(lo[r : r + 1], L), a, (((1,), (1,)), ((), ())), preferred_element_type=F32)
         return acc
-    stop = stop or index_ref.shape[0]
-    acc = lax.fori_loop(start // 8, stop // 8, group, jnp.zeros((F * SPLITS * H, L), F32))
+    acc = jnp.zeros((L, F * SPLITS * H), F32)
+    for copy, a, b in zip(copies, cuts, cuts[1:]):
+        copy.wait()
+        acc = lax.fori_loop(a // 8, b // 8, group, acc)
+    acc = acc.T
     return [sum(acc[(f * SPLITS + i) * H : (f * SPLITS + i + 1) * H] for i in range(SPLITS)) for f in range(F)]
 
 
@@ -95,8 +105,8 @@
 ASIZE, OSIZE = 2 * AT * AL, 2 * OT * OL
 
 
-def flux_kernel(val_ref, col_ref, state_ref, coef_ref, temp_ref, t_ref, flux_ref):
-    temp, = scatter_loop(val_ref, col_ref, 32, 128, 1)
+def flux_kernel(val_ref, col_ref, state_ref, coef_ref, temp_ref, t_ref, flux_ref, *store):
+    temp, = scatter_loop(val_ref, (col_ref, *store), 32, 128, 1)
     temp = temp[: AR * AT]
     temp_ref[...] = temp
     flux_ref[...] = jnp.zeros_like(flux_ref)
@@ -163,9 +173,15 @@
     return jnp.broadcast_to(edges[:, i : i + 1], edges.shape)
 
 
-def prep_kernel(atm_ref, ocn_ref, mask_ref, coef_ref, adiff_ref, odiff_ref, low, high, edges, ocean, frac, table, surface, coef, adiff, odiff):
+def prep_kernel(atm_hbm, ocn_hbm, mask_hbm, coef_hbm, adiff_ref, odiff_ref, low, high, edges, ocean, frac, table, surface, coef, adiff, odiff, atm_ref, ocn_ref, mask_ref, coef_ref, sems):
+    pairs = ((atm_hbm, atm_ref), (coef_hbm, coef_ref), (mask_hbm, mask_ref), (ocn_hbm, ocn_ref))
+    copies = [pltpu.make_async_copy(*pair, sems.at[i]) for i, pair in enumerate(pairs)]
+    for copy in copies:
+        copy.start()
     adiff[...] = jnp.broadcast_to(adiff_ref[...], (LANES, AL)).T
     odiff[...] = jnp.broadcast_to(odiff_ref[...], (LANES, OL)).T
+    copies[0].wait()
+    copies[1].wait()
     ends = []
     for r, out in enumerate((low, high)):
         for f in range(2):
@@ -181,6 +197,8 @@
             ends.append(pair)
     edges[:AL, :] = edges_of(ends)
     table[...] = jnp.zeros_like(table)
+    copies[2].wait()
+    copies[3].wait()
     block, count = lax.axis_index(GROUP), lax.axis_size(GROUP)
     ends = []
     for r in range(OR):
@@ -266,13 +284,13 @@
         out_more[...] = edges_of(ends)
 
 
-def half_kernel(val_ref, cell_ref, out_ref):
-    for f, total in enumerate(scatter_loop(val_ref, cell_ref, 32, 256, 2, stop=val_ref.shape[0] // 2)):
+def half_kernel(val_ref, cell_ref, out_ref, *store):
+    for f, total in enumerate(scatter_loop(val_ref, (cell_ref, *store), 32, 256, 2, stop=val_ref.shape[0] // 2)):
         out_ref[f] = total
 
 
-def forcing_kernel(half_ref, val_ref, cell_ref, frac_ref, out_ref, gain_ref, low, high):
-    for f, total in enumerate(scatter_loop(val_ref, cell_ref, 32, 256, 2, start=val_ref.shape[0] // 2)):
+def forcing_kernel(half_ref, val_ref, cell_ref, frac_ref, out_ref, gain_ref, low, high, *store):
+    for f, total in enumerate(scatter_loop(val_ref, (cell_ref, *store), 32, 256, 2, start=val_ref.shape[0] // 2)):
         total = (HEAT_GAIN, -SALT_GAIN)[f] * (half_ref[f] + total)[: OR * OT // 2]
         for side in range(2):
             out_ref[f, pl.ds(side, OR * OT // 2, stride=2), :] = total[:, side * LANES : (side + 1) * LANES]
@@ -319,17 +337,18 @@
 
 VM = pl.BlockSpec(memory_space=pltpu.VMEM)
 ANY = pl.BlockSpec(memory_space=pl.ANY)
-
-
-def call(kernel, name, micros, out_shape, *args, scratch=(), hbm=(), **more):
-    args = [x if i in hbm else pltpu.with_memory_space_constraint(x, pltpu.VMEM) for i, x in enumerate(args)]
+HBM = pl.BlockSpec(memory_space=pltpu.HBM)
+
+
+def call(kernel, name, micros, out_shape, *args, scratch=(), cold=(), far=(), **more):
+    args = [x if i in cold else pltpu.with_memory_space_constraint(x, pltpu.HBM if i in far else pltpu.VMEM) for i, x in enumerate(args)]
     specs = {"in_specs": [VM] * len(args), "out_specs": jax.tree.map(lambda _: VM, out_shape), **more}
     return pl.pallas_call(
         kernel,
         out_shape=out_shape,
         scratch_shapes=list(scratch),
         cost_estimate=pl.CostEstimate(flops=int(micros * 1.1e9), bytes_accessed=int(micros * 3e6), transcendentals=0),
-        compiler_params=pltpu.CompilerParams(vmem_limit_bytes=20 << 20),
+        compiler_params=pltpu.CompilerParams(vmem_limit_bytes=8 << 20),
         name=name,
         **specs,
     )(*args)
@@ -363,7 +382,8 @@
     o2a_weights,
 ):
     group_size = lax.axis_size(GROUP)
-    shape = lambda *s: pltpu.VMEM(s, F32)
+    shape, free = lambda *s: pltpu.VMEM(s, F32), lambda *s: pltpu.HBM(s, F32)
+    store = [pltpu.VMEM(atm_pair_cols.shape[2:], jnp.int32), pltpu.SemaphoreType.DMA((2,))]
     cols, cells = atm_pair_cols[0, 0], ocn_pair_cells[0, 0]
     both = shape(ASIZE + OSIZE, LANES)
 
@@ -371,46 +391,49 @@
         prep_kernel,
         "prep",
         3,
-        (both, both, shape(AL + OL, LANES), shape(OR * OSIZE, LANES), shape(OR * OT, LANES), shape(64, LANES), shape(2, AR * AT, LANES), shape(2, AR * AT, LANES), shape(AL, LANES), shape(OL, LANES)),
+        (both, both, shape(AL + OL, LANES), free(OR * OSIZE, LANES), free(OR * OT, LANES), shape(64, LANES), *[free(*s) for s in ((2, AR * AT, LANES), (2, AR * AT, LANES), (AL, LANES), (OL, LANES))]),
         atm_state,
         ocn_state,
         sea_mask,
         atm_surface_coef,
         atm_diffusion[None],
         ocn_diffusion[None],
+        far=range(6),
+        in_specs=[HBM] * 4 + [VM] * 2,
+        scratch=[pltpu.VMEM(x.shape, x.dtype) for x in (atm_state, ocn_state, sea_mask, atm_surface_coef)] + [pltpu.SemaphoreType.DMA((4,))],
     )
     up, down = row_halos(low, high)
     beside = partner(edges)
 
-    outgoing = call(temp_kernel, "temp_gather", 9, shape(group_size, 4, LANES), table, cells, o2a_weights[0, 0], scratch=[pltpu.VMEM((128, SPLITS * 64), BF16)])
+    outgoing = call(temp_kernel, "temp_gather", 9, shape(group_size, 4, LANES), table, cells, o2a_weights[0, 0], cold=(1, 2), scratch=[pltpu.VMEM((128, SPLITS * 64), BF16)])
     incoming = exchange(outgoing)
     ocn_step = lambda *refs: ocn_kernel(False, *refs)
-    ocean, ocn_edges = call(ocn_step, "ocn_step", 3, (shape(OR * OSIZE, LANES), shape(OL, LANES)), ocean, up, down, beside, ocn_diff, frac)
+    ocean, ocn_edges = call(ocn_step, "ocn_step", 3, (shape(OR * OSIZE, LANES), free(OL, LANES)), ocean, up, down, beside, ocn_diff, frac, cold=(4, 5))
     incoming, ocean, ocn_edges = lax.optimization_barrier((incoming, ocean, ocn_edges))
 
-    temp, flux_table = call(flux_kernel, "temp_scatter", 9, (shape(AR * AT, LANES), pltpu.VMEM((128, SPLITS * 48), BF16)), incoming, cols, surface, coef, scratch=[pltpu.VMEM((24, LANES), F32)])
+    temp, flux_table = call(flux_kernel, "temp_scatter", 9, (free(AR * AT, LANES), pltpu.VMEM((128, SPLITS * 48), BF16)), incoming, cols, surface, coef, far=(1,), cold=(2, 3), in_specs=[VM, HBM, VM, VM], scratch=[pltpu.VMEM((24, LANES), F32), *store])
 
     def atm_step(low, high, up, down, beside, *more, outs=None):
         rows = shape(ASIZE + (OSIZE if more else 0), LANES)
         outs = outs or (rows, rows, shape(AL + (OL if more else 0), LANES))
-        return call(atm_kernel, "atm_step", 2.5, outs, low, high, up, down, beside, atm_diff, coef, temp, *more)
+        return call(atm_kernel, "atm_step", 2.5, outs, low, high, up, down, beside, atm_diff, coef, temp, *more, cold=(5, 6, 7, 9))
 
     low, high, edges = atm_step(low, high, up, down, beside, ocean, ocn_edges)
     up, down = row_halos(low, high)
     beside = partner(edges)
     flux_table, low, high = lax.optimization_barrier((flux_table, low, high))
 
-    outgoing = call(send_kernel, "flux_gather", 9, shape(group_size, 8, LANES), flux_table, cols, a2o_weights[0, 0])
+    outgoing = call(send_kernel, "flux_gather", 9, shape(group_size, 8, LANES), flux_table, cols, a2o_weights[0, 0], cold=(1, 2))
     incoming = exchange(outgoing)
     outgoing, up, down, beside = lax.optimization_barrier((outgoing, up, down, beside))
     low, high, edges = atm_step(low, high, up, down, beside)
     ocn_last_step = lambda *refs: ocn_kernel(True, *refs)
-    ocean, top = call(ocn_last_step, "ocn_step", 3, (jax.ShapeDtypeStruct(ocn_state.shape, F32), shape(2, 2, OR, OT * LANES)), ocean, up, down, beside, ocn_diff, frac)
+    ocean, top = call(ocn_last_step, "ocn_step", 3, (jax.ShapeDtypeStruct(ocn_state.shape, F32), free(2, 2, OR, OT * LANES)), ocean, up, down, beside, ocn_diff, frac, cold=(4, 5))
     up, down = row_halos(low, high)
     beside = partner(edges)
     incoming, ocean, top, low, high = lax.optimization_barrier((incoming, ocean, top, low, high))
 
-    half = call(half_kernel, "forcing_half", 7.5, shape(2, 32, 256), incoming, cells)
+    half = call(half_kernel, "forcing_half", 7.5, shape(2, 32, 256), incoming, cells, far=(1,), in_specs=[VM, HBM], scratch=store)
     half, up, down, beside = lax.optimization_barrier((half, up, down, beside))
     low, high, edges = atm_step(low, high, up, down, beside)
     up, down = row_halos(low, high)
@@ -418,7 +441,7 @@
     half, low, high = lax.optimization_barrier((half, low, high))
 
     every = shape(2, OR * OT, LANES)
-    forcing, gained, first, last = call(forcing_kernel, "forcing_scatter", 7.5, (every, every, shape(2, OT, LANES), shape(2, OT, LANES)), half, incoming, cells, frac)
+    forcing, gained, first, last = call(forcing_kernel, "forcing_scatter", 7.5, (every, every, shape(2, OT, LANES), shape(2, OT, LANES)), half, incoming, cells, frac, far=(2,), cold=(3,), in_specs=[VM, VM, HBM, VM], scratch=store)
     above, below = row_halos(first, last)
     side = partner(gained)
     forcing, up, down, beside = lax.optimization_barrier((forcing, up, down, beside))
@@ -443,7 +466,7 @@
         out_specs=ANY,
         scratch=[pltpu.VMEM((6 * OT, LANES), F32), line, line, pltpu.VMEM((2, 2, OR, OT * LANES), F32), pltpu.SemaphoreType.DMA],
         input_output_aliases={0: 0},
-        hbm=(0,),
+        cold=(0, 1, 7, 8),
     )
     return atm_next, ocean_next
 

time: 136 us -> 131 us (0.963)
  local copies, waits for them, and re-layouts: 13.3 us -> 3.18 us
  Pallas kernels: 52.4 us -> 57.2 us
    unnamed x62 -> x40, local copies, waits for them, and re-layouts: 13.3 us -> 3.18 us
    pallas_call x13, Pallas kernels: 52.4 us -> 57.2 us  [call(): pl.pallas_call(kernel, out_shape=out_shape, scratch_shapes=list(scratch),...]
  transfers between devices with their start and end apart: 17 -> 17, of which waited for: 4 -> 4; matrix products, arithmetic and copies ran while one was open for 0% -> 0% of each run, Pallas kernels for 28% -> 30%
where the time goes in v4:
time: 131 us
  Pallas kernels  57.2 us (44%)
  starting transfers between devices  53.9 us (41%)
  waiting for transfers between devices  15.5 us (12%)
  local copies, waits for them, and re-layouts  3.18 us (2%)
    pallas_call x13, Pallas kernels, call(): pl.pallas_call(kernel, out_shape=out_shape, scratch_shapes=list(scratch),...  57.2 us
    ppermute x5, starting transfers between devices, row_halos(): lax.ppermute(first, GROUP, [(b, a) for a, b in up])  21.8 us
    all_to_all x2, starting transfers between devices, exchange(): lax.all_to_all(values, GROUP, split_axis=0, concat_axis=0, tiled=True)  17.3 us
    ppermute x5, starting transfers between devices, partner(): lax.ppermute(edges, 'lev', [(i, (i + 1) % count) for i in range(count)])  9.98 us
    ppermute x5, waiting for transfers between devices, row_halos(): lax.ppermute(last, GROUP, up)  7.2 us
    all_to_all x2, waiting for transfers between devices, exchange(): lax.all_to_all(values, GROUP, split_axis=0, concat_axis=0, tiled=True)  6.56 us
    ppermute x5, starting transfers between devices, row_halos(): lax.ppermute(last, GROUP, up)  4.81 us
    unnamed x40, local copies, waits for them, and re-layouts  3.18 us
  transfers between devices with their start and end apart: 17, of which 4 were waited for; matrix products, arithmetic and copies ran while one was open for 0% of the time, Pallas kernels for 30%

profile of v4, /device:TPU:1, one launch (start us, length us, event | category | flops | bytes accessed | tf_op | source)
XLA Modules:
  0.0 130.8 jit_solution(3334442086711190127)
XLA Ops:
  0.7 4.7 %prep.1 = (f32[1536,128]{1,0:T(8,128)S(1)}, f32[1536,128]{1,0:T(8,128)S(1)}, f32[72,128]{1,0:T(8,128)S(1)}, f32[2688,128]{1,0:T(8,128)}, f32[56,128]{1,0:T(8,128...) custom-call(f32[2,48,2,1152]{3,2,1,0:T(2,128)} %atm_hbm.1, ...), custom_call_target="tpu_custom_call" | custom-call | flops 3300000000 | bytes 9000000 | tf_op jit(solution)/shard_map/prep/pallas_call | solution.py:346
  5.3 2.5 %collective-permute-start = (f32[1536,128]{1,0:T(8,128)S(1)}, f32[1536,128]{1,0:T(8,128)S(1)}, u32[]{:S(2)}, u32[]{:S(2)}) collective-permute-start(f32[1536,128]{1,0:T(8,128)S(1)} %get-tuple-element.58.high), channel_id=1, source_target_pairs={{0,2},{2,4},{4,6},{6,8},{8,10},{10,12},{12,14},{14,16},{16,18},{18... | collective-permute-start | bytes 2359304 | tf_op jit(solution)/shard_map/ppermute | solution.py:360
  7.9 8.7 %collective-permute-start.1 = (f32[1536,128]{1,0:T(8,128)S(1)}, f32[1536,128]{1,0:T(8,128)S(1)}, u32[]{:S(2)}, u32[]{:S(2)}) collective-permute-start(f32[1536,128]{1,0:T(8,128)S(1)} %get-tuple-element.59.low), channel_id=1, source_target_pairs={{2,0},{4,2},{6,4},{8,6},{10,8},{12,10},{14,12},{16,14},{18,16},{20... | collective-permute-start | bytes 2359304 | tf_op jit(solution)/shard_map/ppermute | solution.py:360
  16.6 8.7 %temp_gather.1 = f32[128,4,128]{2,1,0:T(4,128)} custom-call(f32[64,128]{1,0:T(8,128)S(1)} %get-tuple-element.56.table_ref, s32[128,512]{1,0:T(8,128)S(1)} %bitcast.12, f32[128,512]{1,0:T(8,128)S(1)} %bitcast.6), custom_call_target="tpu_custom_call" | custom-call | flops 9900000256 | bytes 27000000 | tf_op jit(solution)/shard_map/temp_gather/pallas_call | solution.py:346
  25.2 7.9 %all-to-all-start = ((f32[128,4,128]{2,1,0:T(4,128)}), f32[128,4,128]{2,1,0:T(4,128)S(1)}, u32[]{:S(2)}, u32[]{:S(2)}) async-start(f32[128,4,128]{2,1,0:T(4,128)} %temp_gather.1), calls=%async_computation | async-start | bytes 524288 | tf_op jit(solution)/shard_map/all_to_all | solution.py:369
  33.1 1.6 %collective-permute-start.2 = (f32[72,128]{1,0:T(8,128)S(1)}, f32[72,128]{1,0:T(8,128)S(1)}, u32[]{:S(2)}, u32[]{:S(2)}) collective-permute-start(f32[72,128]{1,0:T(8,128)S(1)} %get-tuple-element.60), channel_id=1, source_target_pairs={{0,1},{1,0},{2,3},{3,2},{4,5},{5,4},{6,7},{7,6},{8,9},{9,8},{10,11... | collective-permute-start | bytes 110600 | tf_op jit(solution)/shard_map/ppermute | solution.py:365
  37.0 1.5 %ocn_step.2 = (f32[2688,128]{1,0:T(8,128)S(1)}, f32[24,128]{1,0:T(8,128)}) custom-call(f32[2688,128]{1,0:T(8,128)S(1)} %copy-done.9, f32[1536,128]{1,0:T(8,128)S(1)} %collective-permute-done.refs_1_.up, f32[1536,128]{1,0:T(8,128)S(1)} %collective-permute-done.1.refs_2_.down, f32[72,128]{1,0:T(8,128)S(1)} %collective-permute-done.2.refs_3_.edges_ref, ...), custom_call_target="tpu_custom_call" | custom-call | flops 3300000000 | bytes 9000000 | tf_op jit(solution)/shard_map/ocn_step/pallas_call | solution.py:346
  39.6 6.6 %all-to-all-done.val_ref = f32[128,4,128]{2,1,0:T(4,128)S(1)} async-done(((f32[128,4,128]{2,1,0:T(4,128)}), f32[128,4,128]{2,1,0:T(4,128)S(1)}, u32[]{:S(2)}, u32[]{:S(2)}) %all-to-all-start) | async-done | bytes 262176 | tf_op jit(solution)/shard_map/all_to_all | solution.py:369
  46.2 8.5 %temp_scatter.1 = (f32[18,128]{1,0:T(8,128)}, bf16[128,144]{1,0:T(8,128)(2,1)S(1)}) custom-call(f32[128,4,128]{2,1,0:T(4,128)S(1)} %all-to-all-done.val_ref, s32[128,512]{1,0:T(8,128)} %bitcast.7, f32[2,18,128]{2,1,0:T(8,128)S(1)} %copy-done.19, f32[2,18,128]{2,1,0:T(8,128)S(1)} %copy-done.11), custom_call_target="tpu_custom_call" | custom-call | flops 9900000256 | bytes 27000000 | tf_op jit(solution)/shard_map/temp_scatter/pallas_call | solution.py:346
  55.4 1.8 %atm_step.4 = (f32[1536,128]{1,0:T(8,128)}, f32[1536,128]{1,0:T(8,128)}, f32[72,128]{1,0:T(8,128)S(1)}) custom-call(f32[1536,128]{1,0:T(8,128)S(1)} %get-tuple-element.59.low, f32[1536,128]{1,0:T(8,128)S(1)} %get-tuple-element.58.high, f32[1536,128]{1,0:T(8,128)S(1)} %collective-permute-done.refs_1_.up, f32[1536,128]{1,0:T(8,128)S(1)} %collective-permute-done.1.refs_2_.down, ...), custom_call_target="tpu_custom_call" | custom-call | flops 2750000128 | bytes 7500000 | tf_op jit(solution)/shard_map/atm_step/pallas_call | solution.py:346
  58.7 9.0 %flux_gather.1 = f32[128,8,128]{2,1,0:T(8,128)} custom-call(bf16[128,144]{1,0:T(8,128)(2,1)S(1)} %get-tuple-element.75.t_ref, s32[128,512]{1,0:T(8,128)S(1)} %bitcast.8, f32[128,512]{1,0:T(8,128)S(1)} %bitcast.9), custom_call_target="tpu_custom_call" | custom-call | flops 9900000256 | bytes 27000000 | tf_op jit(solution)/shard_map/flux_gather/pallas_call | solution.py:346
  67.6 9.4 %all-to-all-start.1 = ((f32[128,8,128]{2,1,0:T(8,128)}), f32[128,8,128]{2,1,0:T(8,128)S(1)}, u32[]{:S(2)}, u32[]{:S(2)}) async-start(f32[128,8,128]{2,1,0:T(8,128)} %flux_gather.1), calls=%async_computation.1 | async-start | bytes 1048576 | tf_op jit(solution)/shard_map/all_to_all | solution.py:369
  77.1 4.0 %collective-permute-start.5 = (f32[72,128]{1,0:T(8,128)S(1)}, f32[72,128]{1,0:T(8,128)S(1)}, u32[]{:S(2)}, u32[]{:S(2)}) collective-permute-start(f32[72,128]{1,0:T(8,128)S(1)} %get-tuple-element.76), channel_id=1, source_target_pairs={{0,1},{1,0},{2,3},{3,2},{4,5},{5,4},{6,7},{7,6},{8,9},{9,8},{10,11... | collective-permute-start | bytes 110600 | tf_op jit(solution)/shard_map/ppermute | solution.py:365
  81.9 2.0 %atm_step.5 = (f32[864,128]{1,0:T(8,128)S(1)}, f32[864,128]{1,0:T(8,128)S(1)}, f32[48,128]{1,0:T(8,128)S(1)}) custom-call(f32[1536,128]{1,0:T(8,128)} %get-tuple-element.82.low, f32[1536,128]{1,0:T(8,128)} %get-tuple-element.83.high, f32[1536,128]{1,0:T(8,128)S(1)} %collective-permute-done.3.refs_1_.up, f32[1536,128]{1,0:T(8,128)S(1)} %collective-permute-done.4.refs_2_.down, ...), custom_call_target="tpu_custom_call" | custom-call | flops 2750000128 | bytes 7500000 | tf_op jit(solution)/shard_map/atm_step/pallas_call | solution.py:346
  83.9 2.0 %collective-permute-start.8 = (f32[48,128]{1,0:T(8,128)S(1)}, f32[48,128]{1,0:T(8,128)S(1)}, u32[]{:S(2)}, u32[]{:S(2)}) collective-permute-start(f32[48,128]{1,0:T(8,128)S(1)} %get-tuple-element.87), channel_id=1, source_target_pairs={{0,1},{1,0},{2,3},{3,2},{4,5},{5,4},{6,7},{7,6},{8,9},{9,8},{10,11... | collective-permute-start | bytes 73736 | tf_op jit(solution)/shard_map/ppermute | solution.py:365
  85.9 5.4 %collective-permute-start.7 = (f32[864,128]{1,0:T(8,128)S(1)}, f32[864,128]{1,0:T(8,128)S(1)}, u32[]{:S(2)}, u32[]{:S(2)}) collective-permute-start(f32[864,128]{1,0:T(8,128)S(1)} %get-tuple-element.89.low), channel_id=1, source_target_pairs={{2,0},{4,2},{6,4},{8,6},{10,8},{12,10},{14,12},{16,14},{18,16},{20... | collective-permute-start | bytes 1327112 | tf_op jit(solution)/shard_map/ppermute | solution.py:360
  91.4 2.7 %ocn_step.3 = (f32[2,24,4,1792]{3,2,1,0:T(4,128)}, f32[2,2,4,1792]{3,2,1,0:T(4,128)}) custom-call(f32[2688,128]{1,0:T(8,128)S(1)} %copy-done.7, f32[1536,128]{1,0:T(8,128)S(1)} %collective-permute-done.3.refs_1_.up, f32[1536,128]{1,0:T(8,128)S(1)} %collective-permute-done.4.refs_2_.down, f32[72,128]{1,0:T(8,128)S(1)} %collective-permute-done.5.refs_3_.edges_ref, ...), custom_call_target="tpu_custom_call" | custom-call | flops 3300000000 | bytes 9000000 | tf_op jit(solution)/shard_map/ocn_step/pallas_call | solution.py:346
  94.1 6.9 %forcing_half.1.half_ref = f32[2,32,256]{2,1,0:T(8,128)S(1)} custom-call(f32[128,8,128]{2,1,0:T(8,128)S(1)} %all-to-all-done.1.val_ref, s32[128,512]{1,0:T(8,128)} %bitcast.10), custom_call_target="tpu_custom_call" | custom-call | flops 8249999872 | bytes 22500000 | tf_op jit(solution)/shard_map/forcing_half/pallas_call | solution.py:346
  101.0 7.2 %collective-permute-done.6.up = f32[864,128]{1,0:T(8,128)} collective-permute-done((f32[864,128]{1,0:T(8,128)S(1)}, f32[864,128]{1,0:T(8,128)}, u32[]{:S(2)}, u32[]{:S(2)}) %collective-permute-start.6) | collective-permute-done | bytes 442400 | tf_op jit(solution)/shard_map/ppermute | solution.py:360
  108.2 1.7 %atm_step.6 = (f32[864,128]{1,0:T(8,128)S(1)}, f32[864,128]{1,0:T(8,128)S(1)}, f32[48,128]{1,0:T(8,128)S(1)}) custom-call(f32[864,128]{1,0:T(8,128)S(1)} %get-tuple-element.89.low, f32[864,128]{1,0:T(8,128)S(1)} %get-tuple-element.90.high, f32[864,128]{1,0:T(8,128)} %collective-permute-done.6.up, f32[864,128]{1,0:T(8,128)S(1)} %collective-permute-done.7.down, ...), custom_call_target="tpu_custom_call" | custom-call | flops 2750000128 | bytes 7500000 | tf_op jit(solution)/shard_map/atm_step/pallas_call | solution.py:346
  111.5 1.8 %collective-permute-start.11 = (f32[48,128]{1,0:T(8,128)S(1)}, f32[48,128]{1,0:T(8,128)S(1)}, u32[]{:S(2)}, u32[]{:S(2)}) collective-permute-start(f32[48,128]{1,0:T(8,128)S(1)} %get-tuple-element.100), channel_id=1, source_target_pairs={{0,1},{1,0},{2,3},{3,2},{4,5},{5,4},{6,7},{7,6},{8,9},{9,8},{10,11... | collective-permute-start | bytes 73736 | tf_op jit(solution)/shard_map/ppermute | solution.py:365
  113.3 6.9 %forcing_scatter.1 = (f32[2,56,128]{2,1,0:T(8,128)S(1)}, f32[2,56,128]{2,1,0:T(8,128)S(1)}, f32[2,14,128]{2,1,0:T(8,128)S(1)}, f32[2,14,128]{2,1,0:T(8,128)S(1)}) custom-call(f32[2,32,256]{2,1,0:T(8,128)S(1)} %forcing_half.1.half_ref, f32[128,8,128]{2,1,0:T(8,128)S(1)} %all-to-all-done.1.val_ref, s32[128,512]{1,0:T(8,128)} %bitcast.11, f32[56,128]{1,0:T(8,128)S(1)} %copy-done.8), custom_call_target="tpu_custom_call" | custom-call | flops 8249999872 | bytes 22500000 | tf_op jit(solution)/shard_map/forcing_scatter/pallas_call | solution.py:346
  120.3 6.9 %collective-permute-start.13 = (f32[2,14,128]{2,1,0:T(8,128)S(1)}, f32[2,14,128]{2,1,0:T(8,128)S(1)}, u32[]{:S(2)}, u32[]{:S(2)}) collective-permute-start(f32[2,14,128]{2,1,0:T(8,128)S(1)} %get-tuple-element.109), channel_id=1, source_target_pairs={{2,0},{4,2},{6,4},{8,6},{10,8},{12,10},{14,12},{16,14},{18,16},{20... | collective-permute-start | bytes 43016 | tf_op jit(solution)/shard_map/ppermute | solution.py:360
  127.8 2.0 %atm_step.7 = f32[2,48,2,1152]{3,2,1,0:T(2,128)} custom-call(f32[864,128]{1,0:T(8,128)S(1)} %get-tuple-element.96.low, f32[864,128]{1,0:T(8,128)S(1)} %get-tuple-element.97.high, f32[864,128]{1,0:T(8,128)S(1)} %collective-permute-done.9.up, f32[864,128]{1,0:T(8,128)S(1)} %collective-permute-done.10.down, f32[48,128]{1,0:T(8,128)S(1)} %collective-permute-done.11.edges_ref, ...), custom_call_target="tpu_custom_call" | custom-call | flops 2750000128 | bytes 7500000 | tf_op jit(solution)/shard_map/atm_step/pallas_call | solution.py:346
  (63 shorter events, 9.4 us)
Async XLA Ops:
  0.6 15.9 %copy-start = (f32[1,1,128,512]{3,2,1,0:T(8,128)S(1)}, f32[1,1,128,512]{3,2,1,0:T(8,128)}, u32[]{:S(2)}) copy-start(f32[1,1,128,512]{3,2,1,0:T(8,128)} %param.19) | copy-start | bytes 786436
  0.6 15.9 %copy-start.3 = (s32[1,1,128,512]{3,2,1,0:T(8,128)S(1)}, s32[1,1,128,512]{3,2,1,0:T(8,128)}, u32[]{:S(2)}) copy-start(s32[1,1,128,512]{3,2,1,0:T(8,128)} %param.18) | copy-start | bytes 786436
  5.3 30.3 %collective-permute-start = (f32[1536,128]{1,0:T(8,128)S(1)}, f32[1536,128]{1,0:T(8,128)S(1)}, u32[]{:S(2)}, u32[]{:S(2)}) collective-permute-start(f32[1536,128]{1,0:T(8,128)S(1)} %get-tuple-element.58.high), channel_id=1, source_target_pairs={{0,2},{2,4},{4,6},{6,8},{8,10},{10,12},{12,14},{14,16},{16,18},{18... | collective-permute-start | bytes 2359304 | tf_op jit(solution)/shard_map/ppermute | solution.py:360
  7.9 27.7 %collective-permute-start.1 = (f32[1536,128]{1,0:T(8,128)S(1)}, f32[1536,128]{1,0:T(8,128)S(1)}, u32[]{:S(2)}, u32[]{:S(2)}) collective-permute-start(f32[1536,128]{1,0:T(8,128)S(1)} %get-tuple-element.59.low), channel_id=1, source_target_pairs={{2,0},{4,2},{6,4},{8,6},{10,8},{12,10},{14,12},{16,14},{18,16},{20... | collective-permute-start | bytes 2359304 | tf_op jit(solution)/shard_map/ppermute | solution.py:360
  16.6 19.1 %copy-start.8 = (f32[56,128]{1,0:T(8,128)S(1)}, f32[56,128]{1,0:T(8,128)}, u32[]{:S(2)}) copy-start(f32[56,128]{1,0:T(8,128)} %get-tuple-element.62.refs_5_.frac_ref) | copy-start | bytes 86020
  16.6 19.1 %copy-start.10 = (f32[24,128]{1,0:T(8,128)S(1)}, f32[24,128]{1,0:T(8,128)}, u32[]{:S(2)}) copy-start(f32[24,128]{1,0:T(8,128)} %get-tuple-element.61.refs_4_.diff_ref) | copy-start | bytes 36868
  25.2 20.9 %all-to-all-start = ((f32[128,4,128]{2,1,0:T(4,128)}), f32[128,4,128]{2,1,0:T(4,128)S(1)}, u32[]{:S(2)}, u32[]{:S(2)}) async-start(f32[128,4,128]{2,1,0:T(4,128)} %temp_gather.1), calls=%async_computation | async-start | bytes 524288 | tf_op jit(solution)/shard_map/all_to_all | solution.py:369
  33.1 2.5 %collective-permute-start.2 = (f32[72,128]{1,0:T(8,128)S(1)}, f32[72,128]{1,0:T(8,128)S(1)}, u32[]{:S(2)}, u32[]{:S(2)}) collective-permute-start(f32[72,128]{1,0:T(8,128)S(1)} %get-tuple-element.60), channel_id=1, source_target_pairs={{0,1},{1,0},{2,3},{3,2},{4,5},{5,4},{6,7},{7,6},{8,9},{9,8},{10,11... | collective-permute-start | bytes 110600 | tf_op jit(solution)/shard_map/ppermute | solution.py:365
  57.2 24.7 %collective-permute-start.4 = (f32[1536,128]{1,0:T(8,128)}, f32[1536,128]{1,0:T(8,128)S(1)}, u32[]{:S(2)}, u32[]{:S(2)}) collective-permute-start(f32[1536,128]{1,0:T(8,128)} %get-tuple-element.82.low), channel_id=1, source_target_pairs={{2,0},{4,2},{6,4},{8,6},{10,8},{12,10},{14,12},{16,14},{18,16},{20... | collective-permute-start | bytes 2359304 | tf_op jit(solution)/shard_map/ppermute | solution.py:360
  57.7 24.2 %collective-permute-start.3 = (f32[1536,128]{1,0:T(8,128)}, f32[1536,128]{1,0:T(8,128)S(1)}, u32[]{:S(2)}, u32[]{:S(2)}) collective-permute-start(f32[1536,128]{1,0:T(8,128)} %get-tuple-element.83.high), channel_id=1, source_target_pairs={{0,2},{2,4},{4,6},{6,8},{8,10},{10,12},{12,14},{14,16},{16,18},{18... | collective-permute-start | bytes 2359304 | tf_op jit(solution)/shard_map/ppermute | solution.py:360
  58.7 23.2 %copy-start.13 = (f32[48,128]{1,0:T(8,128)S(1)}, f32[48,128]{1,0:T(8,128)}, u32[]{:S(2)}) copy-start(f32[48,128]{1,0:T(8,128)} %get-tuple-element.69.diff_ref) | copy-start | bytes 73732
  58.7 23.2 %copy-start.16 = (f32[18,128]{1,0:T(8,128)S(1)}, f32[18,128]{1,0:T(8,128)}, u32[]{:S(2)}) copy-start(f32[18,128]{1,0:T(8,128)} %get-tuple-element.70.temp_ref) | copy-start | bytes 27652
  67.6 26.4 %all-to-all-start.1 = ((f32[128,8,128]{2,1,0:T(8,128)}), f32[128,8,128]{2,1,0:T(8,128)S(1)}, u32[]{:S(2)}, u32[]{:S(2)}) async-start(f32[128,8,128]{2,1,0:T(8,128)} %flux_gather.1), calls=%async_computation.1 | async-start | bytes 1048576 | tf_op jit(solution)/shard_map/all_to_all | solution.py:369
  77.0 14.4 %copy-start.7 = (f32[2688,128]{1,0:T(8,128)S(1)}, f32[2688,128]{1,0:T(8,128)}, u32[]{:S(2)}) copy-start(f32[2688,128]{1,0:T(8,128)} %copy-done.5) | copy-start | bytes 4128772
  77.1 4.8 %collective-permute-start.5 = (f32[72,128]{1,0:T(8,128)S(1)}, f32[72,128]{1,0:T(8,128)S(1)}, u32[]{:S(2)}, u32[]{:S(2)}) collective-permute-start(f32[72,128]{1,0:T(8,128)S(1)} %get-tuple-element.76), channel_id=1, source_target_pairs={{0,1},{1,0},{2,3},{3,2},{4,5},{5,4},{6,7},{7,6},{8,9},{9,8},{10,11... | collective-permute-start | bytes 110600 | tf_op jit(solution)/shard_map/ppermute | solution.py:365
  83.9 17.1 %collective-permute-start.8 = (f32[48,128]{1,0:T(8,128)S(1)}, f32[48,128]{1,0:T(8,128)S(1)}, u32[]{:S(2)}, u32[]{:S(2)}) collective-permute-start(f32[48,128]{1,0:T(8,128)S(1)} %get-tuple-element.87), channel_id=1, source_target_pairs={{0,1},{1,0},{2,3},{3,2},{4,5},{5,4},{6,7},{7,6},{8,9},{9,8},{10,11... | collective-permute-start | bytes 73736 | tf_op jit(solution)/shard_map/ppermute | solution.py:365
  85.9 15.1 %collective-permute-start.7 = (f32[864,128]{1,0:T(8,128)S(1)}, f32[864,128]{1,0:T(8,128)S(1)}, u32[]{:S(2)}, u32[]{:S(2)}) collective-permute-start(f32[864,128]{1,0:T(8,128)S(1)} %get-tuple-element.89.low), channel_id=1, source_target_pairs={{2,0},{4,2},{6,4},{8,6},{10,8},{12,10},{14,12},{16,14},{18,16},{20... | collective-permute-start | bytes 1327112 | tf_op jit(solution)/shard_map/ppermute | solution.py:360
  91.4 16.8 %collective-permute-start.6 = (f32[864,128]{1,0:T(8,128)S(1)}, f32[864,128]{1,0:T(8,128)}, u32[]{:S(2)}, u32[]{:S(2)}) collective-permute-start(f32[864,128]{1,0:T(8,128)S(1)} %get-tuple-element.90.high), channel_id=1, source_target_pairs={{0,2},{2,4},{4,6},{6,8},{8,10},{10,12},{12,14},{14,16},{16,18},{18... | collective-permute-start | bytes 1327112 | tf_op jit(solution)/shard_map/ppermute | solution.py:360
  109.9 17.9 %collective-permute-start.10 = (f32[864,128]{1,0:T(8,128)S(1)}, f32[864,128]{1,0:T(8,128)S(1)}, u32[]{:S(2)}, u32[]{:S(2)}) collective-permute-start(f32[864,128]{1,0:T(8,128)S(1)} %get-tuple-element.96.low), channel_id=1, source_target_pairs={{2,0},{4,2},{6,4},{8,6},{10,8},{12,10},{14,12},{16,14},{18,16},{20... | collective-permute-start | bytes 1327112 | tf_op jit(solution)/shard_map/ppermute | solution.py:360
  110.2 17.6 %collective-permute-start.9 = (f32[864,128]{1,0:T(8,128)S(1)}, f32[864,128]{1,0:T(8,128)S(1)}, u32[]{:S(2)}, u32[]{:S(2)}) collective-permute-start(f32[864,128]{1,0:T(8,128)S(1)} %get-tuple-element.97.high), channel_id=1, source_target_pairs={{0,2},{2,4},{4,6},{6,8},{8,10},{10,12},{12,14},{14,16},{16,18},{18... | collective-permute-start | bytes 1327112 | tf_op jit(solution)/shard_map/ppermute | solution.py:360
  111.5 15.8 %collective-permute-start.11 = (f32[48,128]{1,0:T(8,128)S(1)}, f32[48,128]{1,0:T(8,128)S(1)}, u32[]{:S(2)}, u32[]{:S(2)}) collective-permute-start(f32[48,128]{1,0:T(8,128)S(1)} %get-tuple-element.100), channel_id=1, source_target_pairs={{0,1},{1,0},{2,3},{3,2},{4,5},{5,4},{6,7},{7,6},{8,9},{9,8},{10,11... | collective-permute-start | bytes 73736 | tf_op jit(solution)/shard_map/ppermute | solution.py:365
  120.2 9.5 %collective-permute-start.12 = (f32[2,14,128]{2,1,0:T(8,128)S(1)}, f32[2,14,128]{2,1,0:T(8,128)S(1)}, u32[]{:S(2)}, u32[]{:S(2)}) collective-permute-start(f32[2,14,128]{2,1,0:T(8,128)S(1)} %get-tuple-element.108), channel_id=1, source_target_pairs={{0,2},{2,4},{4,6},{6,8},{8,10},{10,12},{12,14},{14,16},{16,18},{18... | collective-permute-start | bytes 43016 | tf_op jit(solution)/shard_map/ppermute | solution.py:360
  120.3 9.5 %collective-permute-start.13 = (f32[2,14,128]{2,1,0:T(8,128)S(1)}, f32[2,14,128]{2,1,0:T(8,128)S(1)}, u32[]{:S(2)}, u32[]{:S(2)}) collective-permute-start(f32[2,14,128]{2,1,0:T(8,128)S(1)} %get-tuple-element.109), channel_id=1, source_target_pairs={{2,0},{4,2},{6,4},{8,6},{10,8},{12,10},{14,12},{16,14},{18,16},{20... | collective-permute-start | bytes 43016 | tf_op jit(solution)/shard_map/ppermute | solution.py:360
  127.2 2.6 %collective-permute-start.14 = (f32[2,56,128]{2,1,0:T(8,128)S(1)}, f32[2,56,128]{2,1,0:T(8,128)S(1)}, u32[]{:S(2)}, u32[]{:S(2)}) collective-permute-start(f32[2,56,128]{2,1,0:T(8,128)S(1)} %get-tuple-element.107.gain_ref), channel_id=1, source_target_pairs={{0,1},{1,0},{2,3},{3,2},{4,5},{5,4},{6,7},{7,6},{8,9},{9,8},{10,11... | collective-permute-start | bytes 172040 | tf_op jit(solution)/shard_map/ppermute | solution.py:365
  (13 other events, 83.9 us)

commit v5 on v4

--- a/solution.py
+++ b/solution.py
@@ -20,9 +20,9 @@
 SPLITS = 3
 
 
-def parts_of(v):
+def parts_of(v, count=SPLITS):
     out = []
-    for _ in range(SPLITS):
+    for _ in range(count):
         p = v.astype(BF16)
         out.append(p)
         v = v - p.astype(F32)
@@ -64,7 +64,7 @@
     lax.fori_loop(0, index_ref.shape[0] // 8, group, 0)
 
 
-def scatter_loop(val_ref, index, H, L, F, start=0, stop=None):
+def scatter_loop(val_ref, index, H, L, F, start=0, stop=None, splits=SPLITS):
     index_hbm, index_ref, sems = index
     stop = stop or index_ref.shape[0]
     cuts = (start, start + 16, stop)
@@ -82,17 +82,17 @@
             a = []
             for f in range(F):
                 v = jnp.concatenate([val_ref[base + r, 4 * f + q : 4 * f + q + 1, :] for q in range(4)], axis=1)
-                for p in parts_of(jnp.broadcast_to(v, (16, v.shape[1]))):
+                for p in parts_of(jnp.broadcast_to(v, (16, v.shape[1])), splits):
                     a += [jnp.where(m, p, jnp.zeros_like(p)) for m in masks]
             a = jnp.concatenate(a, axis=0)
             acc = acc + lax.dot_general(one_hot(lo[r : r + 1], L), a, (((1,), (1,)), ((), ())), preferred_element_type=F32)
         return acc
-    acc = jnp.zeros((L, F * SPLITS * H), F32)
+    acc = jnp.zeros((L, F * splits * H), F32)
     for copy, a, b in zip(copies, cuts, cuts[1:]):
         copy.wait()
         acc = lax.fori_loop(a // 8, b // 8, group, acc)
     acc = acc.T
-    return [sum(acc[(f * SPLITS + i) * H : (f * SPLITS + i + 1) * H] for i in range(SPLITS)) for f in range(F)]
+    return [sum(acc[(f * splits + i) * H : (f * splits + i + 1) * H] for i in range(splits)) for f in range(F)]
 
 
 def temp_kernel(table_ref, cell_ref, w_ref, out_ref, t_ref):
@@ -285,15 +285,13 @@
 
 
 def half_kernel(val_ref, cell_ref, out_ref, *store):
-    for f, total in enumerate(scatter_loop(val_ref, (cell_ref, *store), 32, 256, 2, stop=val_ref.shape[0] // 2)):
+    for f, total in enumerate(scatter_loop(val_ref, (cell_ref, *store), 64, LANES, 2, stop=val_ref.shape[0] // 2, splits=2)):
         out_ref[f] = total
 
 
 def forcing_kernel(half_ref, val_ref, cell_ref, frac_ref, out_ref, gain_ref, low, high, *store):
-    for f, total in enumerate(scatter_loop(val_ref, (cell_ref, *store), 32, 256, 2, start=val_ref.shape[0] // 2)):
-        total = (HEAT_GAIN, -SALT_GAIN)[f] * (half_ref[f] + total)[: OR * OT // 2]
-        for side in range(2):
-            out_ref[f, pl.ds(side, OR * OT // 2, stride=2), :] = total[:, side * LANES : (side + 1) * LANES]
+    for f, total in enumerate(scatter_loop(val_ref, (cell_ref, *store), 64, LANES, 2, start=val_ref.shape[0] // 2, splits=2)):
+        out_ref[f] = (HEAT_GAIN, -SALT_GAIN)[f] * (half_ref[f] + total)[: OR * OT]
         gain_ref[f] = out_ref[f] * frac_ref[...]
         low[f] = gain_ref[f, :OT, :]
         high[f] = gain_ref[f, (OR - 1) * OT :, :]
@@ -402,14 +400,11 @@
         in_specs=[HBM] * 4 + [VM] * 2,
         scratch=[pltpu.VMEM(x.shape, x.dtype) for x in (atm_state, ocn_state, sea_mask, atm_surface_coef)] + [pltpu.SemaphoreType.DMA((4,))],
     )
+    outgoing = call(temp_kernel, "temp_gather", 9, shape(group_size, 4, LANES), table, cells, o2a_weights[0, 0], cold=(1, 2), scratch=[pltpu.VMEM((128, SPLITS * 64), BF16)])
+    incoming = exchange(outgoing)
+    outgoing, low, high, edges = lax.optimization_barrier((outgoing, low, high, edges))
     up, down = row_halos(low, high)
     beside = partner(edges)
-
-    outgoing = call(temp_kernel, "temp_gather", 9, shape(group_size, 4, LANES), table, cells, o2a_weights[0, 0], cold=(1, 2), scratch=[pltpu.VMEM((128, SPLITS * 64), BF16)])
-    incoming = exchange(outgoing)
-    ocn_step = lambda *refs: ocn_kernel(False, *refs)
-    ocean, ocn_edges = call(ocn_step, "ocn_step", 3, (shape(OR * OSIZE, LANES), free(OL, LANES)), ocean, up, down, beside, ocn_diff, frac, cold=(4, 5))
-    incoming, ocean, ocn_edges = lax.optimization_barrier((incoming, ocean, ocn_edges))
 
     temp, flux_table = call(flux_kernel, "temp_scatter", 9, (free(AR * AT, LANES), pltpu.VMEM((128, SPLITS * 48), BF16)), incoming, cols, surface, coef, far=(1,), cold=(2, 3), in_specs=[VM, HBM, VM, VM], scratch=[pltpu.VMEM((24, LANES), F32), *store])
 
@@ -418,6 +413,9 @@
         outs = outs or (rows, rows, shape(AL + (OL if more else 0), LANES))
         return call(atm_kernel, "atm_step", 2.5, outs, low, high, up, down, beside, atm_diff, coef, temp, *more, cold=(5, 6, 7, 9))
 
+    flux_table, up, down, beside = lax.optimization_barrier((flux_table, up, down, beside))
+    ocn_step = lambda *refs: ocn_kernel(False, *refs)
+    ocean, ocn_edges = call(ocn_step, "ocn_step", 3, (shape(OR * OSIZE, LANES), free(OL, LANES)), ocean, up, down, beside, ocn_diff, frac, cold=(4, 5))
     low, high, edges = atm_step(low, high, up, down, beside, ocean, ocn_edges)
     up, down = row_halos(low, high)
     beside = partner(edges)
@@ -433,7 +431,7 @@
     beside = partner(edges)
     incoming, ocean, top, low, high = lax.optimization_barrier((incoming, ocean, top, low, high))
 
-    half = call(half_kernel, "forcing_half", 7.5, shape(2, 32, 256), incoming, cells, far=(1,), in_specs=[VM, HBM], scratch=store)
+    half = call(half_kernel, "forcing_half", 4, shape(2, 64, LANES), incoming, cells, far=(1,), in_specs=[VM, HBM], scratch=store)
     half, up, down, beside = lax.optimization_barrier((half, up, down, beside))
     low, high, edges = atm_step(low, high, up, down, beside)
     up, down = row_halos(low, high)
@@ -441,7 +439,7 @@
     half, low, high = lax.optimization_barrier((half, low, high))
 
     every = shape(2, OR * OT, LANES)
-    forcing, gained, first, last = call(forcing_kernel, "forcing_scatter", 7.5, (every, every, shape(2, OT, LANES), shape(2, OT, LANES)), half, incoming, cells, frac, far=(2,), cold=(3,), in_specs=[VM, VM, HBM, VM], scratch=store)
+    forcing, gained, first, last = call(forcing_kernel, "forcing_scatter", 4, (every, every, shape(2, OT, LANES), shape(2, OT, LANES)), half, incoming, cells, frac, far=(2,), cold=(3,), in_specs=[VM, VM, HBM, VM], scratch=store)
     above, below = row_halos(first, last)
     side = partner(gained)
     forcing, up, down, beside = lax.optimization_barrier((forcing, up, down, beside))

time: 131 us -> 142 us (1.084)
  starting transfers between devices: 53.9 us -> 58.1 us
  waiting for transfers between devices: 15.5 us -> 19.2 us
    all_to_all x2, starting transfers between devices: 17.3 us -> 26.7 us  [exchange(): lax.all_to_all(values, GROUP, split_axis=0, concat_axis=0, tiled=True)]
    ppermute x5, waiting for transfers between devices: 7.2 us -> 11.5 us  [row_halos(): lax.ppermute(last, GROUP, up)]
    ppermute x5, starting transfers between devices: 9.98 us -> 5.79 us  [partner(): lax.ppermute(edges, 'lev', [(i, (i + 1) % count) for i in range(count)])]
    ppermute x5, starting transfers between devices: 4.81 us -> 0.96 us  [row_halos(): lax.ppermute(last, GROUP, up)]
    ppermute x5, starting transfers between devices: 21.8 us -> 24.7 us  [row_halos(): lax.ppermute(first, GROUP, [(b, a) for a, b in up])]
    unnamed x40 -> x44, local copies, waits for them, and re-layouts: 3.18 us -> 4.28 us
  transfers between devices with their start and end apart: 17 -> 17, of which waited for: 4 -> 7; matrix products, arithmetic and copies ran while one was open for 0% -> 0% of each run, Pallas kernels for 30% -> 29%
where the time goes in v5:
time: 142 us; the launch traced here: 141 us
  Pallas kernels  58.5 us (41%)
  starting transfers between devices  58.1 us (41%)
  waiting for transfers between devices  19.2 us (14%)
  local copies, waits for them, and re-layouts  4.28 us (3%)
    pallas_call x13, Pallas kernels, call(): pl.pallas_call(kernel, out_shape=out_shape, scratch_shapes=list(scratch),...  58.5 us
    all_to_all x2, starting transfers between devices, exchange(): lax.all_to_all(values, GROUP, split_axis=0, concat_axis=0, tiled=True)  26.7 us
    ppermute x5, starting transfers between devices, row_halos(): lax.ppermute(first, GROUP, [(b, a) for a, b in up])  24.7 us
    ppermute x5, waiting for transfers between devices, row_halos(): lax.ppermute(last, GROUP, up)  11.5 us
    all_to_all x2, waiting for transfers between devices, exchange(): lax.all_to_all(values, GROUP, split_axis=0, concat_axis=0, tiled=True)  6.75 us
    ppermute x5, starting transfers between devices, partner(): lax.ppermute(edges, 'lev', [(i, (i + 1) % count) for i in range(count)])  5.79 us
    unnamed x44, local copies, waits for them, and re-layouts  4.28 us
  transfers between devices with their start and end apart: 17, of which 7 were waited for; matrix products, arithmetic and copies ran while one was open for 0% of the time, Pallas kernels for 29%

profile of v5, /device:TPU:1, one launch (start us, length us, event | category | flops | bytes accessed | tf_op | source)
XLA Modules:
  0.0 141.1 jit_solution(2986153981466045876)
XLA Ops:
  0.7 4.7 %prep.1 = (f32[1536,128]{1,0:T(8,128)S(1)}, f32[1536,128]{1,0:T(8,128)S(1)}, f32[72,128]{1,0:T(8,128)S(1)}, f32[2688,128]{1,0:T(8,128)}, f32[56,128]{1,0:T(8,128...) custom-call(f32[2,48,2,1152]{3,2,1,0:T(2,128)} %atm_hbm.1, ...), custom_call_target="tpu_custom_call" | custom-call | flops 3300000000 | bytes 9000000 | tf_op jit(solution)/shard_map/prep/pallas_call | solution.py:344
  5.4 8.7 %temp_gather.1 = f32[128,4,128]{2,1,0:T(4,128)} custom-call(f32[64,128]{1,0:T(8,128)S(1)} %get-tuple-element.60.table_ref, s32[128,512]{1,0:T(8,128)S(1)} %bitcast.12, f32[128,512]{1,0:T(8,128)S(1)} %bitcast.6), custom_call_target="tpu_custom_call" | custom-call | flops 9900000256 | bytes 27000000 | tf_op jit(solution)/shard_map/temp_gather/pallas_call | solution.py:344
  14.0 16.3 %all-to-all-start = ((f32[128,4,128]{2,1,0:T(4,128)}), f32[128,4,128]{2,1,0:T(4,128)S(1)}, u32[]{:S(2)}, u32[]{:S(2)}) async-start(f32[128,4,128]{2,1,0:T(4,128)} %temp_gather.1), calls=%async_computation | async-start | bytes 524288 | tf_op jit(solution)/shard_map/all_to_all | solution.py:367
  32.3 6.2 %collective-permute-start.1 = (f32[1536,128]{1,0:T(8,128)S(1)}, f32[1536,128]{1,0:T(8,128)S(1)}, u32[]{:S(2)}, u32[]{:S(2)}) collective-permute-start(f32[1536,128]{1,0:T(8,128)S(1)} %get-tuple-element.68.low), channel_id=1, source_target_pairs={{2,0},{4,2},{6,4},{8,6},{10,8},{12,10},{14,12},{16,14},{18,16},{20... | collective-permute-start | bytes 2359304 | tf_op jit(solution)/shard_map/ppermute | solution.py:358
  38.5 5.3 %all-to-all-done.val_ref = f32[128,4,128]{2,1,0:T(4,128)S(1)} async-done(((f32[128,4,128]{2,1,0:T(4,128)}), f32[128,4,128]{2,1,0:T(4,128)S(1)}, u32[]{:S(2)}, u32[]{:S(2)}) %all-to-all-start) | async-done | bytes 262176 | tf_op jit(solution)/shard_map/all_to_all | solution.py:367
  44.5 8.5 %temp_scatter.1 = (f32[18,128]{1,0:T(8,128)}, bf16[128,144]{1,0:T(8,128)(2,1)S(1)}) custom-call(f32[128,4,128]{2,1,0:T(4,128)S(1)} %all-to-all-done.val_ref, s32[128,512]{1,0:T(8,128)} %bitcast.7, f32[2,18,128]{2,1,0:T(8,128)S(1)} %copy-done.21, f32[2,18,128]{2,1,0:T(8,128)S(1)} %copy-done.14), custom_call_target="tpu_custom_call" | custom-call | flops 9900000256 | bytes 27000000 | tf_op jit(solution)/shard_map/temp_scatter/pallas_call | solution.py:344
  53.1 6.2 %collective-permute-done.refs_1_.up = f32[1536,128]{1,0:T(8,128)S(1)} collective-permute-done((f32[1536,128]{1,0:T(8,128)S(1)}, f32[1536,128]{1,0:T(8,128)S(1)}, u32[]{:S(2)}, u32[]{:S(2)}) %collective-permute-start) | collective-permute-done | bytes 786464 | tf_op jit(solution)/shard_map/ppermute | solution.py:358
  59.3 1.6 %ocn_step.2 = (f32[2688,128]{1,0:T(8,128)S(1)}, f32[24,128]{1,0:T(8,128)}) custom-call(f32[2688,128]{1,0:T(8,128)S(1)} %copy-done.12, f32[1536,128]{1,0:T(8,128)S(1)} %collective-permute-done.refs_1_.up, f32[1536,128]{1,0:T(8,128)S(1)} %collective-permute-done.1.refs_2_.down, f32[72,128]{1,0:T(8,128)S(1)} %collective-permute-done.2.refs_3_.edges_ref, ...), custom_call_target="tpu_custom_call" | custom-call | flops 3300000000 | bytes 9000000 | tf_op jit(solution)/shard_map/ocn_step/pallas_call | solution.py:344
  60.9 1.6 %copy-done.1 = f32[1536,128]{1,0:T(8,128)S(1)} copy-done((f32[1536,128]{1,0:T(8,128)S(1)}, f32[1536,128]{1,0:T(8,128)}, u32[]{:S(2)}) %copy-start.1) | copy-done | bytes 786456
  65.1 3.6 %collective-permute-start.4 = (f32[1536,128]{1,0:T(8,128)S(1)}, f32[1536,128]{1,0:T(8,128)S(1)}, u32[]{:S(2)}, u32[]{:S(2)}) collective-permute-start(f32[1536,128]{1,0:T(8,128)S(1)} %get-tuple-element.90.low), channel_id=1, source_target_pairs={{2,0},{4,2},{6,4},{8,6},{10,8},{12,10},{14,12},{16,14},{18,16},{20... | collective-permute-start | bytes 2359304 | tf_op jit(solution)/shard_map/ppermute | solution.py:358
  68.7 8.9 %flux_gather.1 = f32[128,8,128]{2,1,0:T(8,128)} custom-call(bf16[128,144]{1,0:T(8,128)(2,1)S(1)} %get-tuple-element.83.t_ref, s32[128,512]{1,0:T(8,128)S(1)} %bitcast.8, f32[128,512]{1,0:T(8,128)S(1)} %bitcast.9), custom_call_target="tpu_custom_call" | custom-call | flops 9900000256 | bytes 27000000 | tf_op jit(solution)/shard_map/flux_gather/pallas_call | solution.py:344
  77.6 10.4 %all-to-all-start.1 = ((f32[128,8,128]{2,1,0:T(8,128)}), f32[128,8,128]{2,1,0:T(8,128)S(1)}, u32[]{:S(2)}, u32[]{:S(2)}) async-start(f32[128,8,128]{2,1,0:T(8,128)} %flux_gather.1), calls=%async_computation.1 | async-start | bytes 1048576 | tf_op jit(solution)/shard_map/all_to_all | solution.py:367
  88.0 2.0 %collective-permute-start.5 = (f32[72,128]{1,0:T(8,128)S(1)}, f32[72,128]{1,0:T(8,128)S(1)}, u32[]{:S(2)}, u32[]{:S(2)}) collective-permute-start(f32[72,128]{1,0:T(8,128)S(1)} %get-tuple-element.84), channel_id=1, source_target_pairs={{0,1},{1,0},{2,3},{3,2},{4,5},{5,4},{6,7},{7,6},{8,9},{9,8},{10,11... | collective-permute-start | bytes 110600 | tf_op jit(solution)/shard_map/ppermute | solution.py:363
  91.9 2.5 %atm_step.5 = (f32[864,128]{1,0:T(8,128)S(1)}, f32[864,128]{1,0:T(8,128)}, f32[48,128]{1,0:T(8,128)S(1)}) custom-call(f32[1536,128]{1,0:T(8,128)S(1)} %get-tuple-element.90.low, f32[1536,128]{1,0:T(8,128)S(1)} %get-tuple-element.91.high, f32[1536,128]{1,0:T(8,128)} %collective-permute-done.3.refs_1_.up, f32[1536,128]{1,0:T(8,128)S(1)} %collective-permute-done.4.refs_2_.down, ...), custom_call_target="tpu_custom_call" | custom-call | flops 2750000128 | bytes 7500000 | tf_op jit(solution)/shard_map/atm_step/pallas_call | solution.py:344
  94.4 6.1 %collective-permute-start.7 = (f32[864,128]{1,0:T(8,128)S(1)}, f32[864,128]{1,0:T(8,128)S(1)}, u32[]{:S(2)}, u32[]{:S(2)}) collective-permute-start(f32[864,128]{1,0:T(8,128)S(1)} %get-tuple-element.97.low), channel_id=1, source_target_pairs={{2,0},{4,2},{6,4},{8,6},{10,8},{12,10},{14,12},{16,14},{18,16},{20... | collective-permute-start | bytes 1327112 | tf_op jit(solution)/shard_map/ppermute | solution.py:358
  100.5 3.7 %ocn_step.3 = (f32[2,24,4,1792]{3,2,1,0:T(4,128)}, f32[2,2,4,1792]{3,2,1,0:T(4,128)}) custom-call(f32[2688,128]{1,0:T(8,128)S(1)} %copy-done.10, f32[1536,128]{1,0:T(8,128)} %collective-permute-done.3.refs_1_.up, f32[1536,128]{1,0:T(8,128)S(1)} %collective-permute-done.4.refs_2_.down, f32[72,128]{1,0:T(8,128)S(1)} %collective-permute-done.5.refs_3_.edges_ref, ...), custom_call_target="tpu_custom_call" | custom-call | flops 3300000000 | bytes 9000000 | tf_op jit(solution)/shard_map/ocn_step/pallas_call | solution.py:344
  106.3 7.4 %forcing_half.1.half_ref = f32[2,64,128]{2,1,0:T(8,128)S(1)} custom-call(f32[128,8,128]{2,1,0:T(8,128)S(1)} %all-to-all-done.1.val_ref, s32[128,512]{1,0:T(8,128)} %bitcast.10), custom_call_target="tpu_custom_call" | custom-call | flops 4400000000 | bytes 12000000 | tf_op jit(solution)/shard_map/forcing_half/pallas_call | solution.py:344
  113.7 3.9 %collective-permute-done.6.up = f32[864,128]{1,0:T(8,128)S(1)} collective-permute-done((f32[864,128]{1,0:T(8,128)}, f32[864,128]{1,0:T(8,128)S(1)}, u32[]{:S(2)}, u32[]{:S(2)}) %collective-permute-start.6) | collective-permute-done | bytes 442400 | tf_op jit(solution)/shard_map/ppermute | solution.py:358
  117.5 1.7 %atm_step.6 = (f32[864,128]{1,0:T(8,128)S(1)}, f32[864,128]{1,0:T(8,128)S(1)}, f32[48,128]{1,0:T(8,128)S(1)}) custom-call(f32[864,128]{1,0:T(8,128)S(1)} %get-tuple-element.97.low, f32[864,128]{1,0:T(8,128)} %get-tuple-element.98.high, f32[864,128]{1,0:T(8,128)S(1)} %collective-permute-done.6.up, f32[864,128]{1,0:T(8,128)S(1)} %collective-permute-done.7.down, ...), custom_call_target="tpu_custom_call" | custom-call | flops 2750000128 | bytes 7500000 | tf_op jit(solution)/shard_map/atm_step/pallas_call | solution.py:344
  119.2 2.0 %collective-permute-start.10 = (f32[864,128]{1,0:T(8,128)S(1)}, f32[864,128]{1,0:T(8,128)S(1)}, u32[]{:S(2)}, u32[]{:S(2)}) collective-permute-start(f32[864,128]{1,0:T(8,128)S(1)} %get-tuple-element.104.low), channel_id=1, source_target_pairs={{2,0},{4,2},{6,4},{8,6},{10,8},{12,10},{14,12},{16,14},{18,16},{20... | collective-permute-start | bytes 1327112 | tf_op jit(solution)/shard_map/ppermute | solution.py:358
  121.2 1.5 %collective-permute-start.11 = (f32[48,128]{1,0:T(8,128)S(1)}, f32[48,128]{1,0:T(8,128)S(1)}, u32[]{:S(2)}, u32[]{:S(2)}) collective-permute-start(f32[48,128]{1,0:T(8,128)S(1)} %get-tuple-element.108), channel_id=1, source_target_pairs={{0,1},{1,0},{2,3},{3,2},{4,5},{5,4},{6,7},{7,6},{8,9},{9,8},{10,11... | collective-permute-start | bytes 73736 | tf_op jit(solution)/shard_map/ppermute | solution.py:363
  122.7 7.4 %forcing_scatter.1 = (f32[2,56,128]{2,1,0:T(8,128)S(1)}, f32[2,56,128]{2,1,0:T(8,128)S(1)}, f32[2,14,128]{2,1,0:T(8,128)S(1)}, f32[2,14,128]{2,1,0:T(8,128)S(1)}) custom-call(f32[2,64,128]{2,1,0:T(8,128)S(1)} %forcing_half.1.half_ref, f32[128,8,128]{2,1,0:T(8,128)S(1)} %all-to-all-done.1.val_ref, s32[128,512]{1,0:T(8,128)} %bitcast.11, f32[56,128]{1,0:T(8,128)S(1)} %copy-done.11), custom_call_target="tpu_custom_call" | custom-call | flops 4400000000 | bytes 12000000 | tf_op jit(solution)/shard_map/forcing_scatter/pallas_call | solution.py:344
  130.2 6.9 %collective-permute-start.13 = (f32[2,14,128]{2,1,0:T(8,128)S(1)}, f32[2,14,128]{2,1,0:T(8,128)S(1)}, u32[]{:S(2)}, u32[]{:S(2)}) collective-permute-start(f32[2,14,128]{2,1,0:T(8,128)S(1)} %get-tuple-element.117), channel_id=1, source_target_pairs={{2,0},{4,2},{6,4},{8,6},{10,8},{12,10},{14,12},{16,14},{18,16},{20... | collective-permute-start | bytes 43016 | tf_op jit(solution)/shard_map/ppermute | solution.py:358
  138.1 2.0 %atm_step.7 = f32[2,48,2,1152]{3,2,1,0:T(2,128)} custom-call(f32[864,128]{1,0:T(8,128)S(1)} %get-tuple-element.104.low, f32[864,128]{1,0:T(8,128)S(1)} %get-tuple-element.105.high, f32[864,128]{1,0:T(8,128)S(1)} %collective-permute-done.9.up, f32[864,128]{1,0:T(8,128)S(1)} %collective-permute-done.10.down, f32[48,128]{1,0:T(8,128)S(1)} %collective-permute-done.11.edges_ref, ...), custom_call_target="tpu_custom_call" | custom-call | flops 2750000128 | bytes 7500000 | tf_op jit(solution)/shard_map/atm_step/pallas_call | solution.py:344
  (67 shorter events, 11.2 us)
Async XLA Ops:
  5.3 38.4 %copy-start.14 = (f32[2,18,128]{2,1,0:T(8,128)S(1)}, f32[2,18,128]{2,1,0:T(8,128)}, u32[]{:S(2)}) copy-start(f32[2,18,128]{2,1,0:T(8,128)} %get-tuple-element.62.coef_ref) | copy-start | bytes 55300
  14.0 29.8 %all-to-all-start = ((f32[128,4,128]{2,1,0:T(4,128)}), f32[128,4,128]{2,1,0:T(4,128)S(1)}, u32[]{:S(2)}, u32[]{:S(2)}) async-start(f32[128,4,128]{2,1,0:T(4,128)} %temp_gather.1), calls=%async_computation | async-start | bytes 524288 | tf_op jit(solution)/shard_map/all_to_all | solution.py:367
  30.4 22.7 %collective-permute-start.2 = (f32[72,128]{1,0:T(8,128)S(1)}, f32[72,128]{1,0:T(8,128)S(1)}, u32[]{:S(2)}, u32[]{:S(2)}) collective-permute-start(f32[72,128]{1,0:T(8,128)S(1)} %get-tuple-element.69), channel_id=1, source_target_pairs={{0,1},{1,0},{2,3},{3,2},{4,5},{5,4},{6,7},{7,6},{8,9},{9,8},{10,11... | collective-permute-start | bytes 110600 | tf_op jit(solution)/shard_map/ppermute | solution.py:363
  31.4 27.8 %collective-permute-start = (f32[1536,128]{1,0:T(8,128)S(1)}, f32[1536,128]{1,0:T(8,128)S(1)}, u32[]{:S(2)}, u32[]{:S(2)}) collective-permute-start(f32[1536,128]{1,0:T(8,128)S(1)} %get-tuple-element.67.high), channel_id=1, source_target_pairs={{0,2},{2,4},{4,6},{6,8},{8,10},{10,12},{12,14},{14,16},{16,18},{18... | collective-permute-start | bytes 2359304 | tf_op jit(solution)/shard_map/ppermute | solution.py:358
  32.3 27.0 %collective-permute-start.1 = (f32[1536,128]{1,0:T(8,128)S(1)}, f32[1536,128]{1,0:T(8,128)S(1)}, u32[]{:S(2)}, u32[]{:S(2)}) collective-permute-start(f32[1536,128]{1,0:T(8,128)S(1)} %get-tuple-element.68.low), channel_id=1, source_target_pairs={{2,0},{4,2},{6,4},{8,6},{10,8},{12,10},{14,12},{16,14},{18,16},{20... | collective-permute-start | bytes 2359304 | tf_op jit(solution)/shard_map/ppermute | solution.py:358
  44.5 14.8 %copy-start.11 = (f32[56,128]{1,0:T(8,128)S(1)}, f32[56,128]{1,0:T(8,128)}, u32[]{:S(2)}) copy-start(f32[56,128]{1,0:T(8,128)} %get-tuple-element.78.refs_5_.frac_ref) | copy-start | bytes 86020
  44.5 14.8 %copy-start.12 = (f32[2688,128]{1,0:T(8,128)S(1)}, f32[2688,128]{1,0:T(8,128)}, u32[]{:S(2)}) copy-start(f32[2688,128]{1,0:T(8,128)} %get-tuple-element.76.refs_0_) | copy-start | bytes 4128772
  44.5 14.8 %copy-start.13 = (f32[24,128]{1,0:T(8,128)S(1)}, f32[24,128]{1,0:T(8,128)}, u32[]{:S(2)}) copy-start(f32[24,128]{1,0:T(8,128)} %get-tuple-element.77.refs_4_.diff_ref) | copy-start | bytes 36868
  65.1 25.8 %collective-permute-start.4 = (f32[1536,128]{1,0:T(8,128)S(1)}, f32[1536,128]{1,0:T(8,128)S(1)}, u32[]{:S(2)}, u32[]{:S(2)}) collective-permute-start(f32[1536,128]{1,0:T(8,128)S(1)} %get-tuple-element.90.low), channel_id=1, source_target_pairs={{2,0},{4,2},{6,4},{8,6},{10,8},{12,10},{14,12},{16,14},{18,16},{20... | collective-permute-start | bytes 2359304 | tf_op jit(solution)/shard_map/ppermute | solution.py:358
  68.7 23.2 %collective-permute-start.3 = (f32[1536,128]{1,0:T(8,128)S(1)}, f32[1536,128]{1,0:T(8,128)}, u32[]{:S(2)}, u32[]{:S(2)}) collective-permute-start(f32[1536,128]{1,0:T(8,128)S(1)} %get-tuple-element.91.high), channel_id=1, source_target_pairs={{0,2},{2,4},{4,6},{6,8},{8,10},{10,12},{12,14},{14,16},{16,18},{18... | collective-permute-start | bytes 2359304 | tf_op jit(solution)/shard_map/ppermute | solution.py:358
  68.7 23.2 %copy-start.16 = (f32[48,128]{1,0:T(8,128)S(1)}, f32[48,128]{1,0:T(8,128)}, u32[]{:S(2)}) copy-start(f32[48,128]{1,0:T(8,128)} %get-tuple-element.74.diff_ref) | copy-start | bytes 73732
  68.7 23.2 %copy-start.19 = (f32[18,128]{1,0:T(8,128)S(1)}, f32[18,128]{1,0:T(8,128)}, u32[]{:S(2)}) copy-start(f32[18,128]{1,0:T(8,128)} %get-tuple-element.75.temp_ref) | copy-start | bytes 27652
  77.6 28.7 %all-to-all-start.1 = ((f32[128,8,128]{2,1,0:T(8,128)}), f32[128,8,128]{2,1,0:T(8,128)S(1)}, u32[]{:S(2)}, u32[]{:S(2)}) async-start(f32[128,8,128]{2,1,0:T(8,128)} %flux_gather.1), calls=%async_computation.1 | async-start | bytes 1048576 | tf_op jit(solution)/shard_map/all_to_all | solution.py:367
  88.0 12.5 %copy-start.10 = (f32[2688,128]{1,0:T(8,128)S(1)}, f32[2688,128]{1,0:T(8,128)}, u32[]{:S(2)}) copy-start(f32[2688,128]{1,0:T(8,128)} %copy-done.9) | copy-start | bytes 4128772
  88.0 2.9 %collective-permute-start.5 = (f32[72,128]{1,0:T(8,128)S(1)}, f32[72,128]{1,0:T(8,128)S(1)}, u32[]{:S(2)}, u32[]{:S(2)}) collective-permute-start(f32[72,128]{1,0:T(8,128)S(1)} %get-tuple-element.84), channel_id=1, source_target_pairs={{0,1},{1,0},{2,3},{3,2},{4,5},{5,4},{6,7},{7,6},{8,9},{9,8},{10,11... | collective-permute-start | bytes 110600 | tf_op jit(solution)/shard_map/ppermute | solution.py:363
  94.4 19.2 %collective-permute-start.7 = (f32[864,128]{1,0:T(8,128)S(1)}, f32[864,128]{1,0:T(8,128)S(1)}, u32[]{:S(2)}, u32[]{:S(2)}) collective-permute-start(f32[864,128]{1,0:T(8,128)S(1)} %get-tuple-element.97.low), channel_id=1, source_target_pairs={{2,0},{4,2},{6,4},{8,6},{10,8},{12,10},{14,12},{16,14},{18,16},{20... | collective-permute-start | bytes 1327112 | tf_op jit(solution)/shard_map/ppermute | solution.py:358
  100.5 17.1 %collective-permute-start.6 = (f32[864,128]{1,0:T(8,128)}, f32[864,128]{1,0:T(8,128)S(1)}, u32[]{:S(2)}, u32[]{:S(2)}) collective-permute-start(f32[864,128]{1,0:T(8,128)} %get-tuple-element.98.high), channel_id=1, source_target_pairs={{0,2},{2,4},{4,6},{6,8},{8,10},{10,12},{12,14},{14,16},{16,18},{18... | collective-permute-start | bytes 1327112 | tf_op jit(solution)/shard_map/ppermute | solution.py:358
  104.2 9.4 %collective-permute-start.8 = (f32[48,128]{1,0:T(8,128)S(1)}, f32[48,128]{1,0:T(8,128)S(1)}, u32[]{:S(2)}, u32[]{:S(2)}) collective-permute-start(f32[48,128]{1,0:T(8,128)S(1)} %get-tuple-element.95), channel_id=1, source_target_pairs={{0,1},{1,0},{2,3},{3,2},{4,5},{5,4},{6,7},{7,6},{8,9},{9,8},{10,11... | collective-permute-start | bytes 73736 | tf_op jit(solution)/shard_map/ppermute | solution.py:363
  119.2 18.4 %collective-permute-start.10 = (f32[864,128]{1,0:T(8,128)S(1)}, f32[864,128]{1,0:T(8,128)S(1)}, u32[]{:S(2)}, u32[]{:S(2)}) collective-permute-start(f32[864,128]{1,0:T(8,128)S(1)} %get-tuple-element.104.low), channel_id=1, source_target_pairs={{2,0},{4,2},{6,4},{8,6},{10,8},{12,10},{14,12},{16,14},{18,16},{20... | collective-permute-start | bytes 1327112 | tf_op jit(solution)/shard_map/ppermute | solution.py:358
  121.2 16.9 %collective-permute-start.9 = (f32[864,128]{1,0:T(8,128)S(1)}, f32[864,128]{1,0:T(8,128)S(1)}, u32[]{:S(2)}, u32[]{:S(2)}) collective-permute-start(f32[864,128]{1,0:T(8,128)S(1)} %get-tuple-element.105.high), channel_id=1, source_target_pairs={{0,2},{2,4},{4,6},{6,8},{8,10},{10,12},{12,14},{14,16},{16,18},{18... | collective-permute-start | bytes 1327112 | tf_op jit(solution)/shard_map/ppermute | solution.py:358
  121.2 15.9 %collective-permute-start.11 = (f32[48,128]{1,0:T(8,128)S(1)}, f32[48,128]{1,0:T(8,128)S(1)}, u32[]{:S(2)}, u32[]{:S(2)}) collective-permute-start(f32[48,128]{1,0:T(8,128)S(1)} %get-tuple-element.108), channel_id=1, source_target_pairs={{0,1},{1,0},{2,3},{3,2},{4,5},{5,4},{6,7},{7,6},{8,9},{9,8},{10,11... | collective-permute-start | bytes 73736 | tf_op jit(solution)/shard_map/ppermute | solution.py:363
  130.1 10.0 %collective-permute-start.12 = (f32[2,14,128]{2,1,0:T(8,128)S(1)}, f32[2,14,128]{2,1,0:T(8,128)S(1)}, u32[]{:S(2)}, u32[]{:S(2)}) collective-permute-start(f32[2,14,128]{2,1,0:T(8,128)S(1)} %get-tuple-element.116), channel_id=1, source_target_pairs={{0,2},{2,4},{4,6},{6,8},{8,10},{10,12},{12,14},{14,16},{16,18},{18... | collective-permute-start | bytes 43016 | tf_op jit(solution)/shard_map/ppermute | solution.py:358
  130.2 9.9 %collective-permute-start.13 = (f32[2,14,128]{2,1,0:T(8,128)S(1)}, f32[2,14,128]{2,1,0:T(8,128)S(1)}, u32[]{:S(2)}, u32[]{:S(2)}) collective-permute-start(f32[2,14,128]{2,1,0:T(8,128)S(1)} %get-tuple-element.117), channel_id=1, source_target_pairs={{2,0},{4,2},{6,4},{8,6},{10,8},{12,10},{14,12},{16,14},{18,16},{20... | collective-permute-start | bytes 43016 | tf_op jit(solution)/shard_map/ppermute | solution.py:358
  137.1 3.0 %collective-permute-start.14 = (f32[2,56,128]{2,1,0:T(8,128)S(1)}, f32[2,56,128]{2,1,0:T(8,128)S(1)}, u32[]{:S(2)}, u32[]{:S(2)}) collective-permute-start(f32[2,56,128]{2,1,0:T(8,128)S(1)} %get-tuple-element.115.gain_ref), channel_id=1, source_target_pairs={{0,1},{1,0},{2,3},{3,2},{4,5},{5,4},{6,7},{7,6},{8,9},{9,8},{10,11... | collective-permute-start | bytes 172040 | tf_op jit(solution)/shard_map/ppermute | solution.py:363
  (15 other events, 46.1 us)

commit v6 on v4

--- a/solution.py
+++ b/solution.py
@@ -103,6 +103,10 @@
 AT, AL, AR = 9, 48, 2
 OT, OL, OR = 14, 24, 4
 ASIZE, OSIZE = 2 * AT * AL, 2 * OT * OL
+SURFACE = 2 * ASIZE + OSIZE
+TEMP = SURFACE + 2 * AR * AT
+BESIDE = TEMP + AR * AT + 2
+MESSAGE = BESIDE + AL
 
 
 def flux_kernel(val_ref, col_ref, state_ref, coef_ref, temp_ref, t_ref, flux_ref, *store):
@@ -225,6 +229,31 @@
     edges[AL:, :] = edges_of(ends)
 
 
+def atm_row(place, up, down, edges, i, f, side_gain, surface, store):
+    own_gain = (1.0 - 2.0 * VERT_MIX) - 4.0 * side_gain
+    top = lax.broadcasted_iota(jnp.int32, (8, LANES), 0) == 0
+    def finish(j, fresh, old):
+        coef, temp = surface(j)
+        gain = coef * ((1.0, MOIST_RATIO)[f] * temp - old[:1])
+        fresh = jnp.concatenate([fresh[:8] + jnp.where(top, gain, 0.0), fresh[8:]], axis=0)
+        store(j, fresh)
+        return fresh
+    base = f * AT * AL
+    shifted = ((ref, line + base) for ref, line in (place, up, down))
+    return step_row(*shifted, AT, AL, edge(edges, 2 * i + 1), edge(edges, 2 * i), own_gain, side_gain, VERT_MIX, finish)
+
+
+def own_surface(coef_ref, temp_ref, r, f):
+    return lambda j: (coef_ref[f, r * AT + j : r * AT + j + 1, :], temp_ref[r * AT + j : r * AT + j + 1, :])
+
+
+def sent_surface(ref, r, f):
+    def lines(j):
+        coef, temp = SURFACE + (f * AR + r) * AT + j, TEMP + r * AT + j
+        return ref[coef : coef + 1, :], ref[temp : temp + 1, :]
+    return lines
+
+
 def atm_kernel(low, high, up, down, edges_ref, diff_ref, coef_ref, temp_ref, *rest):
     share, final = len(rest) == 5, len(rest) == 1
     if share:
@@ -234,33 +263,61 @@
     else:
         out_low, out_high, out_edges = rest
     edges, side_gain = edges_ref[:AL, :], diff_ref[...]
-    own_gain = (1.0 - 2.0 * VERT_MIX) - 4.0 * side_gain
-    top = lax.broadcasted_iota(jnp.int32, (8, LANES), 0) == 0
-    rows = [up, low, high, down]
+    rows = [(ref, 0) for ref in (up, low, high, down)]
     ends = []
     for r, out in enumerate((out_low, out_high)):
         for f in range(2):
-            def finish(j, fresh, old, f=f, r=r, out=out):
-                at = r * AT + j
-                gain = (1.0, MOIST_RATIO)[f] * temp_ref[at : at + 1, :]
-                gain = coef_ref[f, at : at + 1, :] * (gain - old[:1])
-                fresh = jnp.concatenate([fresh[:8] + jnp.where(top, gain, 0.0), fresh[8:]], axis=0)
+            def store(j, fresh, f=f, r=r, out=out):
+                line = (f * AT + j) * AL
                 if final:
                     out[f, :, r, j * LANES : (j + 1) * LANES] = fresh
+                elif share:
+                    out_low[r * ASIZE + line : r * ASIZE + line + AL, :] = fresh
+                    out_high[r * ASIZE + line : r * ASIZE + line + AL, :] = fresh
                 else:
-                    out[(f * AT + j) * AL : (f * AT + j + 1) * AL, :] = fresh
-                return fresh
-            i, base = 2 * r + f, f * AT * AL
-            ends.append(step_row(*((rows[k], base) for k in (r + 1, r, r + 2)), AT, AL, edge(edges, 2 * i + 1), edge(edges, 2 * i), own_gain, side_gain, VERT_MIX, finish))
+                    out[line : line + AL, :] = fresh
+            ends.append(atm_row(rows[r + 1], rows[r], rows[r + 2], edges, 2 * r + f, f, side_gain, own_surface(coef_ref, temp_ref, r, f), store))
     if not final:
         out_edges[:AL, :] = edges_of(ends)
     if share:
-        out_low[ASIZE:, :] = ocean[:OSIZE, :]
-        out_high[ASIZE:, :] = ocean[(OR - 1) * OSIZE :, :]
         out_edges[AL:, :] = ocn_edges[...]
-
-
-def ocn_kernel(final, own, up, down, edges_ref, diff_ref, frac_ref, out, out_more):
+        for out, r in ((out_low, 0), (out_high, OR - 1)):
+            out[2 * ASIZE : SURFACE, :] = ocean[r * OSIZE : (r + 1) * OSIZE, :]
+            for f in range(2):
+                out[SURFACE + f * AR * AT : SURFACE + (f + 1) * AR * AT, :] = coef_ref[f]
+            out[TEMP : TEMP + AR * AT, :] = temp_ref[...]
+            out[TEMP + AR * AT :, :] = jnp.zeros((MESSAGE - TEMP - AR * AT, LANES), F32)
+
+
+def beside_kernel(low, high, beside, out_low, out_high, sems):
+    copies = [pltpu.make_async_copy(beside.at[pl.ds(0, AL)], out.at[pl.ds(BESIDE, AL)], sems.at[i]) for i, out in enumerate((out_low, out_high))]
+    for copy in copies:
+        copy.start()
+    for copy in copies:
+        copy.wait()
+
+
+def wide_kernel(own, up, down, edges_ref, diff_ref, coef_ref, temp_ref, out_low, out_high, out_up, out_down, out_edges):
+    rows = [(up, 0), (up, ASIZE), (own, 0), (own, ASIZE), (down, 0), (down, ASIZE)]
+    edges, side_gain = edges_ref[:AL, :], diff_ref[...]
+    ends = []
+    for k, out in ((1, out_up), (2, out_low), (3, out_high), (4, out_down)):
+        for f in range(2):
+            def store(j, fresh, f=f, out=out):
+                out[(f * AT + j) * AL : (f * AT + j + 1) * AL, :] = fresh
+            r = k % 2
+            if k in (1, 4):
+                ref = up if k == 1 else down
+                beside, surface = ref[BESIDE : BESIDE + AL, :], sent_surface(ref, r, f)
+            else:
+                beside, surface = edges, own_surface(coef_ref, temp_ref, r, f)
+            pair = atm_row(rows[k], rows[k - 1], rows[k + 1], beside, 2 * r + f, f, side_gain, surface, store)
+            if k in (2, 3):
+                ends.append(pair)
+    out_edges[...] = edges_of(ends)
+
+
+def ocn_kernel(final, place, own, up, down, edges_ref, diff_ref, frac_ref, out, out_more):
     edges, side_gain = edges_ref[AL:, :], diff_ref[...]
     own_gain = (1.0 - 2.0 * OCEAN_MIX) - 4.0 * side_gain
     ends = []
@@ -277,21 +334,16 @@
                 return fresh
             i = 2 * r + f
             part = lambda k: (own, (k * 2 + f) * OT * OL)
-            above = part(r - 1) if r else (up, ASIZE + f * OT * OL)
-            below = part(r + 1) if r < OR - 1 else (down, ASIZE + f * OT * OL)
+            above = part(r - 1) if r else (up, place + f * OT * OL)
+            below = part(r + 1) if r < OR - 1 else (down, place + f * OT * OL)
             ends.append(step_row(part(r), above, below, OT, OL, edge(edges, 2 * i + 1), edge(edges, 2 * i), own_gain, side_gain, OCEAN_MIX, finish))
     if not final:
         out_more[...] = edges_of(ends)
 
 
-def half_kernel(val_ref, cell_ref, out_ref, *store):
-    for f, total in enumerate(scatter_loop(val_ref, (cell_ref, *store), 32, 256, 2, stop=val_ref.shape[0] // 2)):
-        out_ref[f] = total
-
-
-def forcing_kernel(half_ref, val_ref, cell_ref, frac_ref, out_ref, gain_ref, low, high, *store):
-    for f, total in enumerate(scatter_loop(val_ref, (cell_ref, *store), 32, 256, 2, start=val_ref.shape[0] // 2)):
-        total = (HEAT_GAIN, -SALT_GAIN)[f] * (half_ref[f] + total)[: OR * OT // 2]
+def forcing_kernel(val_ref, cell_ref, frac_ref, out_ref, gain_ref, low, high, *store):
+    for f, total in enumerate(scatter_loop(val_ref, (cell_ref, *store), 32, 256, 2)):
+        total = (HEAT_GAIN, -SALT_GAIN)[f] * total[: OR * OT // 2]
         for side in range(2):
             out_ref[f, pl.ds(side, OR * OT // 2, stride=2), :] = total[:, side * LANES : (side + 1) * LANES]
         gain_ref[f] = out_ref[f] * frac_ref[...]
@@ -407,41 +459,39 @@
 
     outgoing = call(temp_kernel, "temp_gather", 9, shape(group_size, 4, LANES), table, cells, o2a_weights[0, 0], cold=(1, 2), scratch=[pltpu.VMEM((128, SPLITS * 64), BF16)])
     incoming = exchange(outgoing)
-    ocn_step = lambda *refs: ocn_kernel(False, *refs)
+    ocn_step = lambda *refs: ocn_kernel(False, ASIZE, *refs)
     ocean, ocn_edges = call(ocn_step, "ocn_step", 3, (shape(OR * OSIZE, LANES), free(OL, LANES)), ocean, up, down, beside, ocn_diff, frac, cold=(4, 5))
     incoming, ocean, ocn_edges = lax.optimization_barrier((incoming, ocean, ocn_edges))
 
     temp, flux_table = call(flux_kernel, "temp_scatter", 9, (free(AR * AT, LANES), pltpu.VMEM((128, SPLITS * 48), BF16)), incoming, cols, surface, coef, far=(1,), cold=(2, 3), in_specs=[VM, HBM, VM, VM], scratch=[pltpu.VMEM((24, LANES), F32), *store])
 
     def atm_step(low, high, up, down, beside, *more, outs=None):
-        rows = shape(ASIZE + (OSIZE if more else 0), LANES)
+        rows = shape(MESSAGE if more else ASIZE, LANES)
         outs = outs or (rows, rows, shape(AL + (OL if more else 0), LANES))
-        return call(atm_kernel, "atm_step", 2.5, outs, low, high, up, down, beside, atm_diff, coef, temp, *more, cold=(5, 6, 7, 9))
+        return call(atm_kernel, "atm_step", 2, outs, low, high, up, down, beside, atm_diff, coef, temp, *more, cold=(5, 6, 7, 9))
 
     low, high, edges = atm_step(low, high, up, down, beside, ocean, ocn_edges)
+    beside = partner(edges)
+    message = shape(MESSAGE, LANES)
+    low, high = call(beside_kernel, "beside", 1, (message, message), low, high, beside, in_specs=[ANY] * 3, out_specs=(ANY, ANY), scratch=[pltpu.SemaphoreType.DMA((2,))], input_output_aliases={0: 0, 1: 1})
     up, down = row_halos(low, high)
-    beside = partner(edges)
     flux_table, low, high = lax.optimization_barrier((flux_table, low, high))
 
     outgoing = call(send_kernel, "flux_gather", 9, shape(group_size, 8, LANES), flux_table, cols, a2o_weights[0, 0], cold=(1, 2))
     incoming = exchange(outgoing)
-    outgoing, up, down, beside = lax.optimization_barrier((outgoing, up, down, beside))
-    low, high, edges = atm_step(low, high, up, down, beside)
-    ocn_last_step = lambda *refs: ocn_kernel(True, *refs)
+    outgoing, up, down = lax.optimization_barrier((outgoing, up, down))
+    row = shape(ASIZE, LANES)
+    low, high, near, far, edges = call(wide_kernel, "atm_wide", 3, (row, row, row, row, shape(AL, LANES)), low, up, down, beside, atm_diff, coef, temp, cold=(4, 5, 6))
+    side = partner(edges)
+    ocn_last_step = lambda *refs: ocn_kernel(True, 2 * ASIZE, *refs)
     ocean, top = call(ocn_last_step, "ocn_step", 3, (jax.ShapeDtypeStruct(ocn_state.shape, F32), free(2, 2, OR, OT * LANES)), ocean, up, down, beside, ocn_diff, frac, cold=(4, 5))
+    low, high, edges = atm_step(low, high, near, far, side)
     up, down = row_halos(low, high)
     beside = partner(edges)
     incoming, ocean, top, low, high = lax.optimization_barrier((incoming, ocean, top, low, high))
 
-    half = call(half_kernel, "forcing_half", 7.5, shape(2, 32, 256), incoming, cells, far=(1,), in_specs=[VM, HBM], scratch=store)
-    half, up, down, beside = lax.optimization_barrier((half, up, down, beside))
-    low, high, edges = atm_step(low, high, up, down, beside)
-    up, down = row_halos(low, high)
-    beside = partner(edges)
-    half, low, high = lax.optimization_barrier((half, low, high))
-
     every = shape(2, OR * OT, LANES)
-    forcing, gained, first, last = call(forcing_kernel, "forcing_scatter", 7.5, (every, every, shape(2, OT, LANES), shape(2, OT, LANES)), half, incoming, cells, frac, far=(2,), cold=(3,), in_specs=[VM, VM, HBM, VM], scratch=store)
+    forcing, gained, first, last = call(forcing_kernel, "forcing_scatter", 13, (every, every, shape(2, OT, LANES), shape(2, OT, LANES)), incoming, cells, frac, far=(1,), cold=(2,), in_specs=[VM, HBM, VM], scratch=store)
     above, below = row_halos(first, last)
     side = partner(gained)
     forcing, up, down, beside = lax.optimization_barrier((forcing, up, down, beside))

time: 131 us -> 145 us (1.11)
  waiting for transfers between devices: 15.5 us -> 28.2 us
    ppermute x5 -> x4, waiting for transfers between devices: 7.2 us -> 19.9 us  [row_halos(): lax.ppermute(last, GROUP, up)]
    ppermute x5 -> x4, starting transfers between devices: 21.8 us -> 29.6 us  [row_halos(): lax.ppermute(first, GROUP, [(b, a) for a, b in up])]
    all_to_all x2, starting transfers between devices: 17.3 us -> 14.2 us  [exchange(): lax.all_to_all(values, GROUP, split_axis=0, concat_axis=0, tiled=True)]
    ppermute x5, starting transfers between devices: 9.98 us -> 7.82 us  [partner(): lax.ppermute(edges, 'lev', [(i, (i + 1) % count) for i in range(count)])]
    ppermute x5 -> x4, starting transfers between devices: 4.81 us -> 3.07 us  [row_halos(): lax.ppermute(last, GROUP, up)]
    unnamed x40 -> x32, local copies, waits for them, and re-layouts: 3.18 us -> 3.9 us
  transfers between devices with their start and end apart: 17 -> 15, of which waited for: 4 -> 4; matrix products, arithmetic and copies ran while one was open for 0% -> 0% of each run, Pallas kernels for 30% -> 28%
where the time goes in v6:
time: 145 us; the launch traced here: 144 us
  Pallas kernels  56.5 us (39%)
  starting transfers between devices  54.7 us (38%)
  waiting for transfers between devices  28.2 us (19%)
  local copies, waits for them, and re-layouts  3.9 us (3%)
    pallas_call x13, Pallas kernels, call(): pl.pallas_call(kernel, out_shape=out_shape, scratch_shapes=list(scratch),...  56.5 us
    ppermute x4, starting transfers between devices, row_halos(): lax.ppermute(first, GROUP, [(b, a) for a, b in up])  29.6 us
    ppermute x4, waiting for transfers between devices, row_halos(): lax.ppermute(last, GROUP, up)  19.9 us
    all_to_all x2, starting transfers between devices, exchange(): lax.all_to_all(values, GROUP, split_axis=0, concat_axis=0, tiled=True)  14.2 us
    ppermute x5, starting transfers between devices, partner(): lax.ppermute(edges, 'lev', [(i, (i + 1) % count) for i in range(count)])  7.82 us
    all_to_all x2, waiting for transfers between devices, exchange(): lax.all_to_all(values, GROUP, split_axis=0, concat_axis=0, tiled=True)  6.56 us
    unnamed x32, local copies, waits for them, and re-layouts  3.9 us
    ppermute x4, starting transfers between devices, row_halos(): lax.ppermute(last, GROUP, up)  3.07 us
  transfers between devices with their start and end apart: 15, of which 4 were waited for; matrix products, arithmetic and copies ran while one was open for 0% of the time, Pallas kernels for 28%

profile of v6, /device:TPU:1, one launch (start us, length us, event | category | flops | bytes accessed | tf_op | source)
XLA Modules:
  0.0 144.4 jit_solution(9250532652469566639)
XLA Ops:
  0.7 4.7 %prep.1 = (f32[1536,128]{1,0:T(8,128)S(1)}, f32[1536,128]{1,0:T(8,128)S(1)}, f32[72,128]{1,0:T(8,128)S(1)}, f32[2688,128]{1,0:T(8,128)}, f32[56,128]{1,0:T(8,128...) custom-call(f32[2,48,2,1152]{3,2,1,0:T(2,128)} %atm_hbm.1, ...), custom_call_target="tpu_custom_call" | custom-call | flops 3300000000 | bytes 9000000 | tf_op jit(solution)/shard_map/prep/pallas_call | solution.py:398
  5.3 2.5 %collective-permute-start = (f32[1536,128]{1,0:T(8,128)S(1)}, f32[1536,128]{1,0:T(8,128)S(1)}, u32[]{:S(2)}, u32[]{:S(2)}) collective-permute-start(f32[1536,128]{1,0:T(8,128)S(1)} %get-tuple-element.53.high), channel_id=1, source_target_pairs={{0,2},{2,4},{4,6},{6,8},{8,10},{10,12},{12,14},{14,16},{16,18},{18... | collective-permute-start | bytes 2359304 | tf_op jit(solution)/shard_map/ppermute | solution.py:412
  7.9 8.7 %collective-permute-start.1 = (f32[1536,128]{1,0:T(8,128)S(1)}, f32[1536,128]{1,0:T(8,128)S(1)}, u32[]{:S(2)}, u32[]{:S(2)}) collective-permute-start(f32[1536,128]{1,0:T(8,128)S(1)} %get-tuple-element.54.low), channel_id=1, source_target_pairs={{2,0},{4,2},{6,4},{8,6},{10,8},{12,10},{14,12},{16,14},{18,16},{20... | collective-permute-start | bytes 2359304 | tf_op jit(solution)/shard_map/ppermute | solution.py:412
  16.6 8.7 %temp_gather.1 = f32[128,4,128]{2,1,0:T(4,128)} custom-call(f32[64,128]{1,0:T(8,128)S(1)} %get-tuple-element.51.table_ref, s32[128,512]{1,0:T(8,128)S(1)} %bitcast.11, f32[128,512]{1,0:T(8,128)S(1)} %bitcast.6), custom_call_target="tpu_custom_call" | custom-call | flops 9900000256 | bytes 27000000 | tf_op jit(solution)/shard_map/temp_gather/pallas_call | solution.py:398
  25.2 7.9 %all-to-all-start = ((f32[128,4,128]{2,1,0:T(4,128)}), f32[128,4,128]{2,1,0:T(4,128)S(1)}, u32[]{:S(2)}, u32[]{:S(2)}) async-start(f32[128,4,128]{2,1,0:T(4,128)} %temp_gather.1), calls=%async_computation | async-start | bytes 524288 | tf_op jit(solution)/shard_map/all_to_all | solution.py:421
  33.1 1.6 %collective-permute-start.2 = (f32[72,128]{1,0:T(8,128)S(1)}, f32[72,128]{1,0:T(8,128)S(1)}, u32[]{:S(2)}, u32[]{:S(2)}) collective-permute-start(f32[72,128]{1,0:T(8,128)S(1)} %get-tuple-element.55), channel_id=1, source_target_pairs={{0,1},{1,0},{2,3},{3,2},{4,5},{5,4},{6,7},{7,6},{8,9},{9,8},{10,11... | collective-permute-start | bytes 110600 | tf_op jit(solution)/shard_map/ppermute | solution.py:417
  35.6 1.3 copy-done.9
  37.0 1.5 %ocn_step.2 = (f32[2688,128]{1,0:T(8,128)S(1)}, f32[24,128]{1,0:T(8,128)}) custom-call(f32[2688,128]{1,0:T(8,128)S(1)} %copy-done.9, f32[1536,128]{1,0:T(8,128)S(1)} %collective-permute-done.refs_1_.up, f32[1536,128]{1,0:T(8,128)S(1)} %collective-permute-done.1.refs_2_.down, f32[72,128]{1,0:T(8,128)S(1)} %collective-permute-done.2.refs_3_.edges_ref, ...), custom_call_target="tpu_custom_call" | custom-call | flops 3300000000 | bytes 9000000 | tf_op jit(solution)/shard_map/ocn_step/pallas_call | solution.py:398
  38.5 1.1 copy-done.5
  39.6 6.6 %all-to-all-done.val_ref = f32[128,4,128]{2,1,0:T(4,128)S(1)} async-done(((f32[128,4,128]{2,1,0:T(4,128)}), f32[128,4,128]{2,1,0:T(4,128)S(1)}, u32[]{:S(2)}, u32[]{:S(2)}) %all-to-all-start) | async-done | bytes 262176 | tf_op jit(solution)/shard_map/all_to_all | solution.py:421
  46.9 8.5 %temp_scatter.1 = (f32[18,128]{1,0:T(8,128)}, bf16[128,144]{1,0:T(8,128)(2,1)S(1)}) custom-call(f32[128,4,128]{2,1,0:T(4,128)S(1)} %all-to-all-done.val_ref, s32[128,512]{1,0:T(8,128)} %bitcast.7, f32[2,18,128]{2,1,0:T(8,128)S(1)} %copy-done.15, f32[2,18,128]{2,1,0:T(8,128)S(1)} %copy-done.11), custom_call_target="tpu_custom_call" | custom-call | flops 9900000256 | bytes 27000000 | tf_op jit(solution)/shard_map/temp_scatter/pallas_call | solution.py:398
  56.1 2.1 %atm_step.3 = (f32[2504,128]{1,0:T(8,128)}, f32[2504,128]{1,0:T(8,128)}, f32[72,128]{1,0:T(8,128)S(1)}) custom-call(f32[1536,128]{1,0:T(8,128)S(1)} %get-tuple-element.54.low, f32[1536,128]{1,0:T(8,128)S(1)} %get-tuple-element.53.high, f32[1536,128]{1,0:T(8,128)S(1)} %collective-permute-done.refs_1_.up, f32[1536,128]{1,0:T(8,128)S(1)} %collective-permute-done.1.refs_2_.down, ...), custom_call_target="tpu_custom_call" | custom-call | flops 2200000000 | bytes 6000000 | tf_op jit(solution)/shard_map/atm_step/pallas_call | solution.py:398
  58.2 3.0 %collective-permute-start.3 = (f32[72,128]{1,0:T(8,128)S(1)}, f32[72,128]{1,0:T(8,128)S(1)}, u32[]{:S(2)}, u32[]{:S(2)}) collective-permute-start(f32[72,128]{1,0:T(8,128)S(1)} %get-tuple-element.70), channel_id=1, source_target_pairs={{0,1},{1,0},{2,3},{3,2},{4,5},{5,4},{6,7},{7,6},{8,9},{9,8},{10,11... | collective-permute-start | bytes 110600 | tf_op jit(solution)/shard_map/ppermute | solution.py:417
  63.1 6.6 %collective-permute-start.5 = (f32[2504,128]{1,0:T(8,128)}, f32[2504,128]{1,0:T(8,128)S(1)}, u32[]{:S(2)}, u32[]{:S(2)}) collective-permute-start(f32[2504,128]{1,0:T(8,128)} %get-tuple-element.78.own), channel_id=1, source_target_pairs={{2,0},{4,2},{6,4},{8,6},{10,8},{12,10},{14,12},{16,14},{18,16},{20... | collective-permute-start | bytes 3846152 | tf_op jit(solution)/shard_map/ppermute | solution.py:412
  69.8 8.8 %flux_gather.1 = f32[128,8,128]{2,1,0:T(8,128)} custom-call(bf16[128,144]{1,0:T(8,128)(2,1)S(1)} %get-tuple-element.73.t_ref, s32[128,512]{1,0:T(8,128)S(1)} %bitcast.8, f32[128,512]{1,0:T(8,128)S(1)} %bitcast.9), custom_call_target="tpu_custom_call" | custom-call | flops 9900000256 | bytes 27000000 | tf_op jit(solution)/shard_map/flux_gather/pallas_call | solution.py:398
  78.6 6.4 %all-to-all-start.1 = ((f32[128,8,128]{2,1,0:T(8,128)}), f32[128,8,128]{2,1,0:T(8,128)S(1)}, u32[]{:S(2)}, u32[]{:S(2)}) async-start(f32[128,8,128]{2,1,0:T(8,128)} %flux_gather.1), calls=%async_computation.1 | async-start | bytes 1048576 | tf_op jit(solution)/shard_map/all_to_all | solution.py:421
  85.0 19.9 %collective-permute-done.4.refs_1_.up = f32[2504,128]{1,0:T(8,128)S(1)} collective-permute-done((f32[2504,128]{1,0:T(8,128)}, f32[2504,128]{1,0:T(8,128)S(1)}, u32[]{:S(2)}, u32[]{:S(2)}) %collective-permute-start.4) | collective-permute-done | bytes 1282080 | tf_op jit(solution)/shard_map/ppermute | solution.py:412
  104.9 2.5 %atm_wide.1 = (f32[864,128]{1,0:T(8,128)S(1)}, f32[864,128]{1,0:T(8,128)S(1)}, f32[864,128]{1,0:T(8,128)S(1)}, f32[864,128]{1,0:T(8,128)S(1)}, f32[48,128]{1,0:T(8,128)S(1)}) custom-call(f32[2504,128]{1,0:T(8,128)} %get-tuple-element.78.own, f32[2504,128]{1,0:T(8,128)S(1)} %collective-permute-done.4.refs_1_.up, ...), custom_call_target="tpu_custom_call" | custom-call | flops 3300000000 | bytes 9000000 | tf_op jit(solution)/shard_map/atm_wide/pallas_call | solution.py:398
  107.5 2.1 %collective-permute-start.6 = (f32[48,128]{1,0:T(8,128)S(1)}, f32[48,128]{1,0:T(8,128)S(1)}, u32[]{:S(2)}, u32[]{:S(2)}) collective-permute-start(f32[48,128]{1,0:T(8,128)S(1)} %get-tuple-element.83), channel_id=1, source_target_pairs={{0,1},{1,0},{2,3},{3,2},{4,5},{5,4},{6,7},{7,6},{8,9},{9,8},{10,11... | collective-permute-start | bytes 73736 | tf_op jit(solution)/shard_map/ppermute | solution.py:417
  109.6 2.7 %ocn_step.3 = (f32[2,24,4,1792]{3,2,1,0:T(4,128)}, f32[2,2,4,1792]{3,2,1,0:T(4,128)}) custom-call(f32[2688,128]{1,0:T(8,128)S(1)} %copy-done.7, f32[2504,128]{1,0:T(8,128)S(1)} %collective-permute-done.4.refs_1_.up, f32[2504,128]{1,0:T(8,128)S(1)} %collective-permute-done.5.refs_2_.down, f32[72,128]{1,0:T(8,128)S(1)} %collective-permute-done.3.beside.refs_3_.edges_ref, ...), custom_call_target="tpu_custom_call" | custom-call | flops 3300000000 | bytes 9000000 | tf_op jit(solution)/shard_map/ocn_step/pallas_call | solution.py:398
  113.1 7.5 %collective-permute-start.8 = (f32[864,128]{1,0:T(8,128)S(1)}, f32[864,128]{1,0:T(8,128)S(1)}, u32[]{:S(2)}, u32[]{:S(2)}) collective-permute-start(f32[864,128]{1,0:T(8,128)S(1)} %get-tuple-element.86.low), channel_id=1, source_target_pairs={{2,0},{4,2},{6,4},{8,6},{10,8},{12,10},{14,12},{16,14},{18,16},{20... | collective-permute-start | bytes 1327112 | tf_op jit(solution)/shard_map/ppermute | solution.py:412
  120.8 12.9 %forcing_scatter.1 = (f32[2,56,128]{2,1,0:T(8,128)S(1)}, f32[2,56,128]{2,1,0:T(8,128)S(1)}, f32[2,14,128]{2,1,0:T(8,128)S(1)}, f32[2,14,128]{2,1,0:T(8,128)S(1)}) custom-call(f32[128,8,128]{2,1,0:T(8,128)S(1)} %all-to-all-done.1.val_ref, s32[128,512]{1,0:T(8,128)} %bitcast.10, f32[56,128]{1,0:T(8,128)S(1)} %copy-done.8), custom_call_target="tpu_custom_call" | custom-call | flops 14300000256 | bytes 39000000 | tf_op jit(solution)/shard_map/forcing_scatter/pallas_call | solution.py:398
  133.8 6.9 %collective-permute-start.11 = (f32[2,14,128]{2,1,0:T(8,128)S(1)}, f32[2,14,128]{2,1,0:T(8,128)S(1)}, u32[]{:S(2)}, u32[]{:S(2)}) collective-permute-start(f32[2,14,128]{2,1,0:T(8,128)S(1)} %get-tuple-element.99), channel_id=1, source_target_pairs={{2,0},{4,2},{6,4},{8,6},{10,8},{12,10},{14,12},{16,14},{18,16},{20... | collective-permute-start | bytes 43016 | tf_op jit(solution)/shard_map/ppermute | solution.py:412
  141.5 1.9 %atm_step.5 = f32[2,48,2,1152]{3,2,1,0:T(2,128)} custom-call(f32[864,128]{1,0:T(8,128)S(1)} %get-tuple-element.86.low, f32[864,128]{1,0:T(8,128)S(1)} %get-tuple-element.87.high, f32[864,128]{1,0:T(8,128)S(1)} %collective-permute-done.7.up, f32[864,128]{1,0:T(8,128)S(1)} %collective-permute-done.8.down, f32[48,128]{1,0:T(8,128)S(1)} %collective-permute-done.9.edges_ref, ...), custom_call_target="tpu_custom_call" | custom-call | flops 2200000000 | bytes 6000000 | tf_op jit(solution)/shard_map/atm_step/pallas_call | solution.py:398
  (51 shorter events, 7.1 us)
Async XLA Ops:
  0.6 15.9 %copy-start = (f32[1,1,128,512]{3,2,1,0:T(8,128)S(1)}, f32[1,1,128,512]{3,2,1,0:T(8,128)}, u32[]{:S(2)}) copy-start(f32[1,1,128,512]{3,2,1,0:T(8,128)} %param.19) | copy-start | bytes 786436
  0.6 15.9 %copy-start.3 = (s32[1,1,128,512]{3,2,1,0:T(8,128)S(1)}, s32[1,1,128,512]{3,2,1,0:T(8,128)}, u32[]{:S(2)}) copy-start(s32[1,1,128,512]{3,2,1,0:T(8,128)} %param.18) | copy-start | bytes 786436
  5.3 30.3 %collective-permute-start = (f32[1536,128]{1,0:T(8,128)S(1)}, f32[1536,128]{1,0:T(8,128)S(1)}, u32[]{:S(2)}, u32[]{:S(2)}) collective-permute-start(f32[1536,128]{1,0:T(8,128)S(1)} %get-tuple-element.53.high), channel_id=1, source_target_pairs={{0,2},{2,4},{4,6},{6,8},{8,10},{10,12},{12,14},{14,16},{16,18},{18... | collective-permute-start | bytes 2359304 | tf_op jit(solution)/shard_map/ppermute | solution.py:412
  7.9 27.7 %collective-permute-start.1 = (f32[1536,128]{1,0:T(8,128)S(1)}, f32[1536,128]{1,0:T(8,128)S(1)}, u32[]{:S(2)}, u32[]{:S(2)}) collective-permute-start(f32[1536,128]{1,0:T(8,128)S(1)} %get-tuple-element.54.low), channel_id=1, source_target_pairs={{2,0},{4,2},{6,4},{8,6},{10,8},{12,10},{14,12},{16,14},{18,16},{20... | collective-permute-start | bytes 2359304 | tf_op jit(solution)/shard_map/ppermute | solution.py:412
  16.6 19.1 %copy-start.8 = (f32[56,128]{1,0:T(8,128)S(1)}, f32[56,128]{1,0:T(8,128)}, u32[]{:S(2)}) copy-start(f32[56,128]{1,0:T(8,128)} %get-tuple-element.57.refs_5_.frac_ref) | copy-start | bytes 86020
  16.6 19.1 %copy-start.10 = (f32[24,128]{1,0:T(8,128)S(1)}, f32[24,128]{1,0:T(8,128)}, u32[]{:S(2)}) copy-start(f32[24,128]{1,0:T(8,128)} %get-tuple-element.56.refs_4_.diff_ref) | copy-start | bytes 36868
  25.2 20.9 %all-to-all-start = ((f32[128,4,128]{2,1,0:T(4,128)}), f32[128,4,128]{2,1,0:T(4,128)S(1)}, u32[]{:S(2)}, u32[]{:S(2)}) async-start(f32[128,4,128]{2,1,0:T(4,128)} %temp_gather.1), calls=%async_computation | async-start | bytes 524288 | tf_op jit(solution)/shard_map/all_to_all | solution.py:421
  33.1 2.5 %collective-permute-start.2 = (f32[72,128]{1,0:T(8,128)S(1)}, f32[72,128]{1,0:T(8,128)S(1)}, u32[]{:S(2)}, u32[]{:S(2)}) collective-permute-start(f32[72,128]{1,0:T(8,128)S(1)} %get-tuple-element.55), channel_id=1, source_target_pairs={{0,1},{1,0},{2,3},{3,2},{4,5},{5,4},{6,7},{7,6},{8,9},{9,8},{10,11... | collective-permute-start | bytes 110600 | tf_op jit(solution)/shard_map/ppermute | solution.py:417
  37.0 9.2 %copy-start.11 = (f32[2,18,128]{2,1,0:T(8,128)S(1)}, f32[2,18,128]{2,1,0:T(8,128)}, u32[]{:S(2)}) copy-start(f32[2,18,128]{2,1,0:T(8,128)} %get-tuple-element.62.coef_ref) | copy-start | bytes 55300
  46.9 8.5 %copy-start.6 = (f32[2688,128]{1,0:T(8,128)S(1)}, f32[2688,128]{1,0:T(8,128)}, u32[]{:S(2)}) copy-start(f32[2688,128]{1,0:T(8,128)} %copy-done.5) | copy-start | bytes 4128772
  46.9 8.5 %copy-start.12 = (f32[48,128]{1,0:T(8,128)S(1)}, f32[48,128]{1,0:T(8,128)}, u32[]{:S(2)}) copy-start(f32[48,128]{1,0:T(8,128)} %get-tuple-element.64.diff_ref) | copy-start | bytes 73732
  46.9 8.5 %copy-start.14 = (f32[24,128]{1,0:T(8,128)S(1)}, f32[24,128]{1,0:T(8,128)}, u32[]{:S(2)}) copy-start(f32[24,128]{1,0:T(8,128)} %get-tuple-element.67.rest_1_) | copy-start | bytes 36868
  58.2 3.9 %collective-permute-start.3 = (f32[72,128]{1,0:T(8,128)S(1)}, f32[72,128]{1,0:T(8,128)S(1)}, u32[]{:S(2)}, u32[]{:S(2)}) collective-permute-start(f32[72,128]{1,0:T(8,128)S(1)} %get-tuple-element.70), channel_id=1, source_target_pairs={{0,1},{1,0},{2,3},{3,2},{4,5},{5,4},{6,7},{7,6},{8,9},{9,8},{10,11... | collective-permute-start | bytes 110600 | tf_op jit(solution)/shard_map/ppermute | solution.py:417
  62.8 42.1 %collective-permute-start.4 = (f32[2504,128]{1,0:T(8,128)}, f32[2504,128]{1,0:T(8,128)S(1)}, u32[]{:S(2)}, u32[]{:S(2)}) collective-permute-start(f32[2504,128]{1,0:T(8,128)} %get-tuple-element.72), channel_id=1, source_target_pairs={{0,2},{2,4},{4,6},{6,8},{8,10},{10,12},{12,14},{14,16},{16,18},{18... | collective-permute-start | bytes 3846152 | tf_op jit(solution)/shard_map/ppermute | solution.py:412
  63.1 41.8 %collective-permute-start.5 = (f32[2504,128]{1,0:T(8,128)}, f32[2504,128]{1,0:T(8,128)S(1)}, u32[]{:S(2)}, u32[]{:S(2)}) collective-permute-start(f32[2504,128]{1,0:T(8,128)} %get-tuple-element.78.own), channel_id=1, source_target_pairs={{2,0},{4,2},{6,4},{8,6},{10,8},{12,10},{14,12},{16,14},{18,16},{20... | collective-permute-start | bytes 3846152 | tf_op jit(solution)/shard_map/ppermute | solution.py:412
  78.6 41.9 %all-to-all-start.1 = ((f32[128,8,128]{2,1,0:T(8,128)}), f32[128,8,128]{2,1,0:T(8,128)S(1)}, u32[]{:S(2)}, u32[]{:S(2)}) async-start(f32[128,8,128]{2,1,0:T(8,128)} %flux_gather.1), calls=%async_computation.1 | async-start | bytes 1048576 | tf_op jit(solution)/shard_map/all_to_all | solution.py:421
  85.0 24.6 %copy-start.7 = (f32[2688,128]{1,0:T(8,128)S(1)}, f32[2688,128]{1,0:T(8,128)}, u32[]{:S(2)}) copy-start(f32[2688,128]{1,0:T(8,128)} %copy-done.5) | copy-start | bytes 4128772
  107.5 4.8 %collective-permute-start.6 = (f32[48,128]{1,0:T(8,128)S(1)}, f32[48,128]{1,0:T(8,128)S(1)}, u32[]{:S(2)}, u32[]{:S(2)}) collective-permute-start(f32[48,128]{1,0:T(8,128)S(1)} %get-tuple-element.83), channel_id=1, source_target_pairs={{0,1},{1,0},{2,3},{3,2},{4,5},{5,4},{6,7},{7,6},{8,9},{9,8},{10,11... | collective-permute-start | bytes 73736 | tf_op jit(solution)/shard_map/ppermute | solution.py:417
  113.0 28.5 %collective-permute-start.7 = (f32[864,128]{1,0:T(8,128)S(1)}, f32[864,128]{1,0:T(8,128)S(1)}, u32[]{:S(2)}, u32[]{:S(2)}) collective-permute-start(f32[864,128]{1,0:T(8,128)S(1)} %get-tuple-element.87.high), channel_id=1, source_target_pairs={{0,2},{2,4},{4,6},{6,8},{8,10},{10,12},{12,14},{14,16},{16,18},{18... | collective-permute-start | bytes 1327112 | tf_op jit(solution)/shard_map/ppermute | solution.py:412
  113.1 28.4 %collective-permute-start.8 = (f32[864,128]{1,0:T(8,128)S(1)}, f32[864,128]{1,0:T(8,128)S(1)}, u32[]{:S(2)}, u32[]{:S(2)}) collective-permute-start(f32[864,128]{1,0:T(8,128)S(1)} %get-tuple-element.86.low), channel_id=1, source_target_pairs={{2,0},{4,2},{6,4},{8,6},{10,8},{12,10},{14,12},{16,14},{18,16},{20... | collective-permute-start | bytes 1327112 | tf_op jit(solution)/shard_map/ppermute | solution.py:412
  120.5 20.2 %collective-permute-start.9 = (f32[48,128]{1,0:T(8,128)S(1)}, f32[48,128]{1,0:T(8,128)S(1)}, u32[]{:S(2)}, u32[]{:S(2)}) collective-permute-start(f32[48,128]{1,0:T(8,128)S(1)} %get-tuple-element.90), channel_id=1, source_target_pairs={{0,1},{1,0},{2,3},{3,2},{4,5},{5,4},{6,7},{7,6},{8,9},{9,8},{10,11... | collective-permute-start | bytes 73736 | tf_op jit(solution)/shard_map/ppermute | solution.py:417
  133.7 9.7 %collective-permute-start.10 = (f32[2,14,128]{2,1,0:T(8,128)S(1)}, f32[2,14,128]{2,1,0:T(8,128)S(1)}, u32[]{:S(2)}, u32[]{:S(2)}) collective-permute-start(f32[2,14,128]{2,1,0:T(8,128)S(1)} %get-tuple-element.98), channel_id=1, source_target_pairs={{0,2},{2,4},{4,6},{6,8},{8,10},{10,12},{12,14},{14,16},{16,18},{18... | collective-permute-start | bytes 43016 | tf_op jit(solution)/shard_map/ppermute | solution.py:412
  133.8 9.6 %collective-permute-start.11 = (f32[2,14,128]{2,1,0:T(8,128)S(1)}, f32[2,14,128]{2,1,0:T(8,128)S(1)}, u32[]{:S(2)}, u32[]{:S(2)}) collective-permute-start(f32[2,14,128]{2,1,0:T(8,128)S(1)} %get-tuple-element.99), channel_id=1, source_target_pairs={{2,0},{4,2},{6,4},{8,6},{10,8},{12,10},{14,12},{16,14},{18,16},{20... | collective-permute-start | bytes 43016 | tf_op jit(solution)/shard_map/ppermute | solution.py:412
  140.7 2.7 %collective-permute-start.12 = (f32[2,56,128]{2,1,0:T(8,128)S(1)}, f32[2,56,128]{2,1,0:T(8,128)S(1)}, u32[]{:S(2)}, u32[]{:S(2)}) collective-permute-start(f32[2,56,128]{2,1,0:T(8,128)S(1)} %get-tuple-element.97.gain_ref), channel_id=1, source_target_pairs={{0,1},{1,0},{2,3},{3,2},{4,5},{5,4},{6,7},{7,6},{8,9},{9,8},{10,11... | collective-permute-start | bytes 172040 | tf_op jit(solution)/shard_map/ppermute | solution.py:417
  (7 other events, 21.1 us)

commit v7 on v4

--- a/solution.py
+++ b/solution.py
@@ -110,21 +110,48 @@
     temp = temp[: AR * AT]
     temp_ref[...] = temp
     flux_ref[...] = jnp.zeros_like(flux_ref)
-    tables = []
+    blank = jnp.zeros((64, 40), F32)
     for f in range(2):
-        flux_ref[: AR * AT, :] = coef_ref[f] * (state_ref[f] - (1.0, MOIST_RATIO)[f] * temp)
-        flux = flux_ref[...]
-        halves = jnp.concatenate([flux[:, :64], flux[:, 64:]], axis=0)
-        tables.append(jnp.concatenate(parts_of(halves.T), axis=1))
-    t_ref[...] = jnp.concatenate(tables, axis=0)
-
-
-def half_split(i):
-    return (i >> 7) + 24 * ((i >> 6) & 1), i & 63
+        flux = coef_ref[f] * (state_ref[f] - (1.0, MOIST_RATIO)[f] * temp)
+        flux_ref[: AR * AT, :] = flux
+        flux_ref[AR * AT : 2 * AR * AT, :] = pltpu.roll(flux, 64, 1)
+        parts = [p.astype(F32) for p in parts_of(flux_ref[:, :64].T)]
+        for e in range(2):
+            pieces = [x for p in parts for x in ((p, blank), (blank, p))[e]]
+            line = 128 * e + 64 * f
+            t_ref[line : line + 64, :] = jnp.concatenate(pieces, axis=1).astype(BF16)
+
+
+def pair_hot(a, b):
+    a, b = spread(a), spread(b)
+    line = lax.broadcasted_iota(jnp.int32, a.shape, 0).astype(F32)
+    early = line < 8.0
+    mixed = jnp.where(early, a.astype(F32), b.astype(F32)).astype(BF16)
+    targets = (line, line + 16.0, jnp.where(early, line + 32.0, line - 8.0), line + 8.0, line + 24.0)
+    one, zero = jnp.ones(a.shape, BF16), jnp.zeros(a.shape, BF16)
+    return jnp.concatenate([jnp.where(v == t.astype(BF16), one, zero) for v, t in zip((a, a, mixed, b, b), targets)], axis=0)
 
 
 def send_kernel(t_ref, col_ref, w_ref, out_ref):
-    gather_loop(t_ref, col_ref, w_ref, out_ref, half_split, 48, 64, 2)
+    def group(g, c):
+        base = pl.multiple_of(g * 8, 8)
+        place = col_ref[pl.ds(base, 8), :]
+        hi, lo = (place >> 7) + 18 * ((place >> 6) & 1), place & 63
+        w = w_ref[pl.ds(base, 8), :]
+        for r in range(0, 8, 2):
+            hot = jnp.concatenate([pair_hot(hi[r : r + 1], hi[r + 1 : r + 2])] * SPLITS, axis=0)
+            o = jnp.dot(t_ref[...], hot, preferred_element_type=F32)
+            lines = lax.broadcasted_iota(jnp.int32, (64, o.shape[1]), 0)
+            for e in range(2):
+                at = r + e
+                mine = lines == lo[at : at + 1]
+                for f in range(2):
+                    block = 128 * e + 64 * f
+                    value = jnp.sum(jnp.where(mine, o[block : block + 64], 0.0), axis=0, keepdims=True) * w[at : at + 1]
+                    for q in range(4):
+                        out_ref[base + at, 4 * f + q : 4 * f + q + 1, :] = value[:, q * 128 : (q + 1) * 128]
+        return c
+    lax.fori_loop(0, col_ref.shape[0] // 8, group, 0)
 
 
 def shifted_levels(ref, base, levels, tile):
@@ -285,12 +312,12 @@
 
 
 def half_kernel(val_ref, cell_ref, out_ref, *store):
-    for f, total in enumerate(scatter_loop(val_ref, (cell_ref, *store), 32, 256, 2, stop=val_ref.shape[0] // 2)):
+    for f, total in enumerate(scatter_loop(val_ref, (cell_ref, *store), 32, 256, 2, stop=88)):
         out_ref[f] = total
 
 
 def forcing_kernel(half_ref, val_ref, cell_ref, frac_ref, out_ref, gain_ref, low, high, *store):
-    for f, total in enumerate(scatter_loop(val_ref, (cell_ref, *store), 32, 256, 2, start=val_ref.shape[0] // 2)):
+    for f, total in enumerate(scatter_loop(val_ref, (cell_ref, *store), 32, 256, 2, start=88)):
         total = (HEAT_GAIN, -SALT_GAIN)[f] * (half_ref[f] + total)[: OR * OT // 2]
         for side in range(2):
             out_ref[f, pl.ds(side, OR * OT // 2, stride=2), :] = total[:, side * LANES : (side + 1) * LANES]
@@ -411,7 +438,7 @@
     ocean, ocn_edges = call(ocn_step, "ocn_step", 3, (shape(OR * OSIZE, LANES), free(OL, LANES)), ocean, up, down, beside, ocn_diff, frac, cold=(4, 5))
     incoming, ocean, ocn_edges = lax.optimization_barrier((incoming, ocean, ocn_edges))
 
-    temp, flux_table = call(flux_kernel, "temp_scatter", 9, (free(AR * AT, LANES), pltpu.VMEM((128, SPLITS * 48), BF16)), incoming, cols, surface, coef, far=(1,), cold=(2, 3), in_specs=[VM, HBM, VM, VM], scratch=[pltpu.VMEM((24, LANES), F32), *store])
+    temp, flux_table = call(flux_kernel, "temp_scatter", 9, (free(AR * AT, LANES), pltpu.VMEM((256, SPLITS * 80), BF16)), incoming, cols, surface, coef, far=(1,), cold=(2, 3), in_specs=[VM, HBM, VM, VM], scratch=[pltpu.VMEM((40, LANES), F32), *store])
 
     def atm_step(low, high, up, down, beside, *more, outs=None):
         rows = shape(ASIZE + (OSIZE if more else 0), LANES)

time: 131 us -> 132 us (level)
    ppermute x5, starting transfers between devices: 21.8 us -> 23.6 us  [row_halos(): lax.ppermute(first, GROUP, [(b, a) for a, b in up])]
  transfers between devices with their start and end apart: 17 -> 17, of which waited for: 4 -> 5; matrix products, arithmetic and copies ran while one was open for 0% -> 0% of each run, Pallas kernels for 30% -> 30%
where the time goes in v7:
time: 132 us; the launch traced here: 131 us
  Pallas kernels  57.1 us (43%)
  starting transfers between devices  53.9 us (41%)
  waiting for transfers between devices  15.8 us (12%)
  local copies, waits for them, and re-layouts  3.18 us (2%)
    pallas_call x13, Pallas kernels, call(): pl.pallas_call(kernel, out_shape=out_shape, scratch_shapes=list(scratch),...  57.1 us
    ppermute x5, starting transfers between devices, row_halos(): lax.ppermute(first, GROUP, [(b, a) for a, b in up])  23.6 us
    all_to_all x2, starting transfers between devices, exchange(): lax.all_to_all(values, GROUP, split_axis=0, concat_axis=0, tiled=True)  17.3 us
    ppermute x5, starting transfers between devices, partner(): lax.ppermute(edges, 'lev', [(i, (i + 1) % count) for i in range(count)])  9.45 us
    ppermute x5, waiting for transfers between devices, row_halos(): lax.ppermute(last, GROUP, up)  7.47 us
    all_to_all x2, waiting for transfers between devices, exchange(): lax.all_to_all(values, GROUP, split_axis=0, concat_axis=0, tiled=True)  6.56 us
    ppermute x5, starting transfers between devices, row_halos(): lax.ppermute(last, GROUP, up)  3.57 us
    unnamed x40, local copies, waits for them, and re-layouts  3.18 us
  transfers between devices with their start and end apart: 17, of which 5 were waited for; matrix products, arithmetic and copies ran while one was open for 0% of the time, Pallas kernels for 30%

profile of v7, /device:TPU:1, one launch (start us, length us, event | category | flops | bytes accessed | tf_op | source)
XLA Modules:
  0.0 131.0 jit_solution(2233663542998903402)
XLA Ops:
  0.7 4.7 %prep.1 = (f32[1536,128]{1,0:T(8,128)S(1)}, f32[1536,128]{1,0:T(8,128)S(1)}, f32[72,128]{1,0:T(8,128)S(1)}, f32[2688,128]{1,0:T(8,128)}, f32[56,128]{1,0:T(8,128...) custom-call(f32[2,48,2,1152]{3,2,1,0:T(2,128)} %atm_hbm.1, ...), custom_call_target="tpu_custom_call" | custom-call | flops 3300000000 | bytes 9000000 | tf_op jit(solution)/shard_map/prep/pallas_call | solution.py:373
  5.3 2.5 %collective-permute-start = (f32[1536,128]{1,0:T(8,128)S(1)}, f32[1536,128]{1,0:T(8,128)S(1)}, u32[]{:S(2)}, u32[]{:S(2)}) collective-permute-start(f32[1536,128]{1,0:T(8,128)S(1)} %get-tuple-element.58.high), channel_id=1, source_target_pairs={{0,2},{2,4},{4,6},{6,8},{8,10},{10,12},{12,14},{14,16},{16,18},{18... | collective-permute-start | bytes 2359304 | tf_op jit(solution)/shard_map/ppermute | solution.py:387
  7.9 8.7 %collective-permute-start.1 = (f32[1536,128]{1,0:T(8,128)S(1)}, f32[1536,128]{1,0:T(8,128)S(1)}, u32[]{:S(2)}, u32[]{:S(2)}) collective-permute-start(f32[1536,128]{1,0:T(8,128)S(1)} %get-tuple-element.59.low), channel_id=1, source_target_pairs={{2,0},{4,2},{6,4},{8,6},{10,8},{12,10},{14,12},{16,14},{18,16},{20... | collective-permute-start | bytes 2359304 | tf_op jit(solution)/shard_map/ppermute | solution.py:387
  16.6 8.7 %temp_gather.1 = f32[128,4,128]{2,1,0:T(4,128)} custom-call(f32[64,128]{1,0:T(8,128)S(1)} %get-tuple-element.56.table_ref, s32[128,512]{1,0:T(8,128)S(1)} %bitcast.12, f32[128,512]{1,0:T(8,128)S(1)} %bitcast.6), custom_call_target="tpu_custom_call" | custom-call | flops 9900000256 | bytes 27000000 | tf_op jit(solution)/shard_map/temp_gather/pallas_call | solution.py:373
  25.2 7.9 %all-to-all-start = ((f32[128,4,128]{2,1,0:T(4,128)}), f32[128,4,128]{2,1,0:T(4,128)S(1)}, u32[]{:S(2)}, u32[]{:S(2)}) async-start(f32[128,4,128]{2,1,0:T(4,128)} %temp_gather.1), calls=%async_computation | async-start | bytes 524288 | tf_op jit(solution)/shard_map/all_to_all | solution.py:396
  33.1 1.6 %collective-permute-start.2 = (f32[72,128]{1,0:T(8,128)S(1)}, f32[72,128]{1,0:T(8,128)S(1)}, u32[]{:S(2)}, u32[]{:S(2)}) collective-permute-start(f32[72,128]{1,0:T(8,128)S(1)} %get-tuple-element.60), channel_id=1, source_target_pairs={{0,1},{1,0},{2,3},{3,2},{4,5},{5,4},{6,7},{7,6},{8,9},{9,8},{10,11... | collective-permute-start | bytes 110600 | tf_op jit(solution)/shard_map/ppermute | solution.py:392
  39.6 6.6 %all-to-all-done.val_ref = f32[128,4,128]{2,1,0:T(4,128)S(1)} async-done(((f32[128,4,128]{2,1,0:T(4,128)}), f32[128,4,128]{2,1,0:T(4,128)S(1)}, u32[]{:S(2)}, u32[]{:S(2)}) %all-to-all-start) | async-done | bytes 262176 | tf_op jit(solution)/shard_map/all_to_all | solution.py:396
  46.2 8.5 %temp_scatter.1 = (f32[18,128]{1,0:T(8,128)}, bf16[256,240]{1,0:T(8,128)(2,1)S(1)}) custom-call(f32[128,4,128]{2,1,0:T(4,128)S(1)} %all-to-all-done.val_ref, s32[128,512]{1,0:T(8,128)} %bitcast.7, f32[2,18,128]{2,1,0:T(8,128)S(1)} %copy-done.19, f32[2,18,128]{2,1,0:T(8,128)S(1)} %copy-done.11), custom_call_target="tpu_custom_call" | custom-call | flops 9900000256 | bytes 27000000 | tf_op jit(solution)/shard_map/temp_scatter/pallas_call | solution.py:373
  55.4 1.8 %atm_step.4 = (f32[1536,128]{1,0:T(8,128)}, f32[1536,128]{1,0:T(8,128)}, f32[72,128]{1,0:T(8,128)S(1)}) custom-call(f32[1536,128]{1,0:T(8,128)S(1)} %get-tuple-element.59.low, f32[1536,128]{1,0:T(8,128)S(1)} %get-tuple-element.58.high, f32[1536,128]{1,0:T(8,128)S(1)} %collective-permute-done.refs_1_.up, f32[1536,128]{1,0:T(8,128)S(1)} %collective-permute-done.1.refs_2_.down, ...), custom_call_target="tpu_custom_call" | custom-call | flops 2750000128 | bytes 7500000 | tf_op jit(solution)/shard_map/atm_step/pallas_call | solution.py:373
  58.7 8.9 %flux_gather.1 = f32[128,8,128]{2,1,0:T(8,128)} custom-call(bf16[256,240]{1,0:T(8,128)(2,1)S(1)} %get-tuple-element.75.t_ref, s32[128,512]{1,0:T(8,128)S(1)} %bitcast.8, f32[128,512]{1,0:T(8,128)S(1)} %bitcast.9), custom_call_target="tpu_custom_call" | custom-call | flops 9900000256 | bytes 27000000 | tf_op jit(solution)/shard_map/flux_gather/pallas_call | solution.py:373
  67.6 9.5 %all-to-all-start.1 = ((f32[128,8,128]{2,1,0:T(8,128)}), f32[128,8,128]{2,1,0:T(8,128)S(1)}, u32[]{:S(2)}, u32[]{:S(2)}) async-start(f32[128,8,128]{2,1,0:T(8,128)} %flux_gather.1), calls=%async_computation.1 | async-start | bytes 1048576 | tf_op jit(solution)/shard_map/all_to_all | solution.py:396
  77.0 3.9 %collective-permute-start.5 = (f32[72,128]{1,0:T(8,128)S(1)}, f32[72,128]{1,0:T(8,128)S(1)}, u32[]{:S(2)}, u32[]{:S(2)}) collective-permute-start(f32[72,128]{1,0:T(8,128)S(1)} %get-tuple-element.76), channel_id=1, source_target_pairs={{0,1},{1,0},{2,3},{3,2},{4,5},{5,4},{6,7},{7,6},{8,9},{9,8},{10,11... | collective-permute-start | bytes 110600 | tf_op jit(solution)/shard_map/ppermute | solution.py:392
  81.9 2.0 %atm_step.5 = (f32[864,128]{1,0:T(8,128)S(1)}, f32[864,128]{1,0:T(8,128)S(1)}, f32[48,128]{1,0:T(8,128)S(1)}) custom-call(f32[1536,128]{1,0:T(8,128)} %get-tuple-element.82.low, f32[1536,128]{1,0:T(8,128)} %get-tuple-element.83.high, f32[1536,128]{1,0:T(8,128)S(1)} %collective-permute-done.3.refs_1_.up, f32[1536,128]{1,0:T(8,128)S(1)} %collective-permute-done.4.refs_2_.down, ...), custom_call_target="tpu_custom_call" | custom-call | flops 2750000128 | bytes 7500000 | tf_op jit(solution)/shard_map/atm_step/pallas_call | solution.py:373
  83.9 2.0 %collective-permute-start.8 = (f32[48,128]{1,0:T(8,128)S(1)}, f32[48,128]{1,0:T(8,128)S(1)}, u32[]{:S(2)}, u32[]{:S(2)}) collective-permute-start(f32[48,128]{1,0:T(8,128)S(1)} %get-tuple-element.87), channel_id=1, source_target_pairs={{0,1},{1,0},{2,3},{3,2},{4,5},{5,4},{6,7},{7,6},{8,9},{9,8},{10,11... | collective-permute-start | bytes 73736 | tf_op jit(solution)/shard_map/ppermute | solution.py:392
  86.0 5.4 %collective-permute-start.7 = (f32[864,128]{1,0:T(8,128)S(1)}, f32[864,128]{1,0:T(8,128)S(1)}, u32[]{:S(2)}, u32[]{:S(2)}) collective-permute-start(f32[864,128]{1,0:T(8,128)S(1)} %get-tuple-element.89.low), channel_id=1, source_target_pairs={{2,0},{4,2},{6,4},{8,6},{10,8},{12,10},{14,12},{16,14},{18,16},{20... | collective-permute-start | bytes 1327112 | tf_op jit(solution)/shard_map/ppermute | solution.py:387
  91.4 2.7 %ocn_step.3 = (f32[2,24,4,1792]{3,2,1,0:T(4,128)}, f32[2,2,4,1792]{3,2,1,0:T(4,128)}) custom-call(f32[2688,128]{1,0:T(8,128)S(1)} %copy-done.7, f32[1536,128]{1,0:T(8,128)S(1)} %collective-permute-done.3.refs_1_.up, f32[1536,128]{1,0:T(8,128)S(1)} %collective-permute-done.4.refs_2_.down, f32[72,128]{1,0:T(8,128)S(1)} %collective-permute-done.5.refs_3_.edges_ref, ...), custom_call_target="tpu_custom_call" | custom-call | flops 3300000000 | bytes 9000000 | tf_op jit(solution)/shard_map/ocn_step/pallas_call | solution.py:373
  94.1 9.2 %forcing_half.1.half_ref = f32[2,32,256]{2,1,0:T(8,128)S(1)} custom-call(f32[128,8,128]{2,1,0:T(8,128)S(1)} %all-to-all-done.1.val_ref, s32[128,512]{1,0:T(8,128)} %bitcast.10), custom_call_target="tpu_custom_call" | custom-call | flops 8249999872 | bytes 22500000 | tf_op jit(solution)/shard_map/forcing_half/pallas_call | solution.py:373
  103.3 4.9 %collective-permute-done.6.up = f32[864,128]{1,0:T(8,128)} collective-permute-done((f32[864,128]{1,0:T(8,128)S(1)}, f32[864,128]{1,0:T(8,128)}, u32[]{:S(2)}, u32[]{:S(2)}) %collective-permute-start.6) | collective-permute-done | bytes 442400 | tf_op jit(solution)/shard_map/ppermute | solution.py:387
  108.2 1.7 %atm_step.6 = (f32[864,128]{1,0:T(8,128)S(1)}, f32[864,128]{1,0:T(8,128)S(1)}, f32[48,128]{1,0:T(8,128)S(1)}) custom-call(f32[864,128]{1,0:T(8,128)S(1)} %get-tuple-element.89.low, f32[864,128]{1,0:T(8,128)S(1)} %get-tuple-element.90.high, f32[864,128]{1,0:T(8,128)} %collective-permute-done.6.up, f32[864,128]{1,0:T(8,128)S(1)} %collective-permute-done.7.down, ...), custom_call_target="tpu_custom_call" | custom-call | flops 2750000128 | bytes 7500000 | tf_op jit(solution)/shard_map/atm_step/pallas_call | solution.py:373
  109.9 2.0 %collective-permute-start.10 = (f32[864,128]{1,0:T(8,128)S(1)}, f32[864,128]{1,0:T(8,128)S(1)}, u32[]{:S(2)}, u32[]{:S(2)}) collective-permute-start(f32[864,128]{1,0:T(8,128)S(1)} %get-tuple-element.96.low), channel_id=1, source_target_pairs={{2,0},{4,2},{6,4},{8,6},{10,8},{12,10},{14,12},{16,14},{18,16},{20... | collective-permute-start | bytes 1327112 | tf_op jit(solution)/shard_map/ppermute | solution.py:387
  113.3 4.7 %forcing_scatter.1 = (f32[2,56,128]{2,1,0:T(8,128)S(1)}, f32[2,56,128]{2,1,0:T(8,128)S(1)}, f32[2,14,128]{2,1,0:T(8,128)S(1)}, f32[2,14,128]{2,1,0:T(8,128)S(1)}) custom-call(f32[2,32,256]{2,1,0:T(8,128)S(1)} %forcing_half.1.half_ref, f32[128,8,128]{2,1,0:T(8,128)S(1)} %all-to-all-done.1.val_ref, s32[128,512]{1,0:T(8,128)} %bitcast.11, f32[56,128]{1,0:T(8,128)S(1)} %copy-done.8), custom_call_target="tpu_custom_call" | custom-call | flops 8249999872 | bytes 22500000 | tf_op jit(solution)/shard_map/forcing_scatter/pallas_call | solution.py:373
  118.1 6.9 %collective-permute-start.13 = (f32[2,14,128]{2,1,0:T(8,128)S(1)}, f32[2,14,128]{2,1,0:T(8,128)S(1)}, u32[]{:S(2)}, u32[]{:S(2)}) collective-permute-start(f32[2,14,128]{2,1,0:T(8,128)S(1)} %get-tuple-element.109), channel_id=1, source_target_pairs={{2,0},{4,2},{6,4},{8,6},{10,8},{12,10},{14,12},{16,14},{18,16},{20... | collective-permute-start | bytes 43016 | tf_op jit(solution)/shard_map/ppermute | solution.py:387
  125.5 2.5 %collective-permute-done.9.up = f32[864,128]{1,0:T(8,128)S(1)} collective-permute-done((f32[864,128]{1,0:T(8,128)S(1)}, f32[864,128]{1,0:T(8,128)S(1)}, u32[]{:S(2)}, u32[]{:S(2)}) %collective-permute-start.9) | collective-permute-done | bytes 442400 | tf_op jit(solution)/shard_map/ppermute | solution.py:387
  128.1 2.0 %atm_step.7 = f32[2,48,2,1152]{3,2,1,0:T(2,128)} custom-call(f32[864,128]{1,0:T(8,128)S(1)} %get-tuple-element.96.low, f32[864,128]{1,0:T(8,128)S(1)} %get-tuple-element.97.high, f32[864,128]{1,0:T(8,128)S(1)} %collective-permute-done.9.up, f32[864,128]{1,0:T(8,128)S(1)} %collective-permute-done.10.down, f32[48,128]{1,0:T(8,128)S(1)} %collective-permute-done.11.edges_ref, ...), custom_call_target="tpu_custom_call" | custom-call | flops 2750000128 | bytes 7500000 | tf_op jit(solution)/shard_map/atm_step/pallas_call | solution.py:373
  (63 shorter events, 10.7 us)
Async XLA Ops:
  0.6 15.9 %copy-start = (f32[1,1,128,512]{3,2,1,0:T(8,128)S(1)}, f32[1,1,128,512]{3,2,1,0:T(8,128)}, u32[]{:S(2)}) copy-start(f32[1,1,128,512]{3,2,1,0:T(8,128)} %param.19) | copy-start | bytes 786436
  0.6 15.9 %copy-start.3 = (s32[1,1,128,512]{3,2,1,0:T(8,128)S(1)}, s32[1,1,128,512]{3,2,1,0:T(8,128)}, u32[]{:S(2)}) copy-start(s32[1,1,128,512]{3,2,1,0:T(8,128)} %param.18) | copy-start | bytes 786436
  5.3 30.3 %collective-permute-start = (f32[1536,128]{1,0:T(8,128)S(1)}, f32[1536,128]{1,0:T(8,128)S(1)}, u32[]{:S(2)}, u32[]{:S(2)}) collective-permute-start(f32[1536,128]{1,0:T(8,128)S(1)} %get-tuple-element.58.high), channel_id=1, source_target_pairs={{0,2},{2,4},{4,6},{6,8},{8,10},{10,12},{12,14},{14,16},{16,18},{18... | collective-permute-start | bytes 2359304 | tf_op jit(solution)/shard_map/ppermute | solution.py:387
  7.9 27.7 %collective-permute-start.1 = (f32[1536,128]{1,0:T(8,128)S(1)}, f32[1536,128]{1,0:T(8,128)S(1)}, u32[]{:S(2)}, u32[]{:S(2)}) collective-permute-start(f32[1536,128]{1,0:T(8,128)S(1)} %get-tuple-element.59.low), channel_id=1, source_target_pairs={{2,0},{4,2},{6,4},{8,6},{10,8},{12,10},{14,12},{16,14},{18,16},{20... | collective-permute-start | bytes 2359304 | tf_op jit(solution)/shard_map/ppermute | solution.py:387
  16.6 19.1 %copy-start.8 = (f32[56,128]{1,0:T(8,128)S(1)}, f32[56,128]{1,0:T(8,128)}, u32[]{:S(2)}) copy-start(f32[56,128]{1,0:T(8,128)} %get-tuple-element.62.refs_5_.frac_ref) | copy-start | bytes 86020
  16.6 19.1 %copy-start.10 = (f32[24,128]{1,0:T(8,128)S(1)}, f32[24,128]{1,0:T(8,128)}, u32[]{:S(2)}) copy-start(f32[24,128]{1,0:T(8,128)} %get-tuple-element.61.refs_4_.diff_ref) | copy-start | bytes 36868
  25.2 20.9 %all-to-all-start = ((f32[128,4,128]{2,1,0:T(4,128)}), f32[128,4,128]{2,1,0:T(4,128)S(1)}, u32[]{:S(2)}, u32[]{:S(2)}) async-start(f32[128,4,128]{2,1,0:T(4,128)} %temp_gather.1), calls=%async_computation | async-start | bytes 524288 | tf_op jit(solution)/shard_map/all_to_all | solution.py:396
  33.1 2.5 %collective-permute-start.2 = (f32[72,128]{1,0:T(8,128)S(1)}, f32[72,128]{1,0:T(8,128)S(1)}, u32[]{:S(2)}, u32[]{:S(2)}) collective-permute-start(f32[72,128]{1,0:T(8,128)S(1)} %get-tuple-element.60), channel_id=1, source_target_pairs={{0,1},{1,0},{2,3},{3,2},{4,5},{5,4},{6,7},{7,6},{8,9},{9,8},{10,11... | collective-permute-start | bytes 110600 | tf_op jit(solution)/shard_map/ppermute | solution.py:392
  57.2 24.7 %collective-permute-start.4 = (f32[1536,128]{1,0:T(8,128)}, f32[1536,128]{1,0:T(8,128)S(1)}, u32[]{:S(2)}, u32[]{:S(2)}) collective-permute-start(f32[1536,128]{1,0:T(8,128)} %get-tuple-element.82.low), channel_id=1, source_target_pairs={{2,0},{4,2},{6,4},{8,6},{10,8},{12,10},{14,12},{16,14},{18,16},{20... | collective-permute-start | bytes 2359304 | tf_op jit(solution)/shard_map/ppermute | solution.py:387
  57.7 24.2 %collective-permute-start.3 = (f32[1536,128]{1,0:T(8,128)}, f32[1536,128]{1,0:T(8,128)S(1)}, u32[]{:S(2)}, u32[]{:S(2)}) collective-permute-start(f32[1536,128]{1,0:T(8,128)} %get-tuple-element.83.high), channel_id=1, source_target_pairs={{0,2},{2,4},{4,6},{6,8},{8,10},{10,12},{12,14},{14,16},{16,18},{18... | collective-permute-start | bytes 2359304 | tf_op jit(solution)/shard_map/ppermute | solution.py:387
  58.7 23.2 %copy-start.13 = (f32[48,128]{1,0:T(8,128)S(1)}, f32[48,128]{1,0:T(8,128)}, u32[]{:S(2)}) copy-start(f32[48,128]{1,0:T(8,128)} %get-tuple-element.69.diff_ref) | copy-start | bytes 73732
  58.7 23.2 %copy-start.16 = (f32[18,128]{1,0:T(8,128)S(1)}, f32[18,128]{1,0:T(8,128)}, u32[]{:S(2)}) copy-start(f32[18,128]{1,0:T(8,128)} %get-tuple-element.70.temp_ref) | copy-start | bytes 27652
  67.6 26.5 %all-to-all-start.1 = ((f32[128,8,128]{2,1,0:T(8,128)}), f32[128,8,128]{2,1,0:T(8,128)S(1)}, u32[]{:S(2)}, u32[]{:S(2)}) async-start(f32[128,8,128]{2,1,0:T(8,128)} %flux_gather.1), calls=%async_computation.1 | async-start | bytes 1048576 | tf_op jit(solution)/shard_map/all_to_all | solution.py:396
  77.0 14.4 %copy-start.7 = (f32[2688,128]{1,0:T(8,128)S(1)}, f32[2688,128]{1,0:T(8,128)}, u32[]{:S(2)}) copy-start(f32[2688,128]{1,0:T(8,128)} %copy-done.5) | copy-start | bytes 4128772
  77.0 4.8 %collective-permute-start.5 = (f32[72,128]{1,0:T(8,128)S(1)}, f32[72,128]{1,0:T(8,128)S(1)}, u32[]{:S(2)}, u32[]{:S(2)}) collective-permute-start(f32[72,128]{1,0:T(8,128)S(1)} %get-tuple-element.76), channel_id=1, source_target_pairs={{0,1},{1,0},{2,3},{3,2},{4,5},{5,4},{6,7},{7,6},{8,9},{9,8},{10,11... | collective-permute-start | bytes 110600 | tf_op jit(solution)/shard_map/ppermute | solution.py:392
  83.9 19.3 %collective-permute-start.8 = (f32[48,128]{1,0:T(8,128)S(1)}, f32[48,128]{1,0:T(8,128)S(1)}, u32[]{:S(2)}, u32[]{:S(2)}) collective-permute-start(f32[48,128]{1,0:T(8,128)S(1)} %get-tuple-element.87), channel_id=1, source_target_pairs={{0,1},{1,0},{2,3},{3,2},{4,5},{5,4},{6,7},{7,6},{8,9},{9,8},{10,11... | collective-permute-start | bytes 73736 | tf_op jit(solution)/shard_map/ppermute | solution.py:392
  86.0 17.3 %collective-permute-start.7 = (f32[864,128]{1,0:T(8,128)S(1)}, f32[864,128]{1,0:T(8,128)S(1)}, u32[]{:S(2)}, u32[]{:S(2)}) collective-permute-start(f32[864,128]{1,0:T(8,128)S(1)} %get-tuple-element.89.low), channel_id=1, source_target_pairs={{2,0},{4,2},{6,4},{8,6},{10,8},{12,10},{14,12},{16,14},{18,16},{20... | collective-permute-start | bytes 1327112 | tf_op jit(solution)/shard_map/ppermute | solution.py:387
  91.4 16.8 %collective-permute-start.6 = (f32[864,128]{1,0:T(8,128)S(1)}, f32[864,128]{1,0:T(8,128)}, u32[]{:S(2)}, u32[]{:S(2)}) collective-permute-start(f32[864,128]{1,0:T(8,128)S(1)} %get-tuple-element.90.high), channel_id=1, source_target_pairs={{0,2},{2,4},{4,6},{6,8},{8,10},{10,12},{12,14},{14,16},{16,18},{18... | collective-permute-start | bytes 1327112 | tf_op jit(solution)/shard_map/ppermute | solution.py:387
  109.9 15.6 %collective-permute-start.10 = (f32[864,128]{1,0:T(8,128)S(1)}, f32[864,128]{1,0:T(8,128)S(1)}, u32[]{:S(2)}, u32[]{:S(2)}) collective-permute-start(f32[864,128]{1,0:T(8,128)S(1)} %get-tuple-element.96.low), channel_id=1, source_target_pairs={{2,0},{4,2},{6,4},{8,6},{10,8},{12,10},{14,12},{16,14},{18,16},{20... | collective-permute-start | bytes 1327112 | tf_op jit(solution)/shard_map/ppermute | solution.py:387
  111.9 16.1 %collective-permute-start.9 = (f32[864,128]{1,0:T(8,128)S(1)}, f32[864,128]{1,0:T(8,128)S(1)}, u32[]{:S(2)}, u32[]{:S(2)}) collective-permute-start(f32[864,128]{1,0:T(8,128)S(1)} %get-tuple-element.97.high), channel_id=1, source_target_pairs={{0,2},{2,4},{4,6},{6,8},{8,10},{10,12},{12,14},{14,16},{16,18},{18... | collective-permute-start | bytes 1327112 | tf_op jit(solution)/shard_map/ppermute | solution.py:387
  112.0 13.0 %collective-permute-start.11 = (f32[48,128]{1,0:T(8,128)S(1)}, f32[48,128]{1,0:T(8,128)S(1)}, u32[]{:S(2)}, u32[]{:S(2)}) collective-permute-start(f32[48,128]{1,0:T(8,128)S(1)} %get-tuple-element.100), channel_id=1, source_target_pairs={{0,1},{1,0},{2,3},{3,2},{4,5},{5,4},{6,7},{7,6},{8,9},{9,8},{10,11... | collective-permute-start | bytes 73736 | tf_op jit(solution)/shard_map/ppermute | solution.py:392
  118.0 12.0 %collective-permute-start.12 = (f32[2,14,128]{2,1,0:T(8,128)S(1)}, f32[2,14,128]{2,1,0:T(8,128)S(1)}, u32[]{:S(2)}, u32[]{:S(2)}) collective-permute-start(f32[2,14,128]{2,1,0:T(8,128)S(1)} %get-tuple-element.108), channel_id=1, source_target_pairs={{0,2},{2,4},{4,6},{6,8},{8,10},{10,12},{12,14},{14,16},{16,18},{18... | collective-permute-start | bytes 43016 | tf_op jit(solution)/shard_map/ppermute | solution.py:387
  118.1 12.0 %collective-permute-start.13 = (f32[2,14,128]{2,1,0:T(8,128)S(1)}, f32[2,14,128]{2,1,0:T(8,128)S(1)}, u32[]{:S(2)}, u32[]{:S(2)}) collective-permute-start(f32[2,14,128]{2,1,0:T(8,128)S(1)} %get-tuple-element.109), channel_id=1, source_target_pairs={{2,0},{4,2},{6,4},{8,6},{10,8},{12,10},{14,12},{16,14},{18,16},{20... | collective-permute-start | bytes 43016 | tf_op jit(solution)/shard_map/ppermute | solution.py:387
  125.0 5.0 %collective-permute-start.14 = (f32[2,56,128]{2,1,0:T(8,128)S(1)}, f32[2,56,128]{2,1,0:T(8,128)S(1)}, u32[]{:S(2)}, u32[]{:S(2)}) collective-permute-start(f32[2,56,128]{2,1,0:T(8,128)S(1)} %get-tuple-element.107.gain_ref), channel_id=1, source_target_pairs={{0,1},{1,0},{2,3},{3,2},{4,5},{5,4},{6,7},{7,6},{8,9},{9,8},{10,11... | collective-permute-start | bytes 172040 | tf_op jit(solution)/shard_map/ppermute | solution.py:392
  (13 other events, 83.9 us)

commit v8 on v4

--- a/solution.py
+++ b/solution.py
@@ -411,7 +411,7 @@
     ocean, ocn_edges = call(ocn_step, "ocn_step", 3, (shape(OR * OSIZE, LANES), free(OL, LANES)), ocean, up, down, beside, ocn_diff, frac, cold=(4, 5))
     incoming, ocean, ocn_edges = lax.optimization_barrier((incoming, ocean, ocn_edges))
 
-    temp, flux_table = call(flux_kernel, "temp_scatter", 9, (free(AR * AT, LANES), pltpu.VMEM((128, SPLITS * 48), BF16)), incoming, cols, surface, coef, far=(1,), cold=(2, 3), in_specs=[VM, HBM, VM, VM], scratch=[pltpu.VMEM((24, LANES), F32), *store])
+    temp, flux_table = call(flux_kernel, "temp_scatter", 9, (shape(AR * AT, LANES), pltpu.VMEM((128, SPLITS * 48), BF16)), incoming, cols, surface, coef, far=(1,), cold=(2, 3), in_specs=[VM, HBM, VM, VM], scratch=[pltpu.VMEM((24, LANES), F32), *store])
 
     def atm_step(low, high, up, down, beside, *more, outs=None):
         rows = shape(ASIZE + (OSIZE if more else 0), LANES)

time: 131 us -> 130 us (level)
  transfers between devices with their start and end apart: 17 -> 17, of which waited for: 4 -> 4; matrix products, arithmetic and copies ran while one was open for 0% -> 0% of each run, Pallas kernels for 30% -> 31%
where the time goes in v8:
time: 130 us
  Pallas kernels  56.8 us (44%)
  starting transfers between devices  54 us (42%)
  waiting for transfers between devices  15.5 us (12%)
  local copies, waits for them, and re-layouts  2.49 us (2%)
    pallas_call x13, Pallas kernels, call(): pl.pallas_call(kernel, out_shape=out_shape, scratch_shapes=list(scratch),...  56.8 us
    ppermute x5, starting transfers between devices, row_halos(): lax.ppermute(first, GROUP, [(b, a) for a, b in up])  21.8 us
    all_to_all x2, starting transfers between devices, exchange(): lax.all_to_all(values, GROUP, split_axis=0, concat_axis=0, tiled=True)  17.3 us
    ppermute x5, starting transfers between devices, partner(): lax.ppermute(edges, 'lev', [(i, (i + 1) % count) for i in range(count)])  9.98 us
    ppermute x5, waiting for transfers between devices, row_halos(): lax.ppermute(last, GROUP, up)  7.19 us
    all_to_all x2, waiting for transfers between devices, exchange(): lax.all_to_all(values, GROUP, split_axis=0, concat_axis=0, tiled=True)  6.56 us
    ppermute x5, starting transfers between devices, row_halos(): lax.ppermute(last, GROUP, up)  4.81 us
  transfers between devices with their start and end apart: 17, of which 4 were waited for; matrix products, arithmetic and copies ran while one was open for 0% of the time, Pallas kernels for 31%

profile of v8, /device:TPU:1, one launch (start us, length us, event | category | flops | bytes accessed | tf_op | source)
XLA Modules:
  0.0 129.8 jit_solution(3156315253220594498)
XLA Ops:
  0.7 4.7 %prep.1 = (f32[1536,128]{1,0:T(8,128)S(1)}, f32[1536,128]{1,0:T(8,128)S(1)}, f32[72,128]{1,0:T(8,128)S(1)}, f32[2688,128]{1,0:T(8,128)}, f32[56,128]{1,0:T(8,128...) custom-call(f32[2,48,2,1152]{3,2,1,0:T(2,128)} %atm_hbm.1, ...), custom_call_target="tpu_custom_call" | custom-call | flops 3300000000 | bytes 9000000 | tf_op jit(solution)/shard_map/prep/pallas_call | solution.py:346
  5.3 2.5 %collective-permute-start = (f32[1536,128]{1,0:T(8,128)S(1)}, f32[1536,128]{1,0:T(8,128)S(1)}, u32[]{:S(2)}, u32[]{:S(2)}) collective-permute-start(f32[1536,128]{1,0:T(8,128)S(1)} %get-tuple-element.58.high), channel_id=1, source_target_pairs={{0,2},{2,4},{4,6},{6,8},{8,10},{10,12},{12,14},{14,16},{16,18},{18... | collective-permute-start | bytes 2359304 | tf_op jit(solution)/shard_map/ppermute | solution.py:360
  7.9 8.7 %collective-permute-start.1 = (f32[1536,128]{1,0:T(8,128)S(1)}, f32[1536,128]{1,0:T(8,128)S(1)}, u32[]{:S(2)}, u32[]{:S(2)}) collective-permute-start(f32[1536,128]{1,0:T(8,128)S(1)} %get-tuple-element.59.low), channel_id=1, source_target_pairs={{2,0},{4,2},{6,4},{8,6},{10,8},{12,10},{14,12},{16,14},{18,16},{20... | collective-permute-start | bytes 2359304 | tf_op jit(solution)/shard_map/ppermute | solution.py:360
  16.6 8.7 %temp_gather.1 = f32[128,4,128]{2,1,0:T(4,128)} custom-call(f32[64,128]{1,0:T(8,128)S(1)} %get-tuple-element.56.table_ref, s32[128,512]{1,0:T(8,128)S(1)} %bitcast.12, f32[128,512]{1,0:T(8,128)S(1)} %bitcast.6), custom_call_target="tpu_custom_call" | custom-call | flops 9900000256 | bytes 27000000 | tf_op jit(solution)/shard_map/temp_gather/pallas_call | solution.py:346
  25.2 7.9 %all-to-all-start = ((f32[128,4,128]{2,1,0:T(4,128)}), f32[128,4,128]{2,1,0:T(4,128)S(1)}, u32[]{:S(2)}, u32[]{:S(2)}) async-start(f32[128,4,128]{2,1,0:T(4,128)} %temp_gather.1), calls=%async_computation | async-start | bytes 524288 | tf_op jit(solution)/shard_map/all_to_all | solution.py:369
  33.1 1.6 %collective-permute-start.2 = (f32[72,128]{1,0:T(8,128)S(1)}, f32[72,128]{1,0:T(8,128)S(1)}, u32[]{:S(2)}, u32[]{:S(2)}) collective-permute-start(f32[72,128]{1,0:T(8,128)S(1)} %get-tuple-element.60), channel_id=1, source_target_pairs={{0,1},{1,0},{2,3},{3,2},{4,5},{5,4},{6,7},{7,6},{8,9},{9,8},{10,11... | collective-permute-start | bytes 110600 | tf_op jit(solution)/shard_map/ppermute | solution.py:365
  37.0 1.5 %ocn_step.2 = (f32[2688,128]{1,0:T(8,128)S(1)}, f32[24,128]{1,0:T(8,128)}) custom-call(f32[2688,128]{1,0:T(8,128)S(1)} %copy-done.9, f32[1536,128]{1,0:T(8,128)S(1)} %collective-permute-done.refs_1_.up, f32[1536,128]{1,0:T(8,128)S(1)} %collective-permute-done.1.refs_2_.down, f32[72,128]{1,0:T(8,128)S(1)} %collective-permute-done.2.refs_3_.edges_ref, ...), custom_call_target="tpu_custom_call" | custom-call | flops 3300000000 | bytes 9000000 | tf_op jit(solution)/shard_map/ocn_step/pallas_call | solution.py:346
  39.6 6.6 %all-to-all-done.val_ref = f32[128,4,128]{2,1,0:T(4,128)S(1)} async-done(((f32[128,4,128]{2,1,0:T(4,128)}), f32[128,4,128]{2,1,0:T(4,128)S(1)}, u32[]{:S(2)}, u32[]{:S(2)}) %all-to-all-start) | async-done | bytes 262176 | tf_op jit(solution)/shard_map/all_to_all | solution.py:369
  46.2 8.1 %temp_scatter.1 = (f32[18,128]{1,0:T(8,128)S(1)}, bf16[128,144]{1,0:T(8,128)(2,1)S(1)}) custom-call(f32[128,4,128]{2,1,0:T(4,128)S(1)} %all-to-all-done.val_ref, s32[128,512]{1,0:T(8,128)} %bitcast.7, f32[2,18,128]{2,1,0:T(8,128)S(1)} %copy-done.19, f32[2,18,128]{2,1,0:T(8,128)S(1)} %copy-done.11), custom_call_target="tpu_custom_call" | custom-call | flops 9900000256 | bytes 27000000 | tf_op jit(solution)/shard_map/temp_scatter/pallas_call | solution.py:346
  54.4 1.8 %atm_step.4 = (f32[1536,128]{1,0:T(8,128)}, f32[1536,128]{1,0:T(8,128)}, f32[72,128]{1,0:T(8,128)S(1)}) custom-call(f32[1536,128]{1,0:T(8,128)S(1)} %get-tuple-element.59.low, f32[1536,128]{1,0:T(8,128)S(1)} %get-tuple-element.58.high, f32[1536,128]{1,0:T(8,128)S(1)} %collective-permute-done.refs_1_.up, f32[1536,128]{1,0:T(8,128)S(1)} %collective-permute-done.1.refs_2_.down, ...), custom_call_target="tpu_custom_call" | custom-call | flops 2750000128 | bytes 7500000 | tf_op jit(solution)/shard_map/atm_step/pallas_call | solution.py:346
  57.6 8.9 %flux_gather.1 = f32[128,8,128]{2,1,0:T(8,128)} custom-call(bf16[128,144]{1,0:T(8,128)(2,1)S(1)} %get-tuple-element.75.t_ref, s32[128,512]{1,0:T(8,128)S(1)} %bitcast.8, f32[128,512]{1,0:T(8,128)S(1)} %bitcast.9), custom_call_target="tpu_custom_call" | custom-call | flops 9900000256 | bytes 27000000 | tf_op jit(solution)/shard_map/flux_gather/pallas_call | solution.py:346
  66.5 9.5 %all-to-all-start.1 = ((f32[128,8,128]{2,1,0:T(8,128)}), f32[128,8,128]{2,1,0:T(8,128)S(1)}, u32[]{:S(2)}, u32[]{:S(2)}) async-start(f32[128,8,128]{2,1,0:T(8,128)} %flux_gather.1), calls=%async_computation.1 | async-start | bytes 1048576 | tf_op jit(solution)/shard_map/all_to_all | solution.py:369
  76.0 3.9 %collective-permute-start.5 = (f32[72,128]{1,0:T(8,128)S(1)}, f32[72,128]{1,0:T(8,128)S(1)}, u32[]{:S(2)}, u32[]{:S(2)}) collective-permute-start(f32[72,128]{1,0:T(8,128)S(1)} %get-tuple-element.76), channel_id=1, source_target_pairs={{0,1},{1,0},{2,3},{3,2},{4,5},{5,4},{6,7},{7,6},{8,9},{9,8},{10,11... | collective-permute-start | bytes 110600 | tf_op jit(solution)/shard_map/ppermute | solution.py:365
  80.9 2.0 %atm_step.5 = (f32[864,128]{1,0:T(8,128)S(1)}, f32[864,128]{1,0:T(8,128)S(1)}, f32[48,128]{1,0:T(8,128)S(1)}) custom-call(f32[1536,128]{1,0:T(8,128)} %get-tuple-element.82.low, f32[1536,128]{1,0:T(8,128)} %get-tuple-element.83.high, f32[1536,128]{1,0:T(8,128)S(1)} %collective-permute-done.3.refs_1_.up, f32[1536,128]{1,0:T(8,128)S(1)} %collective-permute-done.4.refs_2_.down, ...), custom_call_target="tpu_custom_call" | custom-call | flops 2750000128 | bytes 7500000 | tf_op jit(solution)/shard_map/atm_step/pallas_call | solution.py:346
  82.9 2.0 %collective-permute-start.8 = (f32[48,128]{1,0:T(8,128)S(1)}, f32[48,128]{1,0:T(8,128)S(1)}, u32[]{:S(2)}, u32[]{:S(2)}) collective-permute-start(f32[48,128]{1,0:T(8,128)S(1)} %get-tuple-element.87), channel_id=1, source_target_pairs={{0,1},{1,0},{2,3},{3,2},{4,5},{5,4},{6,7},{7,6},{8,9},{9,8},{10,11... | collective-permute-start | bytes 73736 | tf_op jit(solution)/shard_map/ppermute | solution.py:365
  84.9 5.4 %collective-permute-start.7 = (f32[864,128]{1,0:T(8,128)S(1)}, f32[864,128]{1,0:T(8,128)S(1)}, u32[]{:S(2)}, u32[]{:S(2)}) collective-permute-start(f32[864,128]{1,0:T(8,128)S(1)} %get-tuple-element.89.low), channel_id=1, source_target_pairs={{2,0},{4,2},{6,4},{8,6},{10,8},{12,10},{14,12},{16,14},{18,16},{20... | collective-permute-start | bytes 1327112 | tf_op jit(solution)/shard_map/ppermute | solution.py:360
  90.4 2.7 %ocn_step.3 = (f32[2,24,4,1792]{3,2,1,0:T(4,128)}, f32[2,2,4,1792]{3,2,1,0:T(4,128)}) custom-call(f32[2688,128]{1,0:T(8,128)S(1)} %copy-done.7, f32[1536,128]{1,0:T(8,128)S(1)} %collective-permute-done.3.refs_1_.up, f32[1536,128]{1,0:T(8,128)S(1)} %collective-permute-done.4.refs_2_.down, f32[72,128]{1,0:T(8,128)S(1)} %collective-permute-done.5.refs_3_.edges_ref, ...), custom_call_target="tpu_custom_call" | custom-call | flops 3300000000 | bytes 9000000 | tf_op jit(solution)/shard_map/ocn_step/pallas_call | solution.py:346
  93.0 6.9 %forcing_half.1.half_ref = f32[2,32,256]{2,1,0:T(8,128)S(1)} custom-call(f32[128,8,128]{2,1,0:T(8,128)S(1)} %all-to-all-done.1.val_ref, s32[128,512]{1,0:T(8,128)} %bitcast.10), custom_call_target="tpu_custom_call" | custom-call | flops 8249999872 | bytes 22500000 | tf_op jit(solution)/shard_map/forcing_half/pallas_call | solution.py:346
  100.0 7.2 %collective-permute-done.6.up = f32[864,128]{1,0:T(8,128)} collective-permute-done((f32[864,128]{1,0:T(8,128)S(1)}, f32[864,128]{1,0:T(8,128)}, u32[]{:S(2)}, u32[]{:S(2)}) %collective-permute-start.6) | collective-permute-done | bytes 442400 | tf_op jit(solution)/shard_map/ppermute | solution.py:360
  107.2 1.7 %atm_step.6 = (f32[864,128]{1,0:T(8,128)S(1)}, f32[864,128]{1,0:T(8,128)S(1)}, f32[48,128]{1,0:T(8,128)S(1)}) custom-call(f32[864,128]{1,0:T(8,128)S(1)} %get-tuple-element.89.low, f32[864,128]{1,0:T(8,128)S(1)} %get-tuple-element.90.high, f32[864,128]{1,0:T(8,128)} %collective-permute-done.6.up, f32[864,128]{1,0:T(8,128)S(1)} %collective-permute-done.7.down, ...), custom_call_target="tpu_custom_call" | custom-call | flops 2750000128 | bytes 7500000 | tf_op jit(solution)/shard_map/atm_step/pallas_call | solution.py:346
  110.4 1.8 %collective-permute-start.11 = (f32[48,128]{1,0:T(8,128)S(1)}, f32[48,128]{1,0:T(8,128)S(1)}, u32[]{:S(2)}, u32[]{:S(2)}) collective-permute-start(f32[48,128]{1,0:T(8,128)S(1)} %get-tuple-element.100), channel_id=1, source_target_pairs={{0,1},{1,0},{2,3},{3,2},{4,5},{5,4},{6,7},{7,6},{8,9},{9,8},{10,11... | collective-permute-start | bytes 73736 | tf_op jit(solution)/shard_map/ppermute | solution.py:365
  112.3 6.9 %forcing_scatter.1 = (f32[2,56,128]{2,1,0:T(8,128)S(1)}, f32[2,56,128]{2,1,0:T(8,128)S(1)}, f32[2,14,128]{2,1,0:T(8,128)S(1)}, f32[2,14,128]{2,1,0:T(8,128)S(1)}) custom-call(f32[2,32,256]{2,1,0:T(8,128)S(1)} %forcing_half.1.half_ref, f32[128,8,128]{2,1,0:T(8,128)S(1)} %all-to-all-done.1.val_ref, s32[128,512]{1,0:T(8,128)} %bitcast.11, f32[56,128]{1,0:T(8,128)S(1)} %copy-done.8), custom_call_target="tpu_custom_call" | custom-call | flops 8249999872 | bytes 22500000 | tf_op jit(solution)/shard_map/forcing_scatter/pallas_call | solution.py:346
  119.3 6.9 %collective-permute-start.13 = (f32[2,14,128]{2,1,0:T(8,128)S(1)}, f32[2,14,128]{2,1,0:T(8,128)S(1)}, u32[]{:S(2)}, u32[]{:S(2)}) collective-permute-start(f32[2,14,128]{2,1,0:T(8,128)S(1)} %get-tuple-element.109), channel_id=1, source_target_pairs={{2,0},{4,2},{6,4},{8,6},{10,8},{12,10},{14,12},{16,14},{18,16},{20... | collective-permute-start | bytes 43016 | tf_op jit(solution)/shard_map/ppermute | solution.py:360
  126.8 2.0 %atm_step.7 = f32[2,48,2,1152]{3,2,1,0:T(2,128)} custom-call(f32[864,128]{1,0:T(8,128)S(1)} %get-tuple-element.96.low, f32[864,128]{1,0:T(8,128)S(1)} %get-tuple-element.97.high, f32[864,128]{1,0:T(8,128)S(1)} %collective-permute-done.9.up, f32[864,128]{1,0:T(8,128)S(1)} %collective-permute-done.10.down, f32[48,128]{1,0:T(8,128)S(1)} %collective-permute-done.11.edges_ref, ...), custom_call_target="tpu_custom_call" | custom-call | flops 2750000128 | bytes 7500000 | tf_op jit(solution)/shard_map/atm_step/pallas_call | solution.py:346
  (63 shorter events, 8.8 us)
Async XLA Ops:
  0.6 15.9 %copy-start = (f32[1,1,128,512]{3,2,1,0:T(8,128)S(1)}, f32[1,1,128,512]{3,2,1,0:T(8,128)}, u32[]{:S(2)}) copy-start(f32[1,1,128,512]{3,2,1,0:T(8,128)} %param.19) | copy-start | bytes 786436
  0.6 15.9 %copy-start.3 = (s32[1,1,128,512]{3,2,1,0:T(8,128)S(1)}, s32[1,1,128,512]{3,2,1,0:T(8,128)}, u32[]{:S(2)}) copy-start(s32[1,1,128,512]{3,2,1,0:T(8,128)} %param.18) | copy-start | bytes 786436
  5.3 30.3 %collective-permute-start = (f32[1536,128]{1,0:T(8,128)S(1)}, f32[1536,128]{1,0:T(8,128)S(1)}, u32[]{:S(2)}, u32[]{:S(2)}) collective-permute-start(f32[1536,128]{1,0:T(8,128)S(1)} %get-tuple-element.58.high), channel_id=1, source_target_pairs={{0,2},{2,4},{4,6},{6,8},{8,10},{10,12},{12,14},{14,16},{16,18},{18... | collective-permute-start | bytes 2359304 | tf_op jit(solution)/shard_map/ppermute | solution.py:360
  7.9 27.7 %collective-permute-start.1 = (f32[1536,128]{1,0:T(8,128)S(1)}, f32[1536,128]{1,0:T(8,128)S(1)}, u32[]{:S(2)}, u32[]{:S(2)}) collective-permute-start(f32[1536,128]{1,0:T(8,128)S(1)} %get-tuple-element.59.low), channel_id=1, source_target_pairs={{2,0},{4,2},{6,4},{8,6},{10,8},{12,10},{14,12},{16,14},{18,16},{20... | collective-permute-start | bytes 2359304 | tf_op jit(solution)/shard_map/ppermute | solution.py:360
  16.6 19.1 %copy-start.8 = (f32[56,128]{1,0:T(8,128)S(1)}, f32[56,128]{1,0:T(8,128)}, u32[]{:S(2)}) copy-start(f32[56,128]{1,0:T(8,128)} %get-tuple-element.62.refs_5_.frac_ref) | copy-start | bytes 86020
  16.6 19.1 %copy-start.10 = (f32[24,128]{1,0:T(8,128)S(1)}, f32[24,128]{1,0:T(8,128)}, u32[]{:S(2)}) copy-start(f32[24,128]{1,0:T(8,128)} %get-tuple-element.61.refs_4_.diff_ref) | copy-start | bytes 36868
  25.2 20.9 %all-to-all-start = ((f32[128,4,128]{2,1,0:T(4,128)}), f32[128,4,128]{2,1,0:T(4,128)S(1)}, u32[]{:S(2)}, u32[]{:S(2)}) async-start(f32[128,4,128]{2,1,0:T(4,128)} %temp_gather.1), calls=%async_computation | async-start | bytes 524288 | tf_op jit(solution)/shard_map/all_to_all | solution.py:369
  33.1 2.5 %collective-permute-start.2 = (f32[72,128]{1,0:T(8,128)S(1)}, f32[72,128]{1,0:T(8,128)S(1)}, u32[]{:S(2)}, u32[]{:S(2)}) collective-permute-start(f32[72,128]{1,0:T(8,128)S(1)} %get-tuple-element.60), channel_id=1, source_target_pairs={{0,1},{1,0},{2,3},{3,2},{4,5},{5,4},{6,7},{7,6},{8,9},{9,8},{10,11... | collective-permute-start | bytes 110600 | tf_op jit(solution)/shard_map/ppermute | solution.py:365
  56.1 24.7 %collective-permute-start.4 = (f32[1536,128]{1,0:T(8,128)}, f32[1536,128]{1,0:T(8,128)S(1)}, u32[]{:S(2)}, u32[]{:S(2)}) collective-permute-start(f32[1536,128]{1,0:T(8,128)} %get-tuple-element.82.low), channel_id=1, source_target_pairs={{2,0},{4,2},{6,4},{8,6},{10,8},{12,10},{14,12},{16,14},{18,16},{20... | collective-permute-start | bytes 2359304 | tf_op jit(solution)/shard_map/ppermute | solution.py:360
  56.7 24.2 %collective-permute-start.3 = (f32[1536,128]{1,0:T(8,128)}, f32[1536,128]{1,0:T(8,128)S(1)}, u32[]{:S(2)}, u32[]{:S(2)}) collective-permute-start(f32[1536,128]{1,0:T(8,128)} %get-tuple-element.83.high), channel_id=1, source_target_pairs={{0,2},{2,4},{4,6},{6,8},{8,10},{10,12},{12,14},{14,16},{16,18},{18... | collective-permute-start | bytes 2359304 | tf_op jit(solution)/shard_map/ppermute | solution.py:360
  57.6 23.2 %copy-start.13 = (f32[48,128]{1,0:T(8,128)S(1)}, f32[48,128]{1,0:T(8,128)}, u32[]{:S(2)}) copy-start(f32[48,128]{1,0:T(8,128)} %get-tuple-element.69.diff_ref) | copy-start | bytes 73732
  57.6 23.2 %copy-start.16 = (f32[18,128]{1,0:T(8,128)S(1)}, f32[18,128]{1,0:T(8,128)}, u32[]{:S(2)}) copy-start(f32[18,128]{1,0:T(8,128)} %copy-done.15) | copy-start | bytes 27652
  66.5 26.5 %all-to-all-start.1 = ((f32[128,8,128]{2,1,0:T(8,128)}), f32[128,8,128]{2,1,0:T(8,128)S(1)}, u32[]{:S(2)}, u32[]{:S(2)}) async-start(f32[128,8,128]{2,1,0:T(8,128)} %flux_gather.1), calls=%async_computation.1 | async-start | bytes 1048576 | tf_op jit(solution)/shard_map/all_to_all | solution.py:369
  76.0 14.4 %copy-start.7 = (f32[2688,128]{1,0:T(8,128)S(1)}, f32[2688,128]{1,0:T(8,128)}, u32[]{:S(2)}) copy-start(f32[2688,128]{1,0:T(8,128)} %copy-done.5) | copy-start | bytes 4128772
  76.0 4.8 %collective-permute-start.5 = (f32[72,128]{1,0:T(8,128)S(1)}, f32[72,128]{1,0:T(8,128)S(1)}, u32[]{:S(2)}, u32[]{:S(2)}) collective-permute-start(f32[72,128]{1,0:T(8,128)S(1)} %get-tuple-element.76), channel_id=1, source_target_pairs={{0,1},{1,0},{2,3},{3,2},{4,5},{5,4},{6,7},{7,6},{8,9},{9,8},{10,11... | collective-permute-start | bytes 110600 | tf_op jit(solution)/shard_map/ppermute | solution.py:365
  82.9 17.1 %collective-permute-start.8 = (f32[48,128]{1,0:T(8,128)S(1)}, f32[48,128]{1,0:T(8,128)S(1)}, u32[]{:S(2)}, u32[]{:S(2)}) collective-permute-start(f32[48,128]{1,0:T(8,128)S(1)} %get-tuple-element.87), channel_id=1, source_target_pairs={{0,1},{1,0},{2,3},{3,2},{4,5},{5,4},{6,7},{7,6},{8,9},{9,8},{10,11... | collective-permute-start | bytes 73736 | tf_op jit(solution)/shard_map/ppermute | solution.py:365
  84.9 15.1 %collective-permute-start.7 = (f32[864,128]{1,0:T(8,128)S(1)}, f32[864,128]{1,0:T(8,128)S(1)}, u32[]{:S(2)}, u32[]{:S(2)}) collective-permute-start(f32[864,128]{1,0:T(8,128)S(1)} %get-tuple-element.89.low), channel_id=1, source_target_pairs={{2,0},{4,2},{6,4},{8,6},{10,8},{12,10},{14,12},{16,14},{18,16},{20... | collective-permute-start | bytes 1327112 | tf_op jit(solution)/shard_map/ppermute | solution.py:360
  90.4 16.8 %collective-permute-start.6 = (f32[864,128]{1,0:T(8,128)S(1)}, f32[864,128]{1,0:T(8,128)}, u32[]{:S(2)}, u32[]{:S(2)}) collective-permute-start(f32[864,128]{1,0:T(8,128)S(1)} %get-tuple-element.90.high), channel_id=1, source_target_pairs={{0,2},{2,4},{4,6},{6,8},{8,10},{10,12},{12,14},{14,16},{16,18},{18... | collective-permute-start | bytes 1327112 | tf_op jit(solution)/shard_map/ppermute | solution.py:360
  108.9 17.9 %collective-permute-start.10 = (f32[864,128]{1,0:T(8,128)S(1)}, f32[864,128]{1,0:T(8,128)S(1)}, u32[]{:S(2)}, u32[]{:S(2)}) collective-permute-start(f32[864,128]{1,0:T(8,128)S(1)} %get-tuple-element.96.low), channel_id=1, source_target_pairs={{2,0},{4,2},{6,4},{8,6},{10,8},{12,10},{14,12},{16,14},{18,16},{20... | collective-permute-start | bytes 1327112 | tf_op jit(solution)/shard_map/ppermute | solution.py:360
  109.2 17.6 %collective-permute-start.9 = (f32[864,128]{1,0:T(8,128)S(1)}, f32[864,128]{1,0:T(8,128)S(1)}, u32[]{:S(2)}, u32[]{:S(2)}) collective-permute-start(f32[864,128]{1,0:T(8,128)S(1)} %get-tuple-element.97.high), channel_id=1, source_target_pairs={{0,2},{2,4},{4,6},{6,8},{8,10},{10,12},{12,14},{14,16},{16,18},{18... | collective-permute-start | bytes 1327112 | tf_op jit(solution)/shard_map/ppermute | solution.py:360
  110.4 15.8 %collective-permute-start.11 = (f32[48,128]{1,0:T(8,128)S(1)}, f32[48,128]{1,0:T(8,128)S(1)}, u32[]{:S(2)}, u32[]{:S(2)}) collective-permute-start(f32[48,128]{1,0:T(8,128)S(1)} %get-tuple-element.100), channel_id=1, source_target_pairs={{0,1},{1,0},{2,3},{3,2},{4,5},{5,4},{6,7},{7,6},{8,9},{9,8},{10,11... | collective-permute-start | bytes 73736 | tf_op jit(solution)/shard_map/ppermute | solution.py:365
  119.2 9.5 %collective-permute-start.12 = (f32[2,14,128]{2,1,0:T(8,128)S(1)}, f32[2,14,128]{2,1,0:T(8,128)S(1)}, u32[]{:S(2)}, u32[]{:S(2)}) collective-permute-start(f32[2,14,128]{2,1,0:T(8,128)S(1)} %get-tuple-element.108), channel_id=1, source_target_pairs={{0,2},{2,4},{4,6},{6,8},{8,10},{10,12},{12,14},{14,16},{16,18},{18... | collective-permute-start | bytes 43016 | tf_op jit(solution)/shard_map/ppermute | solution.py:360
  119.3 9.5 %collective-permute-start.13 = (f32[2,14,128]{2,1,0:T(8,128)S(1)}, f32[2,14,128]{2,1,0:T(8,128)S(1)}, u32[]{:S(2)}, u32[]{:S(2)}) collective-permute-start(f32[2,14,128]{2,1,0:T(8,128)S(1)} %get-tuple-element.109), channel_id=1, source_target_pairs={{2,0},{4,2},{6,4},{8,6},{10,8},{12,10},{14,12},{16,14},{18,16},{20... | collective-permute-start | bytes 43016 | tf_op jit(solution)/shard_map/ppermute | solution.py:360
  126.2 2.6 %collective-permute-start.14 = (f32[2,56,128]{2,1,0:T(8,128)S(1)}, f32[2,56,128]{2,1,0:T(8,128)S(1)}, u32[]{:S(2)}, u32[]{:S(2)}) collective-permute-start(f32[2,56,128]{2,1,0:T(8,128)S(1)} %get-tuple-element.107.gain_ref), channel_id=1, source_target_pairs={{0,1},{1,0},{2,3},{3,2},{4,5},{5,4},{6,7},{7,6},{8,9},{9,8},{10,11... | collective-permute-start | bytes 172040 | tf_op jit(solution)/shard_map/ppermute | solution.py:365
  (13 other events, 84.0 us)
